TPU v7x, 256 devices: a whole 4x4x8 slice. The times are simulated.
256 devices in a mesh: lag: 32 (over x_hi, z, core), pts: 8 (over x_lo, y).
Axes of the slice: x: 4 (x_hi: 2, x_lo: 2; x = x_hi * 2 + x_lo), y: 4, z: 8, core: 2. Of those that a mesh axis runs over, the one named last changes fastest.
Arguments:
- history: bfloat16 [192, 2048, 128], P('lag'), may hold values from -6 to 6
- incident: bfloat16 [4, 2048, 128], P(None, 'pts'), may hold values from -6 to 6
- kernel_blocks: bfloat16 [49152, 128, 128], P(('lag', 'pts')), may hold values from -0.009765625 to 0.009765625
- block_row: int32 [49152], P(('lag', 'pts')), may hold values from 0 to 1
- block_col: int32 [49152], P(('lag', 'pts')), may hold values from 0 to 15
- lag_offset: int32 [49152], P(('lag', 'pts')), may hold values from 0 to 5
- mode_kernel: float32 [192, 128], P('lag'), may hold values from 0.25 to 2
- self_inverse: float32 [2048, 128], P('pts'), as said below
Outputs:
- densities: float32 [4, 2048, 128], P(None, 'pts')
Inputs may be any that keep to these rules, and one draw needn't show every extreme that they name: Each point block of self_inverse is the identity plus independent entries.
All inputs are finite; a program needn't handle non-finite values.
Results may differ from a plain program's by a relative error of at most 0.00031.
Values may be sent and summed in bfloat16 or wider, within the bound.
No kernel may reach another device: no remote copies, remote signals or barrier semaphores. Data moves between devices by JAX's collectives and lax.ppermute only.
A program may use at most 128 MiB of HBM per device.

v0:
```python
import jax
import jax.numpy as jnp
from jax import lax
from jax.sharding import PartitionSpec as P

STEPS = 4


def cut_along(value, dim, peers):
    before, after = (value.shape[:dim], value.shape[dim + 1 :])
    return jnp.moveaxis(value.reshape(*before, peers, -1, *after), dim, 0)


def summed_on_arrival(value, axis, dim):
    blocks = cut_along(value, dim, lax.axis_size(axis))
    arrived = lax.all_to_all(blocks, axis, split_axis=0, concat_axis=0, tiled=True)
    return arrived.sum(axis=0)


def copy_for_each(value, axis):
    peers = lax.axis_size(axis)
    return lax.all_to_all(
        jnp.broadcast_to(value[None], (peers, *value.shape)), axis, 0, 0, tiled=True
    )


def laid_out(blocks, dim):
    lengths = list(blocks.shape[1:])
    lengths[dim] *= blocks.shape[0]
    return jnp.moveaxis(blocks, 0, dim).reshape(lengths)


def gathered_copies(value, axis, dim):
    blocks = copy_for_each(value, axis)
    return laid_out(blocks, dim)


def from_behind(block, axis, distance):
    devices = range(lax.axis_size(axis))
    route = [(i - distance, i) for i in devices if i - distance in devices]
    return lax.ppermute(block, axis, route)


def apply_inverse(inverse_blocks, net_field):
    row_blocks = inverse_blocks.shape[0]
    block_size = inverse_blocks.shape[1]
    shaped = net_field.reshape(row_blocks, block_size, net_field.shape[1])
    solved = jnp.einsum("rij,rjm->rim", inverse_blocks, shaped, precision=lax.Precision.HIGHEST)
    return solved.reshape(net_field.shape[0], net_field.shape[1])


def per_device(
    history, incident, kernel_blocks, block_row, block_col, lag_offset, mode_kernel, self_inverse
):
    lags_held = history.shape[0]
    all_points = history.shape[1]
    mode_cols = history.shape[2]
    entries = kernel_blocks.shape[0]
    block_size = kernel_blocks.shape[1]
    rows_here = self_inverse.shape[0]
    row_blocks = rows_here // block_size
    col_blocks = all_points // block_size
    pair_index = block_row * lags_held + lag_offset
    selector = (
        pair_index[None, :] == jnp.arange(row_blocks * lags_held, dtype=jnp.int32)[:, None]
    ).astype(jnp.float32)
    inverse_blocks = self_inverse.reshape(row_blocks, block_size, block_size)
    first_lag = lax.axis_index("lag") == 0
    held_slabs = history
    densities = []
    for instant in range(STEPS):
        by_block = held_slabs.reshape(lags_held, col_blocks, block_size, mode_cols)
        picked = by_block[lag_offset, block_col]
        products = jnp.einsum(
            "eij,ejm->eim", kernel_blocks, picked, preferred_element_type=jnp.float32
        )
        grouped = jnp.dot(
            selector,
            products.reshape(entries, block_size * mode_cols),
            precision=lax.Precision.HIGHEST,
        )
        grouped = (
            grouped.reshape(row_blocks, lags_held, block_size, mode_cols)
            * mode_kernel[None, :, None, :]
        )
        partial_field = jnp.sum(grouped, axis=1).reshape(rows_here, mode_cols)
        driving = incident[instant].astype(jnp.float32)
        field_share = summed_on_arrival(partial_field, "lag", 1)
        share_cols = field_share.shape[1]
        first_col = lax.axis_index("lag") * share_cols
        net_share = lax.dynamic_slice_in_dim(driving, first_col, share_cols, 1) - field_share
        density = gathered_copies(apply_inverse(inverse_blocks, net_share), "lag", 1)
        densities.append(density)
        if instant + 1 < STEPS:
            new_slab = density.astype(jnp.bfloat16)
            own_rows = lax.dynamic_slice_in_dim(
                held_slabs[lags_held - 1], lax.axis_index("pts") * rows_here, rows_here, 0
            )
            arrived = from_behind(own_rows, "lag", 1)
            entering = gathered_copies(jnp.where(first_lag, new_slab, arrived), "pts", 0)
            held_slabs = jnp.concatenate([entering[None], held_slabs[: lags_held - 1]], axis=0)
    return jnp.stack(densities)


def solution(mesh):
    return jax.shard_map(
        per_device,
        mesh=mesh,
        in_specs=(
            P("lag", None, None),
            P(None, "pts", None),
            P(("lag", "pts"), None, None),
            P(("lag", "pts")),
            P(("lag", "pts")),
            P(("lag", "pts")),
            P("lag", None),
            P("pts", None),
        ),
        out_specs=P(None, "pts", None),
        check_vma=False,
    )
```

profile of v0, /device:TPU:1, one launch (start us, length us, event | category | flops | bytes accessed | tf_op | source)
XLA Modules:
  0.0 423.8 jit_solution(17795098733376738604)
XLA Ops:
  0.8 11.3 %gather_fusion = bf16[192,128,128]{2,1,0:T(8,128)(2,1)} fusion(bf16[6,16,128,128]{3,2,1,0:T(8,128)(2,1)} %bitcast.229, s32[192]{0:T(256)S(1)} %get-tuple-element.13), kind=kCustom, calls=%fused_computation | custom fusion | bytes 12584448 | tf_op jit(solution)/shard_map/gather | solution.py:73
  12.1 13.7 %convolution_bitcast_fusion.3 = f32[192,128,128]{1,2,0:T(8,128)} fusion(bf16[192,128,128]{2,1,0:T(8,128)(2,1)} %gather_fusion, bf16[192,128,128]{2,1,0:T(8,128)(2,1)} %param.10), kind=kOutput, calls=%fused_computation.23 | convolution fusion | flops 805306368 | bytes 25165824 | tf_op jit(solution)/shard_map/eij,ejm->eim/dot_general | solution.py:74
  25.8 12.6 %copy.53 = f32[192,128,128]{2,1,0:T(8,128)} copy(f32[192,128,128]{1,2,0:T(8,128)} %convolution_bitcast_fusion.3) | data formatting | bytes 25165824 | tf_op jit(solution)/shard_map/eij,ejm->eim/dot_general | solution.py:74
  38.4 16.3 %fusion.15 = f32[2,128,128]{2,1,0:T(8,128)S(1)} fusion(f32[6,128]{1,0:T(8,128)S(1)} %copy-done.8, s32[2,6]{1,0:T(2,128)S(1)} %multiply_add_fusion, s32[192]{0:T(256)S(1)} %get-tuple-element.12, f32[24,8,128,128]{3,2,1,0:T(8,128)} %bitcast.226), kind=kOutput, calls=%fused_computation.36 | convolution fusion | flops 453347584 | bytes 12717872 | tf_op jit(solution)/shard_map/dot_general | solution.py:77
  55.6 12.6 %all-to-all-start = ((f32[32,256,4]{1,2,0:T(4,128)}), f32[32,256,4]{1,2,0:T(4,128)S(1)}, u32[]{:S(2)}, u32[]{:S(2)}) async-start(f32[32,256,4]{1,2,0:T(4,128)} %bitcast.7), calls=%async_computation | async-start | bytes 262144 | tf_op jit(solution)/shard_map/all_to_all | solution.py:16
  70.6 8.1 %all-to-all-done = f32[32,256,4]{1,2,0:T(4,128)S(1)} async-done(((f32[32,256,4]{1,2,0:T(4,128)}), f32[32,256,4]{1,2,0:T(4,128)S(1)}, u32[]{:S(2)}, u32[]{:S(2)}) %all-to-all-start) | async-done | bytes 131104 | tf_op jit(solution)/shard_map/all_to_all | solution.py:16
  80.4 5.2 %all-to-all-start.1 = ((f32[32,256,4]{1,2,0:T(4,128)}), f32[32,256,4]{1,2,0:T(4,128)S(1)}, u32[]{:S(2)}, u32[]{:S(2)}) async-start(f32[32,256,4]{1,2,0:T(4,128)} %broadcast_in_dim.29), calls=%async_computation.1 | async-start | bytes 262144 | tf_op jit(solution)/shard_map/all_to_all | solution.py:22
  88.4 3.5 collective-permute-start
  91.9 4.3 %all-to-all-done.1 = f32[32,256,4]{1,2,0:T(4,128)S(1)} async-done(((f32[32,256,4]{1,2,0:T(4,128)}), f32[32,256,4]{1,2,0:T(4,128)S(1)}, u32[]{:S(2)}, u32[]{:S(2)}) %all-to-all-start.1) | async-done | bytes 131104 | tf_op jit(solution)/shard_map/all_to_all | solution.py:22
  98.1 4.5 %all-to-all-start.2 = ((bf16[8,256,128]{2,1,0:T(8,128)(2,1)}), bf16[8,256,128]{2,1,0:T(8,128)(2,1)}, u32[]{:S(2)}, u32[]{:S(2)}) async-start(bf16[8,256,128]{2,1,0:T(8,128)(2,1)} %broadcast_in_dim.30), calls=%async_computation.2 | async-start | bytes 1048576 | tf_op jit(solution)/shard_map/all_to_all | solution.py:22
  102.6 1.7 slice.37
  104.4 6.0 %all-to-all-done.2 = bf16[8,256,128]{2,1,0:T(8,128)(2,1)} async-done(((bf16[8,256,128]{2,1,0:T(8,128)(2,1)}), bf16[8,256,128]{2,1,0:T(8,128)(2,1)}, u32[]{:S(2)}, u32[]{:S(2)}) %all-to-all-start.2) | async-done | bytes 524320 | tf_op jit(solution)/shard_map/all_to_all | solution.py:22
  110.4 2.1 pad_maximum_fusion
  112.5 9.4 %gather_fusion.1 = bf16[192,128,128]{2,1,0:T(8,128)(2,1)} fusion(bf16[6,16,128,128]{3,2,1,0:T(8,128)(2,1)S(1)} %pad_maximum_fusion, s32[192]{0:T(256)S(1)} %get-tuple-element.13), kind=kCustom, calls=%fused_computation.1 | custom fusion | bytes 12584448 | tf_op jit(solution)/shard_map/gather | solution.py:73
  121.9 13.7 %convolution_bitcast_fusion.2 = f32[192,128,128]{1,2,0:T(8,128)} fusion(bf16[192,128,128]{2,1,0:T(8,128)(2,1)} %gather_fusion.1, bf16[192,128,128]{2,1,0:T(8,128)(2,1)} %param.10), kind=kOutput, calls=%fused_computation.22 | convolution fusion | flops 805306368 | bytes 25165824 | tf_op jit(solution)/shard_map/eij,ejm->eim/dot_general | solution.py:74
  135.6 12.6 %copy.60 = f32[192,128,128]{2,1,0:T(8,128)} copy(f32[192,128,128]{1,2,0:T(8,128)} %convolution_bitcast_fusion.2) | data formatting | bytes 25165824 | tf_op jit(solution)/shard_map/eij,ejm->eim/dot_general | solution.py:74
  148.2 16.7 %fusion.14 = f32[2,128,128]{2,1,0:T(8,128)S(1)} fusion(f32[6,128]{1,0:T(8,128)S(1)} %copy-done.8, s32[2,6]{1,0:T(2,128)S(1)} %multiply_add_fusion, s32[192]{0:T(256)S(1)} %get-tuple-element.12, f32[24,8,128,128]{3,2,1,0:T(8,128)} %bitcast.227), kind=kOutput, calls=%fused_computation.35 | convolution fusion | flops 453347584 | bytes 12717872 | tf_op jit(solution)/shard_map/dot_general | solution.py:77
  165.8 10.6 %all-to-all-start.3 = ((f32[32,256,4]{1,2,0:T(4,128)}), f32[32,256,4]{1,2,0:T(4,128)S(1)}, u32[]{:S(2)}, u32[]{:S(2)}) async-start(f32[32,256,4]{1,2,0:T(4,128)} %bitcast.21), calls=%async_computation.3 | async-start | bytes 262144 | tf_op jit(solution)/shard_map/all_to_all | solution.py:16
  176.5 10.3 %all-to-all-done.3 = f32[32,256,4]{1,2,0:T(4,128)S(1)} async-done(((f32[32,256,4]{1,2,0:T(4,128)}), f32[32,256,4]{1,2,0:T(4,128)S(1)}, u32[]{:S(2)}, u32[]{:S(2)}) %all-to-all-start.3) | async-done | bytes 131104 | tf_op jit(solution)/shard_map/all_to_all | solution.py:16
  187.9 5.2 %all-to-all-start.4 = ((f32[32,256,4]{1,2,0:T(4,128)}), f32[32,256,4]{1,2,0:T(4,128)S(1)}, u32[]{:S(2)}, u32[]{:S(2)}) async-start(f32[32,256,4]{1,2,0:T(4,128)} %broadcast_in_dim.32), calls=%async_computation.4 | async-start | bytes 262144 | tf_op jit(solution)/shard_map/all_to_all | solution.py:22
  194.7 3.5 collective-permute-start.1
  198.3 5.4 %all-to-all-done.4 = f32[32,256,4]{1,2,0:T(4,128)S(1)} async-done(((f32[32,256,4]{1,2,0:T(4,128)}), f32[32,256,4]{1,2,0:T(4,128)S(1)}, u32[]{:S(2)}, u32[]{:S(2)}) %all-to-all-start.4) | async-done | bytes 131104 | tf_op jit(solution)/shard_map/all_to_all | solution.py:22
  204.7 3.7 all-to-all-start.5
  208.4 2.8 pad_maximum_fusion.4
  211.2 4.3 %all-to-all-done.5 = bf16[8,256,128]{2,1,0:T(8,128)(2,1)S(1)} async-done(((bf16[8,256,128]{2,1,0:T(8,128)(2,1)}), bf16[8,256,128]{2,1,0:T(8,128)(2,1)S(1)}, u32[]{:S(2)}, u32[]{:S(2)}) %all-to-all-start.5) | async-done | bytes 524320 | tf_op jit(solution)/shard_map/all_to_all | solution.py:22
  216.3 2.1 pad_maximum_fusion.1
  218.4 9.4 %gather_fusion.2 = bf16[192,128,128]{2,1,0:T(8,128)(2,1)} fusion(bf16[6,16,128,128]{3,2,1,0:T(8,128)(2,1)S(1)} %pad_maximum_fusion.1, s32[192]{0:T(256)S(1)} %get-tuple-element.13), kind=kCustom, calls=%fused_computation.2 | custom fusion | bytes 12584448 | tf_op jit(solution)/shard_map/gather | solution.py:73
  227.9 13.7 %convolution_bitcast_fusion.1 = f32[192,128,128]{1,2,0:T(8,128)} fusion(bf16[192,128,128]{2,1,0:T(8,128)(2,1)} %gather_fusion.2, bf16[192,128,128]{2,1,0:T(8,128)(2,1)} %param.10), kind=kOutput, calls=%fused_computation.21 | convolution fusion | flops 805306368 | bytes 25165824 | tf_op jit(solution)/shard_map/eij,ejm->eim/dot_general | solution.py:74
  241.5 12.6 %copy.67 = f32[192,128,128]{2,1,0:T(8,128)} copy(f32[192,128,128]{1,2,0:T(8,128)} %convolution_bitcast_fusion.1) | data formatting | bytes 25165824 | tf_op jit(solution)/shard_map/eij,ejm->eim/dot_general | solution.py:74
  254.1 17.0 %fusion.13 = f32[2,128,128]{2,1,0:T(8,128)} fusion(f32[6,128]{1,0:T(8,128)S(1)} %copy-done.8, s32[2,6]{1,0:T(2,128)S(1)} %multiply_add_fusion, s32[192]{0:T(256)S(1)} %get-tuple-element.12, f32[24,8,128,128]{3,2,1,0:T(8,128)} %bitcast.228), kind=kOutput, calls=%fused_computation.34 | convolution fusion | flops 453347584 | bytes 12717872 | tf_op jit(solution)/shard_map/dot_general | solution.py:77
  274.4 8.8 %all-to-all-start.6 = ((f32[32,256,4]{1,2,0:T(4,128)}), f32[32,256,4]{1,2,0:T(4,128)}, u32[]{:S(2)}, u32[]{:S(2)}) async-start(f32[32,256,4]{1,2,0:T(4,128)} %bitcast.238), calls=%async_computation.6 | async-start | bytes 262144 | tf_op jit(solution)/shard_map/all_to_all | solution.py:16
  286.5 7.4 %all-to-all-done.6 = f32[32,256,4]{1,2,0:T(4,128)} async-done(((f32[32,256,4]{1,2,0:T(4,128)}), f32[32,256,4]{1,2,0:T(4,128)}, u32[]{:S(2)}, u32[]{:S(2)}) %all-to-all-start.6) | async-done | bytes 131104 | tf_op jit(solution)/shard_map/all_to_all | solution.py:16
  297.1 5.8 %all-to-all-start.7 = ((f32[32,256,4]{1,2,0:T(4,128)}), f32[32,256,4]{1,2,0:T(4,128)}, u32[]{:S(2)}, u32[]{:S(2)}) async-start(f32[32,256,4]{1,2,0:T(4,128)} %broadcast_in_dim.35), calls=%async_computation.7 | async-start | bytes 262144 | tf_op jit(solution)/shard_map/all_to_all | solution.py:22
  304.4 3.5 collective-permute-start.2
  308.0 5.5 %all-to-all-done.7 = f32[32,256,4]{1,2,0:T(4,128)} async-done(((f32[32,256,4]{1,2,0:T(4,128)}), f32[32,256,4]{1,2,0:T(4,128)}, u32[]{:S(2)}, u32[]{:S(2)}) %all-to-all-start.7) | async-done | bytes 131104 | tf_op jit(solution)/shard_map/all_to_all | solution.py:22
  319.6 1.7 broadcast_in_dim.36
  321.3 4.4 %all-to-all-start.8 = ((bf16[8,256,128]{2,1,0:T(8,128)(2,1)}), bf16[8,256,128]{2,1,0:T(8,128)(2,1)}, u32[]{:S(2)}, u32[]{:S(2)}) async-start(bf16[8,256,128]{2,1,0:T(8,128)(2,1)} %broadcast_in_dim.36), calls=%async_computation.8 | async-start | bytes 1048576 | tf_op jit(solution)/shard_map/all_to_all | solution.py:22
  325.7 1.7 pad_maximum_fusion.3
  327.5 5.4 %all-to-all-done.8 = bf16[8,256,128]{2,1,0:T(8,128)(2,1)} async-done(((bf16[8,256,128]{2,1,0:T(8,128)(2,1)}), bf16[8,256,128]{2,1,0:T(8,128)(2,1)}, u32[]{:S(2)}, u32[]{:S(2)}) %all-to-all-start.8) | async-done | bytes 524320 | tf_op jit(solution)/shard_map/all_to_all | solution.py:22
  332.9 2.1 pad_maximum_fusion.2
  335.0 9.4 %gather_fusion.3 = bf16[192,128,128]{2,1,0:T(8,128)(2,1)} fusion(bf16[6,16,128,128]{3,2,1,0:T(8,128)(2,1)S(1)} %pad_maximum_fusion.2, s32[192]{0:T(256)S(1)} %get-tuple-element.13), kind=kCustom, calls=%fused_computation.3 | custom fusion | bytes 12584448 | tf_op jit(solution)/shard_map/gather | solution.py:73
  344.4 13.7 %convolution_bitcast_fusion = f32[192,128,128]{1,2,0:T(8,128)} fusion(bf16[192,128,128]{2,1,0:T(8,128)(2,1)} %gather_fusion.3, bf16[192,128,128]{2,1,0:T(8,128)(2,1)} %param.10), kind=kOutput, calls=%fused_computation.20 | convolution fusion | flops 805306368 | bytes 25165824 | tf_op jit(solution)/shard_map/eij,ejm->eim/dot_general | solution.py:74
  358.1 12.6 %copy.74 = f32[192,128,128]{2,1,0:T(8,128)} copy(f32[192,128,128]{1,2,0:T(8,128)} %convolution_bitcast_fusion) | data formatting | bytes 25165824 | tf_op jit(solution)/shard_map/eij,ejm->eim/dot_general | solution.py:74
  370.7 16.2 %fusion.12 = f32[2,128,128]{2,1,0:T(8,128)S(1)} fusion(f32[6,128]{1,0:T(8,128)S(1)} %copy-done.8, s32[2,6]{1,0:T(2,128)S(1)} %multiply_add_fusion, s32[192]{0:T(256)S(1)} %get-tuple-element.12, f32[24,8,128,128]{3,2,1,0:T(8,128)} %bitcast.225), kind=kOutput, calls=%fused_computation.33 | convolution fusion | flops 453347584 | bytes 12717872 | tf_op jit(solution)/shard_map/dot_general | solution.py:77
  387.9 7.0 %all-to-all-start.9 = ((f32[32,256,4]{1,2,0:T(4,128)}), f32[32,256,4]{1,2,0:T(4,128)S(1)}, u32[]{:S(2)}, u32[]{:S(2)}) async-start(f32[32,256,4]{1,2,0:T(4,128)} %bitcast.47), calls=%async_computation.9 | async-start | bytes 262144 | tf_op jit(solution)/shard_map/all_to_all | solution.py:16
  395.0 10.4 %all-to-all-done.9 = f32[32,256,4]{1,2,0:T(4,128)S(1)} async-done(((f32[32,256,4]{1,2,0:T(4,128)}), f32[32,256,4]{1,2,0:T(4,128)S(1)}, u32[]{:S(2)}, u32[]{:S(2)}) %all-to-all-start.9) | async-done | bytes 131104 | tf_op jit(solution)/shard_map/all_to_all | solution.py:16
  406.5 5.2 %all-to-all-start.10 = ((f32[32,256,4]{1,2,0:T(4,128)}), f32[32,256,4]{1,2,0:T(4,128)S(1)}, u32[]{:S(2)}, u32[]{:S(2)}) async-start(f32[32,256,4]{1,2,0:T(4,128)} %broadcast_in_dim.76), calls=%async_computation.10 | async-start | bytes 262144 | tf_op jit(solution)/shard_map/all_to_all | solution.py:22
  412.7 9.5 %all-to-all-done.10 = f32[32,256,4]{1,2,0:T(4,128)S(1)} async-done(((f32[32,256,4]{1,2,0:T(4,128)}), f32[32,256,4]{1,2,0:T(4,128)S(1)}, u32[]{:S(2)}, u32[]{:S(2)}) %all-to-all-start.10) | async-done | bytes 131104 | tf_op jit(solution)/shard_map/all_to_all | solution.py:22
  (78 shorter events, 37.5 us)
Async XLA Ops:
  0.0 78.7 %copy-start = (f32[256,128]{1,0:T(8,128)S(1)}, f32[256,128]{1,0:T(8,128)}, u32[]{:S(2)}) copy-start(f32[256,128]{1,0:T(8,128)} %param.15) | copy-start | bytes 393220
  25.8 12.6 %copy-start.8 = (f32[6,128]{1,0:T(8,128)S(1)}, f32[6,128]{1,0:T(8,128)}, u32[]{:S(2)}) copy-start(f32[6,128]{1,0:T(8,128)} %param.14) | copy-start | bytes 9220
  38.4 47.2 %copy-start.1 = (bf16[6,2048,128]{2,1,0:T(8,128)(2,1)S(1)}, bf16[6,2048,128]{2,1,0:T(8,128)(2,1)}, u32[]{:S(2)}) copy-start(bf16[6,2048,128]{2,1,0:T(8,128)(2,1)} %param.8) | copy-start | bytes 9437188
  55.6 23.1 %all-to-all-start = ((f32[32,256,4]{1,2,0:T(4,128)}), f32[32,256,4]{1,2,0:T(4,128)S(1)}, u32[]{:S(2)}, u32[]{:S(2)}) async-start(f32[32,256,4]{1,2,0:T(4,128)} %bitcast.7), calls=%async_computation | async-start | bytes 262144 | tf_op jit(solution)/shard_map/all_to_all | solution.py:16
  80.4 15.8 %all-to-all-start.1 = ((f32[32,256,4]{1,2,0:T(4,128)}), f32[32,256,4]{1,2,0:T(4,128)S(1)}, u32[]{:S(2)}, u32[]{:S(2)}) async-start(f32[32,256,4]{1,2,0:T(4,128)} %broadcast_in_dim.29), calls=%async_computation.1 | async-start | bytes 262144 | tf_op jit(solution)/shard_map/all_to_all | solution.py:22
  88.4 7.9 %collective-permute-start = (bf16[256,128]{0,1:T(8,128)(2,1)}, bf16[256,128]{0,1:T(8,128)(2,1)}, u32[]{:S(2)}, u32[]{:S(2)}) collective-permute-start(bf16[256,128]{0,1:T(8,128)(2,1)} %bitcast.15), channel_id=1, source_target_pairs={{0,8},{8,16},{16,24},{24,32},{32,40},{40,48},{48,56},{56,64},{64,7... | collective-permute-start | bytes 196616 | tf_op jit(solution)/shard_map/ppermute | solution.py:41
  98.1 12.3 %all-to-all-start.2 = ((bf16[8,256,128]{2,1,0:T(8,128)(2,1)}), bf16[8,256,128]{2,1,0:T(8,128)(2,1)}, u32[]{:S(2)}, u32[]{:S(2)}) async-start(bf16[8,256,128]{2,1,0:T(8,128)(2,1)} %broadcast_in_dim.30), calls=%async_computation.2 | async-start | bytes 1048576 | tf_op jit(solution)/shard_map/all_to_all | solution.py:22
  148.2 28.2 %copy-start.7 = (bf16[1,256,128]{2,1,0:T(8,128)(2,1)S(1)}, bf16[1,256,128]{2,1,0:T(8,128)(2,1)}, u32[]{:S(2)}) copy-start(bf16[1,256,128]{2,1,0:T(8,128)(2,1)} %get-tuple-element.9) | copy-start | bytes 196612
  148.2 60.2 %copy-start.2 = (bf16[5,2048,128]{2,1,0:T(8,128)(2,1)S(1)}, bf16[5,2048,128]{2,1,0:T(8,128)(2,1)}, u32[]{:S(2)}) copy-start(bf16[5,2048,128]{2,1,0:T(8,128)(2,1)} %slice.37) | copy-start | bytes 7864324
  165.8 21.1 %all-to-all-start.3 = ((f32[32,256,4]{1,2,0:T(4,128)}), f32[32,256,4]{1,2,0:T(4,128)S(1)}, u32[]{:S(2)}, u32[]{:S(2)}) async-start(f32[32,256,4]{1,2,0:T(4,128)} %bitcast.21), calls=%async_computation.3 | async-start | bytes 262144 | tf_op jit(solution)/shard_map/all_to_all | solution.py:16
  187.9 15.8 %all-to-all-start.4 = ((f32[32,256,4]{1,2,0:T(4,128)}), f32[32,256,4]{1,2,0:T(4,128)S(1)}, u32[]{:S(2)}, u32[]{:S(2)}) async-start(f32[32,256,4]{1,2,0:T(4,128)} %broadcast_in_dim.32), calls=%async_computation.4 | async-start | bytes 262144 | tf_op jit(solution)/shard_map/all_to_all | solution.py:22
  194.7 9.0 %collective-permute-start.1 = (bf16[256,128]{0,1:T(8,128)(2,1)S(1)}, bf16[256,128]{0,1:T(8,128)(2,1)S(1)}, u32[]{:S(2)}, u32[]{:S(2)}) collective-permute-start(bf16[256,128]{0,1:T(8,128)(2,1)S(1)} %bitcast.239), channel_id=1, source_target_pairs={{0,8},{8,16},{16,24},{24,32},{32,40},{40,48},{48,56},{56,64},{64,7... | collective-permute-start | bytes 196616 | tf_op jit(solution)/shard_map/ppermute | solution.py:41
  204.7 10.8 %all-to-all-start.5 = ((bf16[8,256,128]{2,1,0:T(8,128)(2,1)}), bf16[8,256,128]{2,1,0:T(8,128)(2,1)S(1)}, u32[]{:S(2)}, u32[]{:S(2)}) async-start(bf16[8,256,128]{2,1,0:T(8,128)(2,1)} %broadcast_in_dim.33), calls=%async_computation.5 | async-start | bytes 1048576 | tf_op jit(solution)/shard_map/all_to_all | solution.py:22
  215.5 0.8 copy-start.4
  254.1 71.6 %copy-start.3 = (bf16[5,2048,128]{2,1,0:T(8,128)(2,1)S(1)}, bf16[5,2048,128]{2,1,0:T(8,128)(2,1)}, u32[]{:S(2)}) copy-start(bf16[5,2048,128]{2,1,0:T(8,128)(2,1)} %pad_maximum_fusion.4) | copy-start | bytes 7864324
  254.1 71.6 %copy-start.5 = (bf16[8,256,128]{2,1,0:T(8,128)(2,1)S(1)}, bf16[8,256,128]{2,1,0:T(8,128)(2,1)}, u32[]{:S(2)}) copy-start(bf16[8,256,128]{2,1,0:T(8,128)(2,1)} %copy-done.4) | copy-start | bytes 1572868
  274.4 19.4 %all-to-all-start.6 = ((f32[32,256,4]{1,2,0:T(4,128)}), f32[32,256,4]{1,2,0:T(4,128)}, u32[]{:S(2)}, u32[]{:S(2)}) async-start(f32[32,256,4]{1,2,0:T(4,128)} %bitcast.238), calls=%async_computation.6 | async-start | bytes 262144 | tf_op jit(solution)/shard_map/all_to_all | solution.py:16
  297.1 16.5 %all-to-all-start.7 = ((f32[32,256,4]{1,2,0:T(4,128)}), f32[32,256,4]{1,2,0:T(4,128)}, u32[]{:S(2)}, u32[]{:S(2)}) async-start(f32[32,256,4]{1,2,0:T(4,128)} %broadcast_in_dim.35), calls=%async_computation.7 | async-start | bytes 262144 | tf_op jit(solution)/shard_map/all_to_all | solution.py:22
  304.4 12.1 %collective-permute-start.2 = (bf16[256,128]{0,1:T(8,128)(2,1)}, bf16[256,128]{0,1:T(8,128)(2,1)}, u32[]{:S(2)}, u32[]{:S(2)}) collective-permute-start(bf16[256,128]{0,1:T(8,128)(2,1)} %bitcast.240), channel_id=1, source_target_pairs={{0,8},{8,16},{16,24},{24,32},{32,40},{40,48},{48,56},{56,64},{64,7... | collective-permute-start | bytes 196616 | tf_op jit(solution)/shard_map/ppermute | solution.py:41
  321.3 11.6 %all-to-all-start.8 = ((bf16[8,256,128]{2,1,0:T(8,128)(2,1)}), bf16[8,256,128]{2,1,0:T(8,128)(2,1)}, u32[]{:S(2)}, u32[]{:S(2)}) async-start(bf16[8,256,128]{2,1,0:T(8,128)(2,1)} %broadcast_in_dim.36), calls=%async_computation.8 | async-start | bytes 1048576 | tf_op jit(solution)/shard_map/all_to_all | solution.py:22
  370.7 24.1 %copy-start.6 = (bf16[1,256,128]{2,1,0:T(8,128)(2,1)S(1)}, bf16[1,256,128]{2,1,0:T(8,128)(2,1)}, u32[]{:S(2)}) copy-start(bf16[1,256,128]{2,1,0:T(8,128)(2,1)} %get-tuple-element.8) | copy-start | bytes 196612
  387.9 17.5 %all-to-all-start.9 = ((f32[32,256,4]{1,2,0:T(4,128)}), f32[32,256,4]{1,2,0:T(4,128)S(1)}, u32[]{:S(2)}, u32[]{:S(2)}) async-start(f32[32,256,4]{1,2,0:T(4,128)} %bitcast.47), calls=%async_computation.9 | async-start | bytes 262144 | tf_op jit(solution)/shard_map/all_to_all | solution.py:16
  406.5 15.8 %all-to-all-start.10 = ((f32[32,256,4]{1,2,0:T(4,128)}), f32[32,256,4]{1,2,0:T(4,128)S(1)}, u32[]{:S(2)}, u32[]{:S(2)}) async-start(f32[32,256,4]{1,2,0:T(4,128)} %broadcast_in_dim.76), calls=%async_computation.10 | async-start | bytes 262144 | tf_op jit(solution)/shard_map/all_to_all | solution.py:22
where the time goes:
time: 431 us; the launch traced here: 424 us
  matrix products  123 us (29%)
  local copies, waits for them, and re-layouts  120 us (28%)
  starting transfers between devices  83.5 us (19%)
  waiting for transfers between devices  76.7 us (18%)
  other arithmetic  19.1 us (4%)
    dot_general x4, matrix products, per_device(): jnp.dot(selector, products.reshape(entries, block_size * mode_cols), prec...  66.2 us
    dot_general x4, matrix products, per_device(): jnp.einsum('eij,ejm->eim', kernel_blocks, picked, preferred_element_type=...  54.7 us
    dot_general x4, local copies, waits for them, and re-layouts, per_device(): jnp.einsum('eij,ejm->eim', kernel_blocks, picked, preferred_element_type=...  50.4 us
    all_to_all x7, waiting for transfers between devices, copy_for_each(): lax.all_to_all(jnp.broadcast_to(value[None], (peers, *value.shape)), axis...  40.5 us
    gather x4, local copies, waits for them, and re-layouts, per_device(): picked = by_block[lag_offset, block_col]  39.6 us
    all_to_all x4, starting transfers between devices, summed_on_arrival(): lax.all_to_all(blocks, axis, split_axis=0, concat_axis=0, tiled=True)  38.9 us
    all_to_all x4, waiting for transfers between devices, summed_on_arrival(): lax.all_to_all(blocks, axis, split_axis=0, concat_axis=0, tiled=True)  36.2 us
    all_to_all x7, starting transfers between devices, copy_for_each(): lax.all_to_all(jnp.broadcast_to(value[None], (peers, *value.shape)), axis...  33.9 us
  transfers between devices with their start and end apart: 14, of which 11 were waited for; matrix products, arithmetic and copies ran while one was open for 5% of the time, Pallas kernels for 0%

commit v1 on v0

v1 whole, which is shorter than its diff:
```python
import functools

import jax
import jax.numpy as jnp
from jax import lax
from jax.experimental import pallas as pl
from jax.experimental.pallas import tpu as pltpu
from jax.sharding import PartitionSpec as P

STEPS = 4
UNROLL = 8
CHUNKS = 4
LIMIT = 40 << 20


def accumulate(out_refs, kernel_of, picks_of, scales_of, first, count):
    def group(g, carry):
        base = first + g * UNROLL
        sums = [[None] * len(refs) for refs in out_refs]
        for u in range(UNROLL):
            entry = base + u
            block = kernel_of(entry)
            picks = picks_of(entry)
            scales = scales_of(entry)
            for k, refs in enumerate(out_refs):
                product = jnp.dot(block, picks[k], preferred_element_type=jnp.float32)
                for r in range(len(refs)):
                    term = product * scales[k][r]
                    sums[k][r] = term if sums[k][r] is None else sums[k][r] + term
        for k, refs in enumerate(out_refs):
            for r, ref in enumerate(refs):
                ref[...] += sums[k][r]
        return carry

    lax.fori_loop(0, count // UNROLL, group, 0)


def chunk_copies(source, target, sems):
    size = source.shape[0] // CHUNKS
    return [
        pltpu.make_async_copy(
            source.at[pl.ds(c * size, size)], target.at[pl.ds(c * size, size)], sems.at[c]
        )
        for c in range(CHUNKS)
    ]


def field_kernel(steps, halo_lags, row_s, col_s, lag_s, blocks_h, *rest):
    if halo_lags:
        halo_h, history_h, mode_ref, out_ref, blocks_v, state_v, sems, state_sem = rest
    else:
        history_h, mode_ref, out_ref, blocks_v, state_v, sems, state_sem = rest
    lags_held = history_h.shape[0]
    copies = [
        pltpu.make_async_copy(
            history_h, state_v.at[pl.ds(halo_lags, lags_held)], state_sem.at[0]
        )
    ]
    if halo_lags:
        copies.append(
            pltpu.make_async_copy(halo_h, state_v.at[pl.ds(0, halo_lags)], state_sem.at[1])
        )
    for copy in copies:
        copy.start()
    block_copies = chunk_copies(blocks_h, blocks_v, sems)
    for copy in block_copies:
        copy.start()
    out_ref[...] = jnp.zeros_like(out_ref)
    size = blocks_v.shape[1]
    row_blocks = out_ref.shape[1]

    def picks_of(entry):
        first = pl.multiple_of(col_s[entry] * size, size)
        lag = lag_s[entry]
        return [state_v[halo_lags + lag - s, pl.ds(first, size), :] for s in steps]

    def scales_of(entry):
        factor = mode_ref[pl.ds(lag_s[entry], 1), :]
        row = row_s[entry]
        own = [jnp.where(row == r, factor, 0.0) for r in range(row_blocks)]
        return [own for _ in steps]

    out_refs = [[out_ref.at[k, r] for r in range(row_blocks)] for k in range(len(steps))]
    for copy in copies:
        copy.wait()
    per = blocks_v.shape[0] // CHUNKS
    for c, copy in enumerate(block_copies):
        copy.wait()
        accumulate(out_refs, lambda e: blocks_v[e], picks_of, scales_of, c * per, per)


def fields(steps, halo, history, kernel_blocks, block_row, block_col, lag_offset, mode_kernel, row_blocks):
    halo_lags = 0 if halo is None else halo.shape[0]
    entries, size, _ = kernel_blocks.shape
    lags_held, points, modes = history.shape
    anywhere = pl.BlockSpec(memory_space=pl.ANY)
    in_smem = pl.BlockSpec(memory_space=pltpu.SMEM)
    in_vmem = pl.BlockSpec(memory_space=pltpu.VMEM)
    states = [history] if halo is None else [halo, history]
    return pl.pallas_call(
        functools.partial(field_kernel, steps, halo_lags),
        out_shape=jax.ShapeDtypeStruct((len(steps), row_blocks, size, modes), jnp.float32),
        in_specs=[in_smem] * 3 + [anywhere] * (1 + len(states)) + [in_vmem],
        out_specs=in_vmem,
        scratch_shapes=[
            pltpu.VMEM(kernel_blocks.shape, kernel_blocks.dtype),
            pltpu.VMEM((halo_lags + lags_held, points, modes), history.dtype),
            pltpu.SemaphoreType.DMA((CHUNKS,)),
            pltpu.SemaphoreType.DMA((2,)),
        ],
        compiler_params=pltpu.CompilerParams(vmem_limit_bytes=LIMIT),
        name=f"fields_{len(steps)}",
    )(block_row, block_col, lag_offset, kernel_blocks, *states, mode_kernel)


def solve_into(inverse_ref, net, density_ref, copies_ref):
    row_blocks, size = net.shape[0], net.shape[1]
    for r in range(row_blocks):
        solved = jnp.dot(
            inverse_ref[pl.ds(r * size, size), :],
            net[r],
            precision=lax.Precision.HIGHEST,
            preferred_element_type=jnp.float32,
        )
        density_ref[pl.ds(r * size, size), :] = solved
        if copies_ref is not None:
            rounded = solved.astype(copies_ref.dtype)
            for p in range(copies_ref.shape[0]):
                copies_ref[p, pl.ds(r * size, size), :] = rounded


def first_kernel(incident_ref, field_ref, inverse_ref, density_ref, copies_ref):
    row_blocks, size, modes = field_ref.shape
    net = incident_ref[...].astype(jnp.float32).reshape(field_ref.shape) - field_ref[...]
    solve_into(inverse_ref, net, density_ref, copies_ref)


def chain_kernel(step, last, row_s, col_s, lag_s, blocks_h, *rest):
    fresh = rest[:step]
    rest = rest[step:]
    if last:
        mode_ref, incident_ref, field_ref, inverse_ref, density_ref, blocks_v, acc, sems = rest
        copies_ref = None
    else:
        mode_ref, incident_ref, field_ref, inverse_ref, density_ref, copies_ref, blocks_v, acc, sems = rest
    size = blocks_v.shape[1]
    row_blocks = acc.shape[0]
    block_copies = chunk_copies(blocks_h, blocks_v, sems)
    for copy in block_copies:
        copy.start()
    acc[...] = jnp.zeros_like(acc)

    def picks_of(entry):
        first = pl.multiple_of(col_s[entry] * size, size)
        lag = lag_s[entry]
        pick = fresh[0][pl.ds(first, size), :]
        for t in range(1, step):
            pick = jnp.where(lag == step - 1 - t, fresh[t][pl.ds(first, size), :], pick)
        return [pick]

    def scales_of(entry):
        lag = lag_s[entry]
        factor = jnp.where(lag < step, mode_ref[pl.ds(lag, 1), :], 0.0)
        row = row_s[entry]
        return [[jnp.where(row == r, factor, 0.0) for r in range(row_blocks)]]

    per = blocks_v.shape[0] // CHUNKS
    for c, copy in enumerate(block_copies):
        copy.wait()
        accumulate(
            [[acc.at[r] for r in range(row_blocks)]],
            lambda e: blocks_v[e],
            picks_of,
            scales_of,
            c * per,
            per,
        )
    net = incident_ref[...].astype(jnp.float32).reshape(acc.shape) - field_ref[...] - acc[...]
    solve_into(inverse_ref, net, density_ref, copies_ref)


def densities_of(step, steps, peers, fresh, incident, field, inverse, tables):
    row_blocks, size, modes = field.shape
    rows = row_blocks * size
    last = step == steps - 1
    in_vmem = pl.BlockSpec(memory_space=pltpu.VMEM)
    in_smem = pl.BlockSpec(memory_space=pltpu.SMEM)
    density = jax.ShapeDtypeStruct((rows, modes), jnp.float32)
    copies = jax.ShapeDtypeStruct((peers, rows, modes), jnp.bfloat16)
    params = pltpu.CompilerParams(vmem_limit_bytes=LIMIT)
    if step == 0:
        return pl.pallas_call(
            first_kernel,
            out_shape=(density, copies),
            in_specs=[in_vmem] * 3,
            out_specs=(in_vmem, in_vmem),
            compiler_params=params,
            name="first_density",
        )(incident, field, inverse)
    block_row, block_col, lag_offset, kernel_blocks, mode_kernel = tables
    return pl.pallas_call(
        functools.partial(chain_kernel, step, last),
        out_shape=(density,) if last else (density, copies),
        in_specs=[in_smem] * 3 + [pl.BlockSpec(memory_space=pl.ANY)] + [in_vmem] * (step + 4),
        out_specs=(in_vmem,) if last else (in_vmem, in_vmem),
        scratch_shapes=[
            pltpu.VMEM(kernel_blocks.shape, kernel_blocks.dtype),
            pltpu.VMEM(field.shape, jnp.float32),
            pltpu.SemaphoreType.DMA((CHUNKS,)),
        ],
        compiler_params=params,
        name=f"chain_{step}",
    )(block_row, block_col, lag_offset, kernel_blocks, *fresh, mode_kernel, incident, field, inverse)


def lag_of(x_hi, z, core):
    return x_hi * 16 + z * 2 + core


TREE = (
    ([(lag_of(x, z, 1), lag_of(x, z, 0)) for x in range(2) for z in range(8)],),
    tuple(
        [(lag_of(x, q + k, 0), lag_of(x, q, 0)) for x in range(2) for q in (0, 4)]
        for k in (1, 2, 3)
    ),
    (
        [(lag_of(0, 4, 0), 0)],
        [(lag_of(1, 0, 0), 0)],
        [(lag_of(1, 4, 0), 0)],
    ),
)


def summed_on_first(value):
    for level in TREE:
        arrived = [lax.ppermute(value, "lag", pairs) for pairs in level]
        for piece in arrived:
            value = value + piece
    return value


def cut_along(value, dim, peers):
    before, after = (value.shape[:dim], value.shape[dim + 1 :])
    return jnp.moveaxis(value.reshape(*before, peers, -1, *after), dim, 0)


def spread_from_first(value):
    peers = lax.axis_size("lag")
    steps, rows, modes = value.shape
    blocks = cut_along(value, 1, peers)
    mine = lax.all_to_all(blocks, "lag", 0, 0, tiled=True)[0]
    everyone = lax.all_to_all(
        jnp.broadcast_to(mine[None], (peers, *mine.shape)), "lag", 0, 0, tiled=True
    )
    return jnp.moveaxis(everyone, 0, 1).reshape(steps, rows, modes)


def per_device(
    history, incident, kernel_blocks, block_row, block_col, lag_offset, mode_kernel, self_inverse
):
    size = kernel_blocks.shape[1]
    rows_here = self_inverse.shape[0]
    row_blocks = rows_here // size
    peers = lax.axis_size("pts")
    lags = lax.axis_size("lag")
    lags_held, points, modes = history.shape
    behind = STEPS - 1
    halo = lax.ppermute(
        history[lags_held - behind :], "lag", [(i, i + 1) for i in range(lags - 1)]
    )
    tables = (block_row, block_col, lag_offset, kernel_blocks, mode_kernel)
    now = fields((0,), None, history, kernel_blocks, block_row, block_col, lag_offset, mode_kernel, row_blocks)
    now = summed_on_first(now[0])
    density, copies = densities_of(0, STEPS, peers, [], incident[0], now, self_inverse, tables)
    later = fields(
        tuple(range(1, STEPS)), halo, history, kernel_blocks, block_row, block_col, lag_offset, mode_kernel, row_blocks
    )
    later = summed_on_first(later)
    fresh = []
    out = [density]
    for step in range(1, STEPS):
        everyone = lax.all_to_all(copies, "pts", 0, 0, tiled=True)
        fresh.append(everyone.reshape(points, modes))
        density, *copies = densities_of(
            step, STEPS, peers, fresh, incident[step], later[step - 1], self_inverse, tables
        )
        copies = copies[0] if copies else None
        out.append(density)
    return spread_from_first(jnp.stack(out))


def solution(mesh):
    return jax.shard_map(
        per_device,
        mesh=mesh,
        in_specs=(
            P("lag", None, None),
            P(None, "pts", None),
            P(("lag", "pts"), None, None),
            P(("lag", "pts")),
            P(("lag", "pts")),
            P(("lag", "pts")),
            P("lag", None),
            P("pts", None),
        ),
        out_specs=P(None, "pts", None),
        check_vma=False,
    )
```

time: 431 us -> 188 us (0.44); the launches traced: 424 us -> 187 us
  matrix products: 123 us -> 0 us
  local copies, waits for them, and re-layouts: 120 us -> 10.9 us
  blocking collectives: 0 us -> 102 us
  waiting for transfers between devices: 76.7 us -> 10.9 us
  starting transfers between devices: 83.5 us -> 21.3 us
  Pallas kernels: 0 us -> 41.5 us
  other arithmetic: 19.1 us -> 0.34 us
    dot_general x12 -> x0, matrix products: 123 us -> none  [the longest x4 66.2 us: per_device(): jnp.dot(selector, products.reshape(entries, block_size * mode_cols), prec...]
    all_to_all x0 -> x4, blocking collectives: none -> 102 us  [the longest x1 58.7 us: spread_from_first(): mine = lax.all_to_all(blocks, 'lag', 0, 0, tiled=True)[0]]
    all_to_all x11 -> x1, waiting for transfers between devices: 76.7 us -> 6.98 us  [per_device(): everyone = lax.all_to_all(copies, 'pts', 0, 0, tiled=True)]
    all_to_all x11 -> x1, starting transfers between devices: 72.9 us -> 5.12 us  [per_device(): everyone = lax.all_to_all(copies, 'pts', 0, 0, tiled=True)]
    dot_general x4 -> x0, local copies, waits for them, and re-layouts: 50.4 us -> none  [per_device(): jnp.einsum('eij,ejm->eim', kernel_blocks, picked, preferred_element_type=...]
    pallas_call x0 -> x6, Pallas kernels: none -> 41.5 us  [the longest x3 22.4 us: densities_of(): pl.pallas_call(functools.partial(chain_kernel, step, last), out_shape=(de...]
    gather x4 -> x0, local copies, waits for them, and re-layouts: 39.6 us -> none  [per_device(): picked = by_block[lag_offset, block_col]]
    concatenate x5 -> x0, other arithmetic: 10.9 us -> none  [per_device(): jnp.concatenate([entering[None], held_slabs[:lags_held - 1]], axis=0)]
  transfers between devices with their start and end apart: 14 -> 16, of which waited for: 11 -> 3; matrix products, arithmetic and copies ran while one was open for 5% -> 0% of each run, Pallas kernels for 0% -> 10%
where the time goes in v1:
time: 188 us; the launch traced here: 187 us
  blocking collectives  102 us (54%)
  Pallas kernels  41.5 us (22%)
  starting transfers between devices  21.3 us (11%)
  local copies, waits for them, and re-layouts  10.9 us (6%)
  waiting for transfers between devices  10.9 us (6%)
    all_to_all x1, blocking collectives, spread_from_first(): mine = lax.all_to_all(blocks, 'lag', 0, 0, tiled=True)[0]  58.7 us
    all_to_all x1, blocking collectives, spread_from_first(): lax.all_to_all(jnp.broadcast_to(mine[None], (peers, *mine.shape)), 'lag',...  22.9 us
    pallas_call x3, Pallas kernels, densities_of(): pl.pallas_call(functools.partial(chain_kernel, step, last), out_shape=(de...  22.4 us
    all_to_all x2, blocking collectives, per_device(): everyone = lax.all_to_all(copies, 'pts', 0, 0, tiled=True)  20 us
    pallas_call x2, Pallas kernels, fields(): pl.pallas_call(functools.partial(field_kernel, steps, halo_lags), out_sha...  18.1 us
    ppermute x14, starting transfers between devices, summed_on_first(): arrived = [lax.ppermute(value, 'lag', pairs) for pairs in level]  11.3 us
    unnamed x26, local copies, waits for them, and re-layouts  8.32 us
    all_to_all x1, waiting for transfers between devices, per_device(): everyone = lax.all_to_all(copies, 'pts', 0, 0, tiled=True)  6.98 us
  transfers between devices with their start and end apart: 16, of which 3 were waited for; matrix products, arithmetic and copies ran while one was open for 0% of the time, Pallas kernels for 10%

profile of v1, /device:TPU:1, one launch (start us, length us, event | category | flops | bytes accessed | tf_op | source)
XLA Modules:
  0.0 187.1 jit_solution(963014988197178523)
XLA Ops:
  0.0 1.7 slice.29
  1.7 4.9 %collective-permute-start.7 = (bf16[3,2048,128]{2,1,0:T(8,128)(2,1)S(1)}, bf16[3,2048,128]{2,1,0:T(8,128)(2,1)S(1)}, u32[]{:S(2)}, u32[]{:S(2)}) collective-permute-start(bf16[3,2048,128]{2,1,0:T(8,128)(2,1)S(1)} %slice.29), channel_id=1, source_target_pairs={{0,8},{8,16},{16,24},{24,32},{32,40},{40,48},{48,56},{56,64},{64,7... | collective-permute-start | bytes 4718600 | tf_op jit(solution)/shard_map/ppermute | solution.py:268
  6.6 0.0 copy-start
  6.6 2.8 %copy-done = bf16[192,128,128]{2,1,0:T(8,128)(2,1)S(1)} copy-done((bf16[192,128,128]{2,1,0:T(8,128)(2,1)S(1)}, bf16[192,128,128]{2,1,0:T(8,128)(2,1)}, u32[]{:S(2)}) %copy-start) | copy-done | bytes 6291480
  9.4 0.7 copy-done.4
  10.1 0.7 copy-done.6
  10.8 0.7 copy-done.8
  11.4 0.7 copy-done.10
  12.1 6.9 %fields_1.1 = f32[1,2,128,128]{3,2,1,0:T(8,128)S(1)} custom-call(s32[192]{0:T(256)S(1)} %copy-done.6, s32[192]{0:T(256)S(1)} %copy-done.8, s32[192]{0:T(256)S(1)} %copy-done.10, bf16[192,128,128]{2,1,0:T(8,128)(2,1)S(1)} %copy-done, bf16[6,2048,128]{2,1,0:T(8,128)(2,1)S(1)} %copy-done.2, f32[6,128]{1,0:T(8,128)S(1)} %copy-done.4), custom_call_target="tpu_custom_call" | custom-call | tf_op jit(solution)/shard_map/fields_1/pallas_call | solution.py:100
  19.0 1.6 collective-permute-start
  20.6 3.3 %collective-permute-done.7.rest_0_ = bf16[3,2048,128]{2,1,0:T(8,128)(2,1)S(1)} collective-permute-done((bf16[3,2048,128]{2,1,0:T(8,128)(2,1)S(1)}, bf16[3,2048,128]{2,1,0:T(8,128)(2,1)S(1)}, u32[]{:S(2)}, u32[]{:S(2)}) %collective-permute-start.7) | collective-permute-done | bytes 1572896 | tf_op jit(solution)/shard_map/ppermute | solution.py:268
  23.9 11.1 %fields_3.1 = f32[3,2,128,128]{3,2,1,0:T(8,128)S(1)} custom-call(s32[192]{0:T(256)S(1)} %copy-done.6, s32[192]{0:T(256)S(1)} %copy-done.8, s32[192]{0:T(256)S(1)} %copy-done.10, bf16[192,128,128]{2,1,0:T(8,128)(2,1)S(1)} %copy-done, bf16[3,2048,128]{2,1,0:T(8,128)(2,1)S(1)} %collective-permute-done.7.rest_0_, bf16[6,2048,128]{2,1,0:T(8,128)(2,1)S(1)} %copy-done.2, ...), custom_call_target="tpu_custom_call" | custom-call | tf_op jit(solution)/shard_map/fields_3/pallas_call | solution.py:100
  35.1 0.0 copy-start.12
  35.1 0.0 copy-start.3
  35.1 1.4 collective-permute-start.8
  36.6 0.7 collective-permute-start.1
  37.3 0.6 collective-permute-done.8
  37.9 0.1 add.49
  37.9 0.7 collective-permute-start.10
  38.6 0.7 collective-permute-start.11
  39.3 0.7 collective-permute-start.9
  40.0 0.7 collective-permute-start.2
  40.7 0.7 collective-permute-start.3
  41.4 0.7 collective-permute-start.4
  42.1 0.7 collective-permute-start.5
  42.8 0.7 collective-permute-start.6
  43.5 0.1 add_add_fusion.1
  43.6 0.0 copy-start.5
  43.6 0.0 copy-start.7
  43.6 0.0 copy-start.9
  43.6 0.0 copy-start.11
  43.6 0.8 collective-permute-start.12
  44.5 0.7 collective-permute-start.13
  45.2 0.7 collective-permute-start.14
  46.0 1.1 first_density.1
  47.1 5.1 %all-to-all-start = ((bf16[8,256,128]{2,1,0:T(8,128)(2,1)}), bf16[8,256,128]{2,1,0:T(8,128)(2,1)S(1)}, u32[]{:S(2)}, u32[]{:S(2)}) async-start(bf16[8,256,128]{2,1,0:T(8,128)(2,1)} %get-tuple-element.12), calls=%async_computation | async-start | bytes 1048576 | tf_op jit(solution)/shard_map/all_to_all | solution.py:282
  52.2 0.1 add_add_fusion
  52.3 7.0 %all-to-all-done = bf16[8,256,128]{2,1,0:T(8,128)(2,1)S(1)} async-done(((bf16[8,256,128]{2,1,0:T(8,128)(2,1)}), bf16[8,256,128]{2,1,0:T(8,128)(2,1)S(1)}, u32[]{:S(2)}, u32[]{:S(2)}) %all-to-all-start) | async-done | bytes 524320 | tf_op jit(solution)/shard_map/all_to_all | solution.py:282
  59.3 2.8 %copy-done.1 = bf16[192,128,128]{2,1,0:T(8,128)(2,1)S(1)} copy-done((bf16[192,128,128]{2,1,0:T(8,128)(2,1)S(1)}, bf16[192,128,128]{2,1,0:T(8,128)(2,1)}, u32[]{:S(2)}) %copy-start.1) | copy-done | bytes 6291480
  62.1 7.0 %chain_1.1 = (f32[256,128]{1,0:T(8,128)S(1)}, bf16[8,256,128]{2,1,0:T(8,128)(2,1)S(1)}) custom-call(s32[192]{0:T(256)S(1)} %copy-done.7, s32[192]{0:T(256)S(1)} %copy-done.9, s32[192]{0:T(256)S(1)} %copy-done.11, bf16[192,128,128]{2,1,0:T(8,128)(2,1)S(1)} %copy-done.1, bf16[2048,128]{1,0:T(8,128)(2,1)S(1)} %bitcast.40, f32[6,128]{1,0:T(8,128)S(1)} %copy-done.5, ...), custom_call_target="tpu_custom_call" | custom-call | tf_op jit(solution)/shard_map/chain_1/pallas_call | solution.py:201
  69.1 10.1 %all_to_all.25 = bf16[8,256,128]{2,1,0:T(8,128)(2,1)S(1)} all-to-all(bf16[8,256,128]{2,1,0:T(8,128)(2,1)S(1)} %get-tuple-element.14), channel_id=1, replica_groups=mesh['lag'=32,'pts'=8] {'pts'}, dimensions={0} | all-to-all | bytes 1048576 | tf_op jit(solution)/shard_map/all_to_all | solution.py:282
  79.3 7.3 %chain_2.1 = (f32[256,128]{1,0:T(8,128)S(1)}, bf16[8,256,128]{2,1,0:T(8,128)(2,1)S(1)}) custom-call(s32[192]{0:T(256)S(1)} %copy-done.7, s32[192]{0:T(256)S(1)} %copy-done.9, s32[192]{0:T(256)S(1)} %copy-done.11, bf16[192,128,128]{2,1,0:T(8,128)(2,1)S(1)} %copy-done.1, bf16[2048,128]{1,0:T(8,128)(2,1)S(1)} %bitcast.41, bf16[2048,128]{1,0:T(8,128)(2,1)S(1)} %bitcast.43, ...), custom_call_target="tpu_custom_call" | custom-call | tf_op jit(solution)/shard_map/chain_2/pallas_call | solution.py:201
  86.6 9.9 %all_to_all.26 = bf16[8,256,128]{2,1,0:T(8,128)(2,1)S(1)} all-to-all(bf16[8,256,128]{2,1,0:T(8,128)(2,1)S(1)} %get-tuple-element.16), channel_id=1, replica_groups=mesh['lag'=32,'pts'=8] {'pts'}, dimensions={0} | all-to-all | bytes 1048576 | tf_op jit(solution)/shard_map/all_to_all | solution.py:282
  96.4 8.1 %chain_3.1 = f32[256,128]{1,0:T(8,128)S(1)} custom-call(s32[192]{0:T(256)S(1)} %copy-done.7, s32[192]{0:T(256)S(1)} %copy-done.9, s32[192]{0:T(256)S(1)} %copy-done.11, bf16[192,128,128]{2,1,0:T(8,128)(2,1)S(1)} %copy-done.1, bf16[2048,128]{1,0:T(8,128)(2,1)S(1)} %bitcast.42, bf16[2048,128]{1,0:T(8,128)(2,1)S(1)} %bitcast.44, ...), custom_call_target="tpu_custom_call" | custom-call | tf_op jit(solution)/shard_map/chain_3/pallas_call | solution.py:201
  104.6 58.7 %all_to_all.27 = f32[32,4,8,128]{3,2,1,0:T(8,128)S(1)} all-to-all(f32[32,4,8,128]{3,2,1,0:T(8,128)S(1)} %maximum_bitcast_fusion), channel_id=1, replica_groups=mesh['lag'=32,'pts'=8] {'lag'}, dimensions={0} | all-to-all | bytes 1048576 | tf_op jit(solution)/shard_map/all_to_all | solution.py:251
  163.3 0.1 broadcast_in_dim.8
  163.4 22.9 %all_to_all.28 = f32[32,4,8,128]{3,2,1,0:T(8,128)S(1)} all-to-all(f32[32,4,8,128]{3,2,1,0:T(8,128)S(1)} %broadcast_in_dim.8), channel_id=1, replica_groups=mesh['lag'=32,'pts'=8] {'lag'}, dimensions={0} | all-to-all | bytes 1048576 | tf_op jit(solution)/shard_map/all_to_all | solution.py:252
  186.3 0.8 copy.19
  (33 shorter events, 0.2 us)
Async XLA Ops:
  0.0 6.6 %copy-start.2 = (bf16[6,2048,128]{2,1,0:T(8,128)(2,1)S(1)}, bf16[6,2048,128]{2,1,0:T(8,128)(2,1)}, u32[]{:S(2)}) copy-start(bf16[6,2048,128]{2,1,0:T(8,128)(2,1)} %rest_1_.4) | copy-start | bytes 9437188
  1.7 22.3 %collective-permute-start.7 = (bf16[3,2048,128]{2,1,0:T(8,128)(2,1)S(1)}, bf16[3,2048,128]{2,1,0:T(8,128)(2,1)S(1)}, u32[]{:S(2)}, u32[]{:S(2)}) collective-permute-start(bf16[3,2048,128]{2,1,0:T(8,128)(2,1)S(1)} %slice.29), channel_id=1, source_target_pairs={{0,8},{8,16},{16,24},{24,32},{32,40},{40,48},{48,56},{56,64},{64,7... | collective-permute-start | bytes 4718600 | tf_op jit(solution)/shard_map/ppermute | solution.py:268
  6.6 2.8 %copy-start = (bf16[192,128,128]{2,1,0:T(8,128)(2,1)S(1)}, bf16[192,128,128]{2,1,0:T(8,128)(2,1)}, u32[]{:S(2)}) copy-start(bf16[192,128,128]{2,1,0:T(8,128)(2,1)} %blocks_h.9) | copy-start | bytes 18874372
  9.4 0.7 copy-start.4
  10.1 0.7 copy-start.6
  10.8 0.7 copy-start.8
  11.4 0.7 copy-start.10
  19.0 17.5 %collective-permute-start = (f32[2,128,128]{2,1,0:T(8,128)S(1)}, f32[2,128,128]{2,1,0:T(8,128)S(1)}, u32[]{:S(2)}, u32[]{:S(2)}) collective-permute-start(f32[2,128,128]{2,1,0:T(8,128)S(1)} %bitcast.46), channel_id=1, source_target_pairs={{8,0},{24,16},{40,32},{56,48},{72,64},{88,80},{104,96},{120,112},{... | collective-permute-start | bytes 393224 | tf_op jit(solution)/shard_map/ppermute | solution.py:236
  35.1 10.8 %copy-start.12 = (bf16[4,256,128]{2,1,0:T(8,128)(2,1)S(1)}, bf16[4,256,128]{2,1,0:T(8,128)(2,1)}, u32[]{:S(2)}) copy-start(bf16[4,256,128]{2,1,0:T(8,128)(2,1)} %param.9) | copy-start | bytes 786436
  35.1 10.9 %copy-start.3 = (f32[256,128]{1,0:T(8,128)S(1)}, f32[256,128]{1,0:T(8,128)}, u32[]{:S(2)}) copy-start(f32[256,128]{1,0:T(8,128)} %rest_6_.1) | copy-start | bytes 393220
  35.1 2.8 %collective-permute-start.8 = (f32[3,2,128,128]{3,2,1,0:T(8,128)S(1)}, f32[3,2,128,128]{3,2,1,0:T(8,128)S(1)}, u32[]{:S(2)}, u32[]{:S(2)}) collective-permute-start(f32[3,2,128,128]{3,2,1,0:T(8,128)S(1)} %fields_3.1), channel_id=1, source_target_pairs={{8,0},{24,16},{40,32},{56,48},{72,64},{88,80},{104,96},{120,112},{... | collective-permute-start | bytes 1179656 | tf_op jit(solution)/shard_map/ppermute | solution.py:236
  36.6 4.1 %collective-permute-start.1 = (f32[2,128,128]{2,1,0:T(8,128)S(1)}, f32[2,128,128]{2,1,0:T(8,128)S(1)}, u32[]{:S(2)}, u32[]{:S(2)}) collective-permute-start(f32[2,128,128]{2,1,0:T(8,128)S(1)} %bitcast_add_fusion), channel_id=1, source_target_pairs={{16,0},{80,64},{144,128},{208,192},{17,1},{81,65},{145,129},{209,1... | collective-permute-start | bytes 393224 | tf_op jit(solution)/shard_map/ppermute | solution.py:236
  37.9 4.9 %collective-permute-start.10 = (f32[3,2,128,128]{3,2,1,0:T(8,128)S(1)}, f32[3,2,128,128]{3,2,1,0:T(8,128)S(1)}, u32[]{:S(2)}, u32[]{:S(2)}) collective-permute-start(f32[3,2,128,128]{3,2,1,0:T(8,128)S(1)} %add.49), channel_id=1, source_target_pairs={{32,0},{96,64},{160,128},{224,192},{33,1},{97,65},{161,129},{225,1... | collective-permute-start | bytes 1179656 | tf_op jit(solution)/shard_map/ppermute | solution.py:236
  38.6 4.9 %collective-permute-start.11 = (f32[3,2,128,128]{3,2,1,0:T(8,128)S(1)}, f32[3,2,128,128]{3,2,1,0:T(8,128)S(1)}, u32[]{:S(2)}, u32[]{:S(2)}) collective-permute-start(f32[3,2,128,128]{3,2,1,0:T(8,128)S(1)} %add.49), channel_id=1, source_target_pairs={{48,0},{112,64},{176,128},{240,192},{49,1},{113,65},{177,129},{241... | collective-permute-start | bytes 1179656 | tf_op jit(solution)/shard_map/ppermute | solution.py:236
  39.3 4.2 %collective-permute-start.9 = (f32[3,2,128,128]{3,2,1,0:T(8,128)S(1)}, f32[3,2,128,128]{3,2,1,0:T(8,128)S(1)}, u32[]{:S(2)}, u32[]{:S(2)}) collective-permute-start(f32[3,2,128,128]{3,2,1,0:T(8,128)S(1)} %add.49), channel_id=1, source_target_pairs={{16,0},{80,64},{144,128},{208,192},{17,1},{81,65},{145,129},{209,1... | collective-permute-start | bytes 1179656 | tf_op jit(solution)/shard_map/ppermute | solution.py:236
  40.0 1.4 collective-permute-start.2
  40.7 0.7 collective-permute-start.3
  41.4 3.7 %collective-permute-start.4 = (f32[2,128,128]{2,1,0:T(8,128)S(1)}, f32[2,128,128]{2,1,0:T(8,128)S(1)}, u32[]{:S(2)}, u32[]{:S(2)}) collective-permute-start(f32[2,128,128]{2,1,0:T(8,128)S(1)} %add_add_fusion.3), channel_id=1, source_target_pairs={{64,0},{65,1},{66,2},{67,3},{68,4},{69,5},{70,6},{71,7}} | collective-permute-start | bytes 393224 | tf_op jit(solution)/shard_map/ppermute | solution.py:236
  42.1 3.8 %collective-permute-start.5 = (f32[2,128,128]{2,1,0:T(8,128)S(1)}, f32[2,128,128]{2,1,0:T(8,128)S(1)}, u32[]{:S(2)}, u32[]{:S(2)}) collective-permute-start(f32[2,128,128]{2,1,0:T(8,128)S(1)} %add_add_fusion.3), channel_id=1, source_target_pairs={{128,0},{129,1},{130,2},{131,3},{132,4},{133,5},{134,6},{135,7}} | collective-permute-start | bytes 393224 | tf_op jit(solution)/shard_map/ppermute | solution.py:236
  42.8 3.1 %collective-permute-start.6 = (f32[2,128,128]{2,1,0:T(8,128)S(1)}, f32[2,128,128]{2,1,0:T(8,128)S(1)}, u32[]{:S(2)}, u32[]{:S(2)}) collective-permute-start(f32[2,128,128]{2,1,0:T(8,128)S(1)} %add_add_fusion.3), channel_id=1, source_target_pairs={{192,0},{193,1},{194,2},{195,3},{196,4},{197,5},{198,6},{199,7}} | collective-permute-start | bytes 393224 | tf_op jit(solution)/shard_map/ppermute | solution.py:236
  43.6 15.7 %copy-start.5 = (f32[6,128]{1,0:T(8,128)S(1)}, f32[6,128]{1,0:T(8,128)}, u32[]{:S(2)}) copy-start(f32[6,128]{1,0:T(8,128)} %rest_3_.1) | copy-start | bytes 9220
  43.6 15.7 %copy-start.7 = (s32[192]{0:T(256)S(1)}, s32[192]{0:T(256)}, u32[]{:S(2)}) copy-start(s32[192]{0:T(256)} %row_s.9) | copy-start | bytes 2308
  43.6 15.7 %copy-start.9 = (s32[192]{0:T(256)S(1)}, s32[192]{0:T(256)}, u32[]{:S(2)}) copy-start(s32[192]{0:T(256)} %col_s.9) | copy-start | bytes 2308
  43.6 15.7 %copy-start.11 = (s32[192]{0:T(256)S(1)}, s32[192]{0:T(256)}, u32[]{:S(2)}) copy-start(s32[192]{0:T(256)} %lag_s.9) | copy-start | bytes 2308
  43.6 8.5 %collective-permute-start.12 = (f32[3,2,128,128]{3,2,1,0:T(8,128)S(1)}, f32[3,2,128,128]{3,2,1,0:T(8,128)S(1)}, u32[]{:S(2)}, u32[]{:S(2)}) collective-permute-start(f32[3,2,128,128]{3,2,1,0:T(8,128)S(1)} %add_add_fusion.1), channel_id=1, source_target_pairs={{64,0},{65,1},{66,2},{67,3},{68,4},{69,5},{70,6},{71,7}} | collective-permute-start | bytes 1179656 | tf_op jit(solution)/shard_map/ppermute | solution.py:236
  44.5 7.7 %collective-permute-start.13 = (f32[3,2,128,128]{3,2,1,0:T(8,128)S(1)}, f32[3,2,128,128]{3,2,1,0:T(8,128)S(1)}, u32[]{:S(2)}, u32[]{:S(2)}) collective-permute-start(f32[3,2,128,128]{3,2,1,0:T(8,128)S(1)} %add_add_fusion.1), channel_id=1, source_target_pairs={{128,0},{129,1},{130,2},{131,3},{132,4},{133,5},{134,6},{135,7}} | collective-permute-start | bytes 1179656 | tf_op jit(solution)/shard_map/ppermute | solution.py:236
  45.2 7.0 %collective-permute-start.14 = (f32[3,2,128,128]{3,2,1,0:T(8,128)S(1)}, f32[3,2,128,128]{3,2,1,0:T(8,128)S(1)}, u32[]{:S(2)}, u32[]{:S(2)}) collective-permute-start(f32[3,2,128,128]{3,2,1,0:T(8,128)S(1)} %add_add_fusion.1), channel_id=1, source_target_pairs={{192,0},{193,1},{194,2},{195,3},{196,4},{197,5},{198,6},{199,7}} | collective-permute-start | bytes 1179656 | tf_op jit(solution)/shard_map/ppermute | solution.py:236
  47.1 12.2 %all-to-all-start = ((bf16[8,256,128]{2,1,0:T(8,128)(2,1)}), bf16[8,256,128]{2,1,0:T(8,128)(2,1)S(1)}, u32[]{:S(2)}, u32[]{:S(2)}) async-start(bf16[8,256,128]{2,1,0:T(8,128)(2,1)} %get-tuple-element.12), calls=%async_computation | async-start | bytes 1048576 | tf_op jit(solution)/shard_map/all_to_all | solution.py:282
  59.3 2.8 %copy-start.1 = (bf16[192,128,128]{2,1,0:T(8,128)(2,1)S(1)}, bf16[192,128,128]{2,1,0:T(8,128)(2,1)}, u32[]{:S(2)}) copy-start(bf16[192,128,128]{2,1,0:T(8,128)(2,1)} %blocks_h.9) | copy-start | bytes 18874372

commit v2 on v0

v2 whole, which is shorter than its diff:
```python
import functools

import jax
import jax.numpy as jnp
from jax import lax
from jax.experimental import pallas as pl
from jax.experimental.pallas import tpu as pltpu
from jax.sharding import PartitionSpec as P


STEPS = 4
UNROLL = 8
CHUNKS = 4
LIMIT = 24 << 20


def accumulate(acc, kernel_of, picks_of, factor_of, row_of, entries):
    steps, row_blocks, _, modes = acc.shape

    sums = [[None] * row_blocks for _ in range(steps)]
    for entry in entries:
        picks = picks_of(entry)
        pick = picks[0] if steps == 1 else jnp.concatenate(picks, axis=1)
        product = jnp.dot(kernel_of(entry), pick, preferred_element_type=jnp.float32)
        factor = factor_of(entry)
        row = row_of(entry)
        for k in range(steps):
            part = product[:, k * modes : (k + 1) * modes]
            if steps > 1:
                acc[k, row] += part * factor
                continue
            for r in range(row_blocks):
                term = part * jnp.where(row == r, factor, 0.0)
                sums[k][r] = term if sums[k][r] is None else sums[k][r] + term
    if steps == 1:
        for r in range(row_blocks):
            acc[0, r] += sums[0][r]


def field_kernel(steps, halo_shapes, row_h, col_h, lag_h, mode_h, blocks_h, history_h, *rest):
    halos = rest[: len(halo_shapes)]
    rest = list(rest[len(halo_shapes) :])
    with_lists = len(steps) == 2
    out_ref = rest.pop(0)
    if with_lists:
        lists_ref = rest.pop(0)
    row_s, col_s, lag_s, mode_ref, acc, blocks_v, state_v, sems, state_sems, table_sems = rest
    table_copies = [
        pltpu.make_async_copy(source, target, table_sems.at[k])
        for k, (source, target) in enumerate(((row_h, row_s), (col_h, col_s), (lag_h, lag_s)))
    ]
    table_copies.append(pltpu.make_async_copy(mode_h, mode_ref, table_sems.at[3]))
    halo_lags = sum(halo_shapes)
    own_lags = state_v.shape[0] - halo_lags
    state_copies = [
        pltpu.make_async_copy(
            history_h.at[pl.ds(0, own_lags)],
            state_v.at[pl.ds(halo_lags, own_lags)],
            state_sems.at[0],
        )
    ]
    first = 0
    for k, halo in enumerate(halos):
        state_copies.append(
            pltpu.make_async_copy(
                halo, state_v.at[pl.ds(first, halo_shapes[k])], state_sems.at[k + 1]
            )
        )
        first += halo_shapes[k]
    for copy in table_copies + state_copies:
        copy.start()
    entries, size, _ = blocks_v.shape
    per = entries // CHUNKS

    def chunk_copy(c):
        part = pl.ds(c * per, per)
        return pltpu.make_async_copy(blocks_h.at[part], blocks_v.at[part], sems.at[c])

    for c in range(CHUNKS):
        chunk_copy(c).start()
    acc[...] = jnp.zeros_like(acc)

    def picks_of(entry):
        first = pl.multiple_of(col_s[entry] * size, size)
        lag = lag_s[entry]
        return [state_v[halo_lags + lag - s, pl.ds(first, size), :] for s in steps]

    def factor_of(entry):
        return mode_ref[pl.ds(lag_s[entry], 1), :]

    for copy in table_copies:
        copy.wait()
    if with_lists:
        kinds = STEPS - 1

        def place(entry, counts):
            lag = lag_s[entry]
            kind = jnp.minimum(lag, kinds)
            at = counts[kinds]
            for j in range(kinds):
                at = jnp.where(lag == j, counts[j], at)
            lists_ref[kind * entries + at] = entry + row_s[entry] * 1024 + col_s[entry] * 65536
            return tuple(count + jnp.where(kind == j, 1, 0) for j, count in enumerate(counts))

        counts = lax.fori_loop(0, entries, place, (jnp.int32(0),) * (kinds + 1))
        for j in range(kinds + 1):
            lists_ref[(kinds + 1) * entries + j] = counts[j]
    for copy in state_copies:
        copy.wait()

    def chunk(c, carry):
        chunk_copy(c).wait()
        accumulate(
            acc,
            lambda e: blocks_v[e],
            picks_of,
            factor_of,
            lambda e: row_s[e],
            [c * per + u for u in range(per)],
        )
        return carry

    lax.fori_loop(0, CHUNKS, chunk, 0)
    if with_lists:
        core = lax.axis_index("lag") % 2
        for k in range(2):
            out_ref[k ^ core] = acc[k]
    else:
        out_ref[...] = acc[...]


def fields(steps, halos, history, tables, row_blocks):
    block_row, block_col, lag_offset, kernel_blocks, mode_kernel = tables
    halo_shapes = tuple(halo.shape[0] for halo in halos)
    entries, size, _ = kernel_blocks.shape
    lags_held, points, modes = history.shape
    in_hbm = pl.BlockSpec(memory_space=pltpu.HBM)
    in_smem = pl.BlockSpec(memory_space=pltpu.SMEM)
    in_vmem = pl.BlockSpec(memory_space=pltpu.VMEM)
    shape = (len(steps), row_blocks, size, modes)
    out_shape = [jax.ShapeDtypeStruct(shape, jnp.float32)]
    out_specs = [in_vmem]
    if len(steps) == 2:
        out_shape.append(jax.ShapeDtypeStruct((STEPS * entries + STEPS,), jnp.int32))
        out_specs.append(in_smem)
    return pl.pallas_call(
        functools.partial(field_kernel, steps, halo_shapes),
        out_shape=out_shape,
        in_specs=[in_hbm] * 6 + [pl.BlockSpec(memory_space=pl.ANY)] * len(halos),
        out_specs=out_specs,
        scratch_shapes=[
            *[pltpu.SMEM((entries,), jnp.int32)] * 3,
            pltpu.VMEM(mode_kernel.shape, jnp.float32),
            pltpu.VMEM(shape, jnp.float32),
            pltpu.VMEM(kernel_blocks.shape, kernel_blocks.dtype),
            pltpu.VMEM((sum(halo_shapes) + lags_held - min(steps), points, modes), history.dtype),
            pltpu.SemaphoreType.DMA((CHUNKS,)),
            pltpu.SemaphoreType.DMA((1 + len(halos),)),
            pltpu.SemaphoreType.DMA((4,)),
        ],
        compiler_params=pltpu.CompilerParams(vmem_limit_bytes=LIMIT),
    )(
        *[
            in_hbm_only(v)
            for v in (block_row, block_col, lag_offset, mode_kernel, kernel_blocks, history)
        ],
        *halos,
    )


def halves(value):
    high = value.astype(jnp.bfloat16)
    return high, (value - high.astype(jnp.float32)).astype(jnp.bfloat16)


def solve_into(inverse_ref, net, density_ref, copies_ref):
    row_blocks, size = net.shape[0], net.shape[1]
    for r in range(row_blocks):
        inverse_high, inverse_low = halves(inverse_ref[pl.ds(r * size, size), :])
        net_high, net_low = halves(net[r])
        solved = jnp.dot(
            jnp.concatenate([inverse_high, inverse_low, inverse_high], axis=1),
            jnp.concatenate([net_low, net_high, net_high], axis=0),
            preferred_element_type=jnp.float32,
        )
        density_ref[pl.ds(r * size, size), :] = solved
        if copies_ref is not None:
            rounded = solved.astype(copies_ref.dtype)
            for p in range(copies_ref.shape[0]):
                copies_ref[p, pl.ds(r * size, size), :] = rounded


def first_kernel(incident_ref, field_ref, inverse_ref, density_ref, copies_ref):
    net = incident_ref[...].astype(jnp.float32).reshape(field_ref.shape) - field_ref[...]
    solve_into(inverse_ref, net, density_ref, copies_ref)


def chain_kernel(step, last, lists_s, blocks_h, *rest):
    fresh = rest[:step]
    rest = rest[step:]
    if last:
        mode_ref, incident_ref, field_ref, inverse_ref, density_ref, blocks_v, acc, sems = rest
        copies_ref = None
    else:
        mode_ref, incident_ref, field_ref, inverse_ref, density_ref, copies_ref, blocks_v, acc, sems = rest
    entries, size, _ = blocks_h.shape
    row_blocks = acc.shape[0]
    counts = [lists_s[STEPS * entries + j] for j in range(step)]
    groups = [(count + UNROLL - 1) // UNROLL for count in counts]
    firsts = [sum(groups[:j]) for j in range(step)]

    def code_of(j, g, u):
        at = g * UNROLL + u
        return at, lists_s[j * entries + jnp.minimum(at, counts[j] - 1)]

    for j in range(step):

        def begin(g, carry, j=j):
            slot = firsts[j] + g
            for u in range(UNROLL):
                _, code = code_of(j, g, u)
                pltpu.make_async_copy(
                    blocks_h.at[code % 1024], blocks_v.at[slot * UNROLL + u], sems.at[slot]
                ).start()
            return carry

        lax.fori_loop(0, groups[j], begin, 0)
    acc[...] = jnp.zeros_like(acc)
    for j in range(step):
        state = fresh[step - 1 - j]
        factor = mode_ref[pl.ds(j, 1), :]

        def group(g, carry, j=j, state=state, factor=factor):
            slot = firsts[j] + g
            pltpu.make_async_copy(
                blocks_h.at[pl.ds(0, UNROLL)], blocks_v.at[pl.ds(slot * UNROLL, UNROLL)], sems.at[slot]
            ).wait()
            sums = [None] * row_blocks
            for u in range(UNROLL):
                at, code = code_of(j, g, u)
                first = pl.multiple_of(code // 65536 * size, size)
                product = jnp.dot(
                    blocks_v[slot * UNROLL + u],
                    state[pl.ds(first, size), :],
                    preferred_element_type=jnp.float32,
                )
                row = jnp.where(at < counts[j], code // 1024 % 64, row_blocks)
                for r in range(row_blocks):
                    term = product * jnp.where(row == r, factor, 0.0)
                    sums[r] = term if sums[r] is None else sums[r] + term
            for r in range(row_blocks):
                acc[r] += sums[r]
            return carry

        lax.fori_loop(0, groups[j], group, 0)
    net = incident_ref[...].astype(jnp.float32).reshape(acc.shape) - field_ref[...] - acc[...]
    solve_into(inverse_ref, net, density_ref, copies_ref)


def densities_of(step, peers, fresh, incident, field, inverse, mode_kernel, blocks, lists):
    row_blocks, size, modes = field.shape
    rows = row_blocks * size
    last = step == STEPS - 1
    in_vmem = pl.BlockSpec(memory_space=pltpu.VMEM)
    in_smem = pl.BlockSpec(memory_space=pltpu.SMEM)
    density = jax.ShapeDtypeStruct((rows, modes), jnp.float32)
    copies = jax.ShapeDtypeStruct((peers, rows, modes), jnp.bfloat16)
    params = pltpu.CompilerParams(vmem_limit_bytes=LIMIT)
    if step == 0:
        return pl.pallas_call(
            first_kernel,
            out_shape=(density, copies),
            in_specs=[in_vmem] * 3,
            out_specs=(in_vmem, in_vmem),
            compiler_params=params,
            name="first_density",
        )(incident, field, inverse)
    slots = blocks.shape[0] // UNROLL + step
    return pl.pallas_call(
        functools.partial(chain_kernel, step, last),
        out_shape=(density,) if last else (density, copies),
        in_specs=[in_smem, pl.BlockSpec(memory_space=pltpu.HBM)] + [in_vmem] * (step + 4),
        out_specs=(in_vmem,) if last else (in_vmem, in_vmem),
        scratch_shapes=[
            pltpu.VMEM(((slots * UNROLL), *blocks.shape[1:]), blocks.dtype),
            pltpu.VMEM(field.shape, jnp.float32),
            pltpu.SemaphoreType.DMA((slots,)),
        ],
        compiler_params=params,
    )(lists, in_hbm_only(blocks), *fresh, mode_kernel, incident, field, inverse)


def lag_of(x_hi, z, core):
    return x_hi * 16 + z % 8 * 2 + core


def routes(cores, pairs):
    return [(lag_of(*a, c), lag_of(*b, c)) for a, b in pairs for c in range(cores)]


BOTH = (0, 1)
TO_CORE_0 = [(lag_of(x, z, 1), lag_of(x, z, 0)) for x in BOTH for z in range(8)]
SWAP = TO_CORE_0 + [(b, a) for a, b in TO_CORE_0]
FROM_CORE_0 = [(b, a) for a, b in TO_CORE_0]
HUBS = [[((x, q + k), (x, q)) for x in BOTH for q in (0, 4)] for k in (1, -1, 2)]
TOPS = [[((0, 4), (0, 0))], [((1, 0), (0, 0))], [((1, 4), (0, 0))]]
ACROSS = [((1, 0), (0, 0)), ((1, 4), (0, 4))]
ALONG = [((0, 4), (0, 0))]


def turned(pairs):
    return [(b, a) for a, b in pairs]


def plus_arrived(value, *levels, operand=None):
    operand = value if operand is None else operand
    arrived = [lax.ppermute(operand, "lag", pairs) for pairs in levels]
    for piece in arrived:
        value = value + piece
    return value


def in_hbm_only(value):
    return pltpu.with_memory_space_constraint(value, pltpu.HBM)


def after(value, other):
    return lax.optimization_barrier((value, other))[0]


def to_everyone(copies):
    everyone = lax.all_to_all(copies, "pts", 0, 0, tiled=True)
    return everyone.reshape(-1, copies.shape[-1])


UP_HUBS = [routes(1, pairs) for pairs in HUBS]
UP_TOPS = [routes(1, pairs) for pairs in TOPS]
DOWN_HUBS = [routes(1, turned(pairs)) for pairs in HUBS]
DOWN_TOPS = [routes(1, turned(pairs)) for pairs in TOPS]


def per_device(
    history, incident, kernel_blocks, block_row, block_col, lag_offset, mode_kernel, self_inverse
):
    size = kernel_blocks.shape[1]
    row_blocks = self_inverse.shape[0] // size
    peers = lax.axis_size("pts")
    lags = lax.axis_size("lag")
    first = lax.axis_index("lag") == 0
    lags_held = history.shape[0]
    next_lag = [(i, i + 1) for i in range(lags - 1)]
    tables = (block_row, block_col, lag_offset, kernel_blocks, mode_kernel)
    halo_1 = lax.ppermute(history[lags_held - 1 :], "lag", next_lag)
    (now,) = fields((0,), [], history, tables, row_blocks)
    now = plus_arrived(now[0], TO_CORE_0)
    halo_2 = lax.ppermute(
        after(history, now)[lags_held - 3 : lags_held - 1], "lag", next_lag
    )
    (second,) = fields((1,), [after(halo_1, now)], history, tables, row_blocks)
    now = plus_arrived(now, *UP_HUBS)
    second = plus_arrived(second[0], TO_CORE_0)
    now = plus_arrived(now, *UP_TOPS)
    second = plus_arrived(second, *UP_HUBS)
    args = (self_inverse, mode_kernel, kernel_blocks)
    density_0, copies = densities_of(0, peers, [], incident[0], now, *args, None)
    fresh = [to_everyone(copies)]
    second = plus_arrived(second, *UP_TOPS)
    pair, lists = fields((2, 3), [after(halo_2, copies), halo_1], history, tables, row_blocks)
    pair = plus_arrived(pair[0], SWAP, operand=pair[1])
    density_1, copies = densities_of(1, peers, fresh, incident[1], second, *args, lists)
    fresh.append(to_everyone(copies))
    pair = after(pair, copies)
    pair = plus_arrived(pair, *[routes(2, pairs) for pairs in HUBS])
    pair = plus_arrived(pair, routes(2, ACROSS))
    pair = plus_arrived(pair, routes(2, ALONG))
    early = jnp.stack([density_0, density_1])
    early = plus_arrived(jnp.where(first, early, 0.0), *DOWN_TOPS, operand=early)
    density_2, copies = densities_of(2, peers, fresh, incident[2], pair, *args, lists)
    fresh.append(to_everyone(copies))
    fourth = lax.ppermute(after(pair, copies), "lag", [(1, 0)])
    third = plus_arrived(jnp.where(first, density_2, 0.0), *DOWN_TOPS, operand=density_2)
    early = plus_arrived(after(early, copies), *DOWN_HUBS)
    early = plus_arrived(early, FROM_CORE_0)
    (density_3,) = densities_of(3, peers, fresh, incident[3], fourth, *args, lists)
    final = plus_arrived(jnp.where(first, density_3, 0.0), *DOWN_TOPS, operand=density_3)
    late = jnp.stack([third, final])
    late = plus_arrived(late, *DOWN_HUBS)
    late = plus_arrived(late, FROM_CORE_0)
    return jnp.concatenate([early, late])


def solution(mesh):
    return jax.shard_map(
        per_device,
        mesh=mesh,
        in_specs=(
            P("lag", None, None),
            P(None, "pts", None),
            P(("lag", "pts"), None, None),
            P(("lag", "pts")),
            P(("lag", "pts")),
            P(("lag", "pts")),
            P("lag", None),
            P("pts", None),
        ),
        out_specs=P(None, "pts", None),
        check_vma=False,
    )
```

time: 431 us -> 151 us (0.35); the launches traced: 424 us -> 149 us
  matrix products: 123 us -> 0 us
  local copies, waits for them, and re-layouts: 120 us -> 1.14 us
  waiting for transfers between devices: 76.7 us -> 29.2 us
  Pallas kernels: 0 us -> 36 us
  other arithmetic: 19.1 us -> 3.39 us
  starting transfers between devices: 83.5 us -> 78.3 us
    dot_general x12 -> x0, matrix products: 123 us -> none  [the longest x4 66.2 us: per_device(): jnp.dot(selector, products.reshape(entries, block_size * mode_cols), prec...]
    all_to_all x11 -> x3, waiting for transfers between devices: 76.7 us -> 0.01 us  [to_everyone(): everyone = lax.all_to_all(copies, 'pts', 0, 0, tiled=True)]
    all_to_all x11 -> x3, starting transfers between devices: 72.9 us -> 12.7 us  [to_everyone(): everyone = lax.all_to_all(copies, 'pts', 0, 0, tiled=True)]
    ppermute x3 -> x40, starting transfers between devices: 10.6 us -> 65.5 us  [the longest x37 50.5 us: plus_arrived(): arrived = [lax.ppermute(operand, 'lag', pairs) for pairs in levels]]
    dot_general x4 -> x0, local copies, waits for them, and re-layouts: 50.4 us -> none  [per_device(): jnp.einsum('eij,ejm->eim', kernel_blocks, picked, preferred_element_type=...]
    gather x4 -> x0, local copies, waits for them, and re-layouts: 39.6 us -> none  [per_device(): picked = by_block[lag_offset, block_col]]
    pallas_call x0 -> x7, Pallas kernels: none -> 36 us  [the longest x3 19.9 us: fields(): pl.pallas_call(functools.partial(field_kernel, steps, halo_shapes), out_s...]
    ppermute x3 -> x40, waiting for transfers between devices: 0.01 us -> 29.2 us  [the longest x37 29.1 us: plus_arrived(): arrived = [lax.ppermute(operand, 'lag', pairs) for pairs in levels]]
  transfers between devices with their start and end apart: 14 -> 43, of which waited for: 11 -> 5; matrix products, arithmetic and copies ran while one was open for 5% -> 2% of each run, Pallas kernels for 0% -> 20%
where the time goes in v2:
time: 151 us; the launch traced here: 149 us
  starting transfers between devices  78.3 us (52%)
  Pallas kernels  36 us (24%)
  waiting for transfers between devices  29.2 us (19%)
  other arithmetic  3.39 us (2%)
    ppermute x37, starting transfers between devices, plus_arrived(): arrived = [lax.ppermute(operand, 'lag', pairs) for pairs in levels]  50.5 us
    ppermute x37, waiting for transfers between devices, plus_arrived(): arrived = [lax.ppermute(operand, 'lag', pairs) for pairs in levels]  29.1 us
    pallas_call x3, Pallas kernels, fields(): pl.pallas_call(functools.partial(field_kernel, steps, halo_shapes), out_s...  19.9 us
    pallas_call x3, Pallas kernels, densities_of(): pl.pallas_call(functools.partial(chain_kernel, step, last), out_shape=(de...  15.1 us
    all_to_all x3, starting transfers between devices, to_everyone(): everyone = lax.all_to_all(copies, 'pts', 0, 0, tiled=True)  12.7 us
    ppermute x1, starting transfers between devices, per_device(): lax.ppermute(after(history, now)[lags_held - 3:lags_held - 1], 'lag', nex...  6.67 us
    ppermute x1, starting transfers between devices, per_device(): fourth = lax.ppermute(after(pair, copies), 'lag', [(1, 0)])  6.42 us
  transfers between devices with their start and end apart: 43, of which 5 were waited for; matrix products, arithmetic and copies ran while one was open for 2% of the time, Pallas kernels for 20%

profile of v2, /device:TPU:1, one launch (start us, length us, event | category | flops | bytes accessed | tf_op | source)
XLA Modules:
  0.0 148.8 jit_solution(1766989394675488305)
XLA Ops:
  0.0 6.1 %shard_map.82 = f32[1,2,128,128]{3,2,1,0:T(8,128)S(1)} custom-call(s32[192]{0:T(256)} %row_h.5, s32[192]{0:T(256)} %col_h.5, s32[192]{0:T(256)} %lag_h.5, f32[6,128]{1,0:T(8,128)} %rest_3_.1, bf16[192,128,128]{2,1,0:T(8,128)(2,1)} %blocks_h.11, bf16[6,2048,128]{2,1,0:T(8,128)(2,1)} %history_h.5), custom_call_target="tpu_custom_call" | custom-call | tf_op jit(solution)/shard_map/pallas_call | solution.py:146
  6.2 5.1 %collective-permute-start = (f32[2,128,128]{2,1,0:T(8,128)S(1)}, f32[2,128,128]{2,1,0:T(8,128)S(1)}, u32[]{:S(2)}, u32[]{:S(2)}) collective-permute-start(f32[2,128,128]{2,1,0:T(8,128)S(1)} %bitcast.32), channel_id=1, source_target_pairs={{8,0},{24,16},{40,32},{56,48},{72,64},{88,80},{104,96},{120,112},{... | collective-permute-start | bytes 393224 | tf_op jit(solution)/shard_map/ppermute | solution.py:317
  11.3 1.9 %collective-permute-start.8 = (bf16[1,2048,128]{2,1,0:T(8,128)(2,1)S(1)}, bf16[1,2048,128]{2,1,0:T(8,128)(2,1)S(1)}, u32[]{:S(2)}, u32[]{:S(2)}) collective-permute-start(bf16[1,2048,128]{2,1,0:T(8,128)(2,1)S(1)} %slice.26), channel_id=1, source_target_pairs={{0,8},{8,16},{16,24},{24,32},{32,40},{40,48},{48,56},{56,64},{64,7... | collective-permute-start | bytes 1572872 | tf_op jit(solution)/shard_map/ppermute | solution.py:353
  13.3 0.7 collective-permute-start.3
  14.0 0.7 collective-permute-start.2
  14.6 0.7 collective-permute-start.1
  15.3 1.1 slice.25
  16.4 6.7 %collective-permute-start.7 = (bf16[2,2048,128]{2,1,0:T(8,128)(2,1)}, bf16[2,2048,128]{2,1,0:T(8,128)(2,1)S(1)}, u32[]{:S(2)}, u32[]{:S(2)}) collective-permute-start(bf16[2,2048,128]{2,1,0:T(8,128)(2,1)} %slice.25), channel_id=1, source_target_pairs={{0,8},{8,16},{16,24},{24,32},{32,40},{40,48},{48,56},{56,64},{64,7... | collective-permute-start | bytes 3145736 | tf_op jit(solution)/shard_map/ppermute | solution.py:356
  23.1 4.9 %shard_map.84 = f32[1,2,128,128]{3,2,1,0:T(8,128)S(1)} custom-call(s32[192]{0:T(256)} %row_h.5, s32[192]{0:T(256)} %col_h.5, s32[192]{0:T(256)} %lag_h.5, f32[6,128]{1,0:T(8,128)} %rest_3_.1, bf16[192,128,128]{2,1,0:T(8,128)(2,1)} %blocks_h.11, bf16[6,2048,128]{2,1,0:T(8,128)(2,1)} %history_h.5, bf16[1,2048,128]{2,1,0:T(8,128)(2,1)S(1)} %collective-permute-done.8.rest_1_.rest_0_), custom_call_target="tpu_custom_call" | custom-call | tf_op jit(solution)/shard_map/pallas_call | solution.py:146
  28.0 1.3 collective-permute-start.9
  31.5 0.7 collective-permute-start.12
  33.6 1.0 first_density.1
  34.6 3.5 %all-to-all-start = ((bf16[8,256,128]{2,1,0:T(8,128)(2,1)}), bf16[8,256,128]{2,1,0:T(8,128)(2,1)S(1)}, u32[]{:S(2)}, u32[]{:S(2)}) async-start(bf16[8,256,128]{2,1,0:T(8,128)(2,1)} %get-tuple-element.21), calls=%async_computation | async-start | bytes 1048576 | tf_op jit(solution)/shard_map/all_to_all | solution.py:332
  40.2 8.9 %shard_map.83 = (f32[2,2,128,128]{3,2,1,0:T(8,128)S(1)}, s32[772]{0:T(1024)S(1)}) custom-call(s32[192]{0:T(256)} %row_h.5, s32[192]{0:T(256)} %col_h.5, s32[192]{0:T(256)} %lag_h.5, f32[6,128]{1,0:T(8,128)} %rest_3_.1, bf16[192,128,128]{2,1,0:T(8,128)(2,1)} %blocks_h.11, bf16[6,2048,128]{2,1,0:T(8,128)(2,1)} %history_h.5, ...), custom_call_target="tpu_custom_call" | custom-call | tf_op jit(solution)/shard_map/pallas_call | solution.py:146
  49.1 15.0 %collective-permute-start.19 = (f32[2,128,128]{2,1,0:T(8,128)S(1)}, f32[2,128,128]{2,1,0:T(8,128)S(1)}, u32[]{:S(2)}, u32[]{:S(2)}) collective-permute-start(f32[2,128,128]{2,1,0:T(8,128)S(1)} %slice_bitcast_fusion), channel_id=1, source_target_pairs={{8,0},{24,16},{40,32},{56,48},{72,64},{88,80},{104,96},{120,112},{... | collective-permute-start | bytes 393224 | tf_op jit(solution)/shard_map/ppermute | solution.py:317
  64.2 4.0 %shard_map.85 = (f32[256,128]{1,0:T(8,128)S(1)}, bf16[8,256,128]{2,1,0:T(8,128)(2,1)}) custom-call(s32[772]{0:T(1024)S(1)} %get-tuple-element.23.lists_s, bf16[192,128,128]{2,1,0:T(8,128)(2,1)} %blocks_h.11, bf16[2048,128]{1,0:T(8,128)(2,1)S(1)} %bitcast.25, f32[6,128]{1,0:T(8,128)S(1)} %copy-done.1, bf16[256,128]{1,0:T(8,128)(2,1)S(1)} %get-tuple-element.34.rest_2_, ...), custom_call_target="tpu_custom_call" | custom-call | tf_op jit(solution)/shard_map/pallas_call | solution.py:279
  68.2 1.3 collective-permute-start.22
  69.5 1.3 collective-permute-start.21
  70.8 1.3 collective-permute-start.20
  72.1 5.4 %all-to-all-start.1 = ((bf16[8,256,128]{2,1,0:T(8,128)(2,1)}), bf16[8,256,128]{2,1,0:T(8,128)(2,1)S(1)}, u32[]{:S(2)}, u32[]{:S(2)}) async-start(bf16[8,256,128]{2,1,0:T(8,128)(2,1)} %get-tuple-element.26), calls=%async_computation.1 | async-start | bytes 1048576 | tf_op jit(solution)/shard_map/all_to_all | solution.py:332
  77.6 1.7 %collective-permute-done.20 = f32[2,128,128]{2,1,0:T(8,128)S(1)} collective-permute-done((f32[2,128,128]{2,1,0:T(8,128)S(1)}, f32[2,128,128]{2,1,0:T(8,128)S(1)}, u32[]{:S(2)}, u32[]{:S(2)}) %collective-permute-start.20) | collective-permute-done | bytes 131104 | tf_op jit(solution)/shard_map/ppermute | solution.py:317
  79.3 1.3 collective-permute-start.23
  80.6 10.9 %collective-permute-done.23 = f32[2,128,128]{2,1,0:T(8,128)S(1)} collective-permute-done((f32[2,128,128]{2,1,0:T(8,128)S(1)}, f32[2,128,128]{2,1,0:T(8,128)S(1)}, u32[]{:S(2)}, u32[]{:S(2)}) %collective-permute-start.23) | collective-permute-done | bytes 131104 | tf_op jit(solution)/shard_map/ppermute | solution.py:317
  91.6 1.3 collective-permute-start.24
  92.9 0.7 collective-permute-start.18
  93.6 0.7 collective-permute-start.17
  94.3 1.4 collective-permute-start.16
  95.6 6.4 %collective-permute-done.24 = f32[2,128,128]{2,1,0:T(8,128)S(1)} collective-permute-done((f32[2,128,128]{2,1,0:T(8,128)S(1)}, f32[2,128,128]{2,1,0:T(8,128)S(1)}, u32[]{:S(2)}, u32[]{:S(2)}) %collective-permute-start.24) | collective-permute-done | bytes 131104 | tf_op jit(solution)/shard_map/ppermute | solution.py:317
  102.1 5.4 %shard_map.86 = (f32[256,128]{1,0:T(8,128)S(1)}, bf16[8,256,128]{2,1,0:T(8,128)(2,1)}) custom-call(s32[772]{0:T(1024)S(1)} %get-tuple-element.23.lists_s, bf16[192,128,128]{2,1,0:T(8,128)(2,1)} %blocks_h.11, bf16[2048,128]{1,0:T(8,128)(2,1)S(1)} %bitcast.26, bf16[2048,128]{1,0:T(8,128)(2,1)S(1)} %bitcast.28, f32[6,128]{1,0:T(8,128)S(1)} %copy-done.1, ...), custom_call_target="tpu_custom_call" | custom-call | tf_op jit(solution)/shard_map/pallas_call | solution.py:279
  107.5 3.8 %all-to-all-start.2 = ((bf16[8,256,128]{2,1,0:T(8,128)(2,1)}), bf16[8,256,128]{2,1,0:T(8,128)(2,1)S(1)}, u32[]{:S(2)}, u32[]{:S(2)}) async-start(bf16[8,256,128]{2,1,0:T(8,128)(2,1)} %get-tuple-element.29), calls=%async_computation.2 | async-start | bytes 1048576 | tf_op jit(solution)/shard_map/all_to_all | solution.py:332
  111.9 1.3 collective-permute-start.30
  113.3 1.3 collective-permute-start.29
  114.6 6.4 %collective-permute-start.32 = (f32[2,128,128]{2,1,0:T(8,128)S(1)}, f32[2,128,128]{2,1,0:T(8,128)S(1)}, u32[]{:S(2)}, u32[]{:S(2)}) collective-permute-start(f32[2,128,128]{2,1,0:T(8,128)S(1)} %add.133.rest_4_), channel_id=1, source_target_pairs={{8,0},{9,1},{10,2},{11,3},{12,4},{13,5},{14,6},{15,7}} | collective-permute-start | bytes 393224 | tf_op jit(solution)/shard_map/ppermute | solution.py:380
  121.0 1.0 add_add_fusion.2
  122.1 0.7 collective-permute-start.27
  122.8 0.7 collective-permute-start.26
  123.5 5.7 %shard_map.87 = f32[256,128]{1,0:T(8,128)S(1)} custom-call(s32[772]{0:T(1024)S(1)} %get-tuple-element.23.lists_s, bf16[192,128,128]{2,1,0:T(8,128)(2,1)} %blocks_h.11, bf16[2048,128]{1,0:T(8,128)(2,1)S(1)} %bitcast.27, bf16[2048,128]{1,0:T(8,128)(2,1)S(1)} %bitcast.29, bf16[2048,128]{1,0:T(8,128)(2,1)S(1)} %bitcast.30, f32[6,128]{1,0:T(8,128)S(1)} %copy-done.1, ...), custom_call_target="tpu_custom_call" | custom-call | tf_op jit(solution)/shard_map/pallas_call | solution.py:279
  129.2 0.7 collective-permute-start.35
  131.2 1.0 add_bitcast_fusion.1
  132.2 0.7 collective-permute-start.25
  133.0 0.7 collective-permute-start.38
  133.7 0.7 collective-permute-start.37
  134.4 0.7 collective-permute-start.36
  135.2 1.3 collective-permute-start.28
  136.6 1.3 collective-permute-start.39
  137.9 4.8 %collective-permute-done.28 = f32[2,256,128]{2,1,0:T(8,128)S(1)} collective-permute-done((f32[2,256,128]{2,1,0:T(8,128)S(1)}, f32[2,256,128]{2,1,0:T(8,128)S(1)}, u32[]{:S(2)}, u32[]{:S(2)}) %collective-permute-start.28) | collective-permute-done | bytes 262176 | tf_op jit(solution)/shard_map/ppermute | solution.py:317
  142.7 5.2 %collective-permute-done.39 = f32[2,256,128]{2,1,0:T(8,128)S(1)} collective-permute-done((f32[2,256,128]{2,1,0:T(8,128)S(1)}, f32[2,256,128]{2,1,0:T(8,128)S(1)}, u32[]{:S(2)}, u32[]{:S(2)}) %collective-permute-start.39) | collective-permute-done | bytes 262176 | tf_op jit(solution)/shard_map/ppermute | solution.py:317
  147.9 0.8 pad_maximum_fusion
  (77 shorter events, 8.1 us)
Async XLA Ops:
  0.0 11.3 %copy-start.2 = (bf16[6,2048,128]{2,1,0:T(8,128)(2,1)S(1)}, bf16[6,2048,128]{2,1,0:T(8,128)(2,1)}, u32[]{:S(2)}) copy-start(bf16[6,2048,128]{2,1,0:T(8,128)(2,1)} %history_h.5) | copy-start | bytes 9437188
  0.0 23.1 %copy-start.3 = (bf16[4,256,128]{2,1,0:T(8,128)(2,1)S(1)}, bf16[4,256,128]{2,1,0:T(8,128)(2,1)}, u32[]{:S(2)}) copy-start(bf16[4,256,128]{2,1,0:T(8,128)(2,1)} %param.9) | copy-start | bytes 786436
  6.2 7.1 %collective-permute-start = (f32[2,128,128]{2,1,0:T(8,128)S(1)}, f32[2,128,128]{2,1,0:T(8,128)S(1)}, u32[]{:S(2)}, u32[]{:S(2)}) collective-permute-start(f32[2,128,128]{2,1,0:T(8,128)S(1)} %bitcast.32), channel_id=1, source_target_pairs={{8,0},{24,16},{40,32},{56,48},{72,64},{88,80},{104,96},{120,112},{... | collective-permute-start | bytes 393224 | tf_op jit(solution)/shard_map/ppermute | solution.py:317
  11.3 11.8 %collective-permute-start.8 = (bf16[1,2048,128]{2,1,0:T(8,128)(2,1)S(1)}, bf16[1,2048,128]{2,1,0:T(8,128)(2,1)S(1)}, u32[]{:S(2)}, u32[]{:S(2)}) collective-permute-start(bf16[1,2048,128]{2,1,0:T(8,128)(2,1)S(1)} %slice.26), channel_id=1, source_target_pairs={{0,8},{8,16},{16,24},{24,32},{32,40},{40,48},{48,56},{56,64},{64,7... | collective-permute-start | bytes 1572872 | tf_op jit(solution)/shard_map/ppermute | solution.py:353
  13.3 16.0 %collective-permute-start.3 = (f32[2,128,128]{2,1,0:T(8,128)S(1)}, f32[2,128,128]{2,1,0:T(8,128)S(1)}, u32[]{:S(2)}, u32[]{:S(2)}) collective-permute-start(f32[2,128,128]{2,1,0:T(8,128)S(1)} %bitcast_add_fusion.2), channel_id=1, source_target_pairs={{32,0},{96,64},{160,128},{224,192},{33,1},{97,65},{161,129},{225,1... | collective-permute-start | bytes 393224 | tf_op jit(solution)/shard_map/ppermute | solution.py:317
  14.0 15.4 %collective-permute-start.2 = (f32[2,128,128]{2,1,0:T(8,128)S(1)}, f32[2,128,128]{2,1,0:T(8,128)S(1)}, u32[]{:S(2)}, u32[]{:S(2)}) collective-permute-start(f32[2,128,128]{2,1,0:T(8,128)S(1)} %bitcast_add_fusion.2), channel_id=1, source_target_pairs={{112,0},{48,64},{240,128},{176,192},{113,1},{49,65},{241,129},{177... | collective-permute-start | bytes 393224 | tf_op jit(solution)/shard_map/ppermute | solution.py:317
  14.6 14.7 %collective-permute-start.1 = (f32[2,128,128]{2,1,0:T(8,128)S(1)}, f32[2,128,128]{2,1,0:T(8,128)S(1)}, u32[]{:S(2)}, u32[]{:S(2)}) collective-permute-start(f32[2,128,128]{2,1,0:T(8,128)S(1)} %bitcast_add_fusion.2), channel_id=1, source_target_pairs={{16,0},{80,64},{144,128},{208,192},{17,1},{81,65},{145,129},{209,1... | collective-permute-start | bytes 393224 | tf_op jit(solution)/shard_map/ppermute | solution.py:317
  16.4 17.2 %copy-start = (f32[256,128]{1,0:T(8,128)S(1)}, f32[256,128]{1,0:T(8,128)}, u32[]{:S(2)}) copy-start(f32[256,128]{1,0:T(8,128)} %rest_6_.1) | copy-start | bytes 393220
  16.4 23.8 %collective-permute-start.7 = (bf16[2,2048,128]{2,1,0:T(8,128)(2,1)}, bf16[2,2048,128]{2,1,0:T(8,128)(2,1)S(1)}, u32[]{:S(2)}, u32[]{:S(2)}) collective-permute-start(bf16[2,2048,128]{2,1,0:T(8,128)(2,1)} %slice.25), channel_id=1, source_target_pairs={{0,8},{8,16},{16,24},{24,32},{32,40},{40,48},{48,56},{56,64},{64,7... | collective-permute-start | bytes 3145736 | tf_op jit(solution)/shard_map/ppermute | solution.py:356
  28.0 3.4 %collective-permute-start.9 = (f32[2,128,128]{2,1,0:T(8,128)S(1)}, f32[2,128,128]{2,1,0:T(8,128)S(1)}, u32[]{:S(2)}, u32[]{:S(2)}) collective-permute-start(f32[2,128,128]{2,1,0:T(8,128)S(1)} %bitcast.31), channel_id=1, source_target_pairs={{8,0},{24,16},{40,32},{56,48},{72,64},{88,80},{104,96},{120,112},{... | collective-permute-start | bytes 393224 | tf_op jit(solution)/shard_map/ppermute | solution.py:317
  29.4 2.7 %collective-permute-start.6 = (f32[2,128,128]{2,1,0:T(8,128)S(1)}, f32[2,128,128]{2,1,0:T(8,128)S(1)}, u32[]{:S(2)}, u32[]{:S(2)}) collective-permute-start(f32[2,128,128]{2,1,0:T(8,128)S(1)} %add_add_fusion.7), channel_id=1, source_target_pairs={{192,0},{193,1},{194,2},{195,3},{196,4},{197,5},{198,6},{199,7}} | collective-permute-start | bytes 393224 | tf_op jit(solution)/shard_map/ppermute | solution.py:317
  30.1 2.8 %collective-permute-start.5 = (f32[2,128,128]{2,1,0:T(8,128)S(1)}, f32[2,128,128]{2,1,0:T(8,128)S(1)}, u32[]{:S(2)}, u32[]{:S(2)}) collective-permute-start(f32[2,128,128]{2,1,0:T(8,128)S(1)} %add_add_fusion.7), channel_id=1, source_target_pairs={{128,0},{129,1},{130,2},{131,3},{132,4},{133,5},{134,6},{135,7}} | collective-permute-start | bytes 393224 | tf_op jit(solution)/shard_map/ppermute | solution.py:317
  30.7 2.8 %collective-permute-start.4 = (f32[2,128,128]{2,1,0:T(8,128)S(1)}, f32[2,128,128]{2,1,0:T(8,128)S(1)}, u32[]{:S(2)}, u32[]{:S(2)}) collective-permute-start(f32[2,128,128]{2,1,0:T(8,128)S(1)} %add_add_fusion.7), channel_id=1, source_target_pairs={{64,0},{65,1},{66,2},{67,3},{68,4},{69,5},{70,6},{71,7}} | collective-permute-start | bytes 393224 | tf_op jit(solution)/shard_map/ppermute | solution.py:317
  31.5 6.6 %collective-permute-start.12 = (f32[2,128,128]{2,1,0:T(8,128)S(1)}, f32[2,128,128]{2,1,0:T(8,128)S(1)}, u32[]{:S(2)}, u32[]{:S(2)}) collective-permute-start(f32[2,128,128]{2,1,0:T(8,128)S(1)} %bitcast_add_fusion.1), channel_id=1, source_target_pairs={{32,0},{96,64},{160,128},{224,192},{33,1},{97,65},{161,129},{225,1... | collective-permute-start | bytes 393224 | tf_op jit(solution)/shard_map/ppermute | solution.py:317
  32.1 6.0 %collective-permute-start.11 = (f32[2,128,128]{2,1,0:T(8,128)S(1)}, f32[2,128,128]{2,1,0:T(8,128)S(1)}, u32[]{:S(2)}, u32[]{:S(2)}) collective-permute-start(f32[2,128,128]{2,1,0:T(8,128)S(1)} %bitcast_add_fusion.1), channel_id=1, source_target_pairs={{112,0},{48,64},{240,128},{176,192},{113,1},{49,65},{241,129},{177... | collective-permute-start | bytes 393224 | tf_op jit(solution)/shard_map/ppermute | solution.py:317
  32.8 5.3 %collective-permute-start.10 = (f32[2,128,128]{2,1,0:T(8,128)S(1)}, f32[2,128,128]{2,1,0:T(8,128)S(1)}, u32[]{:S(2)}, u32[]{:S(2)}) collective-permute-start(f32[2,128,128]{2,1,0:T(8,128)S(1)} %bitcast_add_fusion.1), channel_id=1, source_target_pairs={{16,0},{80,64},{144,128},{208,192},{17,1},{81,65},{145,129},{209,1... | collective-permute-start | bytes 393224 | tf_op jit(solution)/shard_map/ppermute | solution.py:317
  34.6 29.6 %all-to-all-start = ((bf16[8,256,128]{2,1,0:T(8,128)(2,1)}), bf16[8,256,128]{2,1,0:T(8,128)(2,1)S(1)}, u32[]{:S(2)}, u32[]{:S(2)}) async-start(bf16[8,256,128]{2,1,0:T(8,128)(2,1)} %get-tuple-element.21), calls=%async_computation | async-start | bytes 1048576 | tf_op jit(solution)/shard_map/all_to_all | solution.py:332
  38.1 26.1 %copy-start.1 = (f32[6,128]{1,0:T(8,128)S(1)}, f32[6,128]{1,0:T(8,128)}, u32[]{:S(2)}) copy-start(f32[6,128]{1,0:T(8,128)} %rest_3_.1) | copy-start | bytes 9220
  38.2 25.9 %collective-permute-start.15 = (f32[2,128,128]{2,1,0:T(8,128)S(1)}, f32[2,128,128]{2,1,0:T(8,128)S(1)}, u32[]{:S(2)}, u32[]{:S(2)}) collective-permute-start(f32[2,128,128]{2,1,0:T(8,128)S(1)} %add_add_fusion.5), channel_id=1, source_target_pairs={{192,0},{193,1},{194,2},{195,3},{196,4},{197,5},{198,6},{199,7}} | collective-permute-start | bytes 393224 | tf_op jit(solution)/shard_map/ppermute | solution.py:317
  38.8 25.3 %collective-permute-start.14 = (f32[2,128,128]{2,1,0:T(8,128)S(1)}, f32[2,128,128]{2,1,0:T(8,128)S(1)}, u32[]{:S(2)}, u32[]{:S(2)}) collective-permute-start(f32[2,128,128]{2,1,0:T(8,128)S(1)} %add_add_fusion.5), channel_id=1, source_target_pairs={{128,0},{129,1},{130,2},{131,3},{132,4},{133,5},{134,6},{135,7}} | collective-permute-start | bytes 393224 | tf_op jit(solution)/shard_map/ppermute | solution.py:317
  39.5 24.6 %collective-permute-start.13 = (f32[2,128,128]{2,1,0:T(8,128)S(1)}, f32[2,128,128]{2,1,0:T(8,128)S(1)}, u32[]{:S(2)}, u32[]{:S(2)}) collective-permute-start(f32[2,128,128]{2,1,0:T(8,128)S(1)} %add_add_fusion.5), channel_id=1, source_target_pairs={{64,0},{65,1},{66,2},{67,3},{68,4},{69,5},{70,6},{71,7}} | collective-permute-start | bytes 393224 | tf_op jit(solution)/shard_map/ppermute | solution.py:317
  49.1 19.0 %collective-permute-start.19 = (f32[2,128,128]{2,1,0:T(8,128)S(1)}, f32[2,128,128]{2,1,0:T(8,128)S(1)}, u32[]{:S(2)}, u32[]{:S(2)}) collective-permute-start(f32[2,128,128]{2,1,0:T(8,128)S(1)} %slice_bitcast_fusion), channel_id=1, source_target_pairs={{8,0},{24,16},{40,32},{56,48},{72,64},{88,80},{104,96},{120,112},{... | collective-permute-start | bytes 393224 | tf_op jit(solution)/shard_map/ppermute | solution.py:317
  68.2 9.3 %collective-permute-start.22 = (f32[2,128,128]{2,1,0:T(8,128)S(1)}, f32[2,128,128]{2,1,0:T(8,128)S(1)}, u32[]{:S(2)}, u32[]{:S(2)}) collective-permute-start(f32[2,128,128]{2,1,0:T(8,128)S(1)} %bitcast_add_fusion), channel_id=1, source_target_pairs={{32,0},{40,8},{96,64},{104,72},{160,128},{168,136},{224,192},{232,... | collective-permute-start | bytes 393224 | tf_op jit(solution)/shard_map/ppermute | solution.py:317
  69.5 8.0 %collective-permute-start.21 = (f32[2,128,128]{2,1,0:T(8,128)S(1)}, f32[2,128,128]{2,1,0:T(8,128)S(1)}, u32[]{:S(2)}, u32[]{:S(2)}) collective-permute-start(f32[2,128,128]{2,1,0:T(8,128)S(1)} %bitcast_add_fusion), channel_id=1, source_target_pairs={{112,0},{120,8},{48,64},{56,72},{240,128},{248,136},{176,192},{184... | collective-permute-start | bytes 393224 | tf_op jit(solution)/shard_map/ppermute | solution.py:317
  70.8 8.5 %collective-permute-start.20 = (f32[2,128,128]{2,1,0:T(8,128)S(1)}, f32[2,128,128]{2,1,0:T(8,128)S(1)}, u32[]{:S(2)}, u32[]{:S(2)}) collective-permute-start(f32[2,128,128]{2,1,0:T(8,128)S(1)} %bitcast_add_fusion), channel_id=1, source_target_pairs={{16,0},{24,8},{80,64},{88,72},{144,128},{152,136},{208,192},{216,2... | collective-permute-start | bytes 393224 | tf_op jit(solution)/shard_map/ppermute | solution.py:317
  72.1 29.9 %all-to-all-start.1 = ((bf16[8,256,128]{2,1,0:T(8,128)(2,1)}), bf16[8,256,128]{2,1,0:T(8,128)(2,1)S(1)}, u32[]{:S(2)}, u32[]{:S(2)}) async-start(bf16[8,256,128]{2,1,0:T(8,128)(2,1)} %get-tuple-element.26), calls=%async_computation.1 | async-start | bytes 1048576 | tf_op jit(solution)/shard_map/all_to_all | solution.py:332
  79.3 12.2 %collective-permute-start.23 = (f32[2,128,128]{2,1,0:T(8,128)S(1)}, f32[2,128,128]{2,1,0:T(8,128)S(1)}, u32[]{:S(2)}, u32[]{:S(2)}) collective-permute-start(f32[2,128,128]{2,1,0:T(8,128)S(1)} %add_add_fusion.3), channel_id=1, source_target_pairs={{128,0},{136,8},{192,64},{200,72},{129,1},{137,9},{193,65},{201,73... | collective-permute-start | bytes 393224 | tf_op jit(solution)/shard_map/ppermute | solution.py:317
  91.6 10.5 %collective-permute-start.24 = (f32[2,128,128]{2,1,0:T(8,128)S(1)}, f32[2,128,128]{2,1,0:T(8,128)S(1)}, u32[]{:S(2)}, u32[]{:S(2)}) collective-permute-start(f32[2,128,128]{2,1,0:T(8,128)S(1)} %add.132), channel_id=1, source_target_pairs={{64,0},{72,8},{65,1},{73,9},{66,2},{74,10},{67,3},{75,11},{68,4},{... | collective-permute-start | bytes 393224 | tf_op jit(solution)/shard_map/ppermute | solution.py:317
  92.9 20.4 %collective-permute-start.18 = (f32[2,256,128]{2,1,0:T(8,128)S(1)}, f32[2,256,128]{2,1,0:T(8,128)S(1)}, u32[]{:S(2)}, u32[]{:S(2)}) collective-permute-start(f32[2,256,128]{2,1,0:T(8,128)S(1)} %pad_maximum_fusion.1), channel_id=1, source_target_pairs={{0,192},{1,193},{2,194},{3,195},{4,196},{5,197},{6,198},{7,199}} | collective-permute-start | bytes 786440 | tf_op jit(solution)/shard_map/ppermute | solution.py:317
  93.6 21.0 %collective-permute-start.17 = (f32[2,256,128]{2,1,0:T(8,128)S(1)}, f32[2,256,128]{2,1,0:T(8,128)S(1)}, u32[]{:S(2)}, u32[]{:S(2)}) collective-permute-start(f32[2,256,128]{2,1,0:T(8,128)S(1)} %pad_maximum_fusion.1), channel_id=1, source_target_pairs={{0,128},{1,129},{2,130},{3,131},{4,132},{5,133},{6,134},{7,135}} | collective-permute-start | bytes 786440 | tf_op jit(solution)/shard_map/ppermute | solution.py:317
  94.3 26.8 %collective-permute-start.16 = (f32[2,256,128]{2,1,0:T(8,128)S(1)}, f32[2,256,128]{2,1,0:T(8,128)}, u32[]{:S(2)}, u32[]{:S(2)}) collective-permute-start(f32[2,256,128]{2,1,0:T(8,128)S(1)} %pad_maximum_fusion.1), channel_id=1, source_target_pairs={{0,64},{1,65},{2,66},{3,67},{4,68},{5,69},{6,70},{7,71}} | collective-permute-start | bytes 786440 | tf_op jit(solution)/shard_map/ppermute | solution.py:317
  107.5 16.0 %all-to-all-start.2 = ((bf16[8,256,128]{2,1,0:T(8,128)(2,1)}), bf16[8,256,128]{2,1,0:T(8,128)(2,1)S(1)}, u32[]{:S(2)}, u32[]{:S(2)}) async-start(bf16[8,256,128]{2,1,0:T(8,128)(2,1)} %get-tuple-element.29), calls=%async_computation.2 | async-start | bytes 1048576 | tf_op jit(solution)/shard_map/all_to_all | solution.py:332
  111.3 17.9 %collective-permute-start.31 = (f32[256,128]{1,0:T(8,128)S(1)}, f32[256,128]{1,0:T(8,128)S(1)}, u32[]{:S(2)}, u32[]{:S(2)}) collective-permute-start(f32[256,128]{1,0:T(8,128)S(1)} %get-tuple-element.31), channel_id=1, source_target_pairs={{0,192},{1,193},{2,194},{3,195},{4,196},{5,197},{6,198},{7,199}} | collective-permute-start | bytes 393224 | tf_op jit(solution)/shard_map/ppermute | solution.py:317
  111.9 17.9 %collective-permute-start.30 = (f32[256,128]{1,0:T(8,128)S(1)}, f32[256,128]{1,0:T(8,128)}, u32[]{:S(2)}, u32[]{:S(2)}) collective-permute-start(f32[256,128]{1,0:T(8,128)S(1)} %get-tuple-element.31), channel_id=1, source_target_pairs={{0,128},{1,129},{2,130},{3,131},{4,132},{5,133},{6,134},{7,135}} | collective-permute-start | bytes 393224 | tf_op jit(solution)/shard_map/ppermute | solution.py:317
  113.3 17.2 %collective-permute-start.29 = (f32[256,128]{1,0:T(8,128)S(1)}, f32[256,128]{1,0:T(8,128)}, u32[]{:S(2)}, u32[]{:S(2)}) collective-permute-start(f32[256,128]{1,0:T(8,128)S(1)} %get-tuple-element.31), channel_id=1, source_target_pairs={{0,64},{1,65},{2,66},{3,67},{4,68},{5,69},{6,70},{7,71}} | collective-permute-start | bytes 393224 | tf_op jit(solution)/shard_map/ppermute | solution.py:317
  114.6 8.2 %collective-permute-start.32 = (f32[2,128,128]{2,1,0:T(8,128)S(1)}, f32[2,128,128]{2,1,0:T(8,128)S(1)}, u32[]{:S(2)}, u32[]{:S(2)}) collective-permute-start(f32[2,128,128]{2,1,0:T(8,128)S(1)} %add.133.rest_4_), channel_id=1, source_target_pairs={{8,0},{9,1},{10,2},{11,3},{12,4},{13,5},{14,6},{15,7}} | collective-permute-start | bytes 393224 | tf_op jit(solution)/shard_map/ppermute | solution.py:380
  122.1 12.3 %collective-permute-start.27 = (f32[2,256,128]{2,1,0:T(8,128)S(1)}, f32[2,256,128]{2,1,0:T(8,128)S(1)}, u32[]{:S(2)}, u32[]{:S(2)}) collective-permute-start(f32[2,256,128]{2,1,0:T(8,128)S(1)} %add_add_fusion.2), channel_id=1, source_target_pairs={{0,32},{64,96},{128,160},{192,224},{1,33},{65,97},{129,161},{193,2... | collective-permute-start | bytes 786440 | tf_op jit(solution)/shard_map/ppermute | solution.py:317
  122.8 12.3 %collective-permute-start.26 = (f32[2,256,128]{2,1,0:T(8,128)S(1)}, f32[2,256,128]{2,1,0:T(8,128)S(1)}, u32[]{:S(2)}, u32[]{:S(2)}) collective-permute-start(f32[2,256,128]{2,1,0:T(8,128)S(1)} %add_add_fusion.2), channel_id=1, source_target_pairs={{0,112},{64,48},{128,240},{192,176},{1,113},{65,49},{129,241},{193... | collective-permute-start | bytes 786440 | tf_op jit(solution)/shard_map/ppermute | solution.py:317
  129.2 3.1 %collective-permute-start.35 = (f32[256,128]{1,0:T(8,128)S(1)}, f32[256,128]{1,0:T(8,128)S(1)}, u32[]{:S(2)}, u32[]{:S(2)}) collective-permute-start(f32[256,128]{1,0:T(8,128)S(1)} %shard_map.87), channel_id=1, source_target_pairs={{0,192},{1,193},{2,194},{3,195},{4,196},{5,197},{6,198},{7,199}} | collective-permute-start | bytes 393224 | tf_op jit(solution)/shard_map/ppermute | solution.py:317
  129.8 3.1 %collective-permute-start.34 = (f32[256,128]{1,0:T(8,128)S(1)}, f32[256,128]{1,0:T(8,128)S(1)}, u32[]{:S(2)}, u32[]{:S(2)}) collective-permute-start(f32[256,128]{1,0:T(8,128)S(1)} %shard_map.87), channel_id=1, source_target_pairs={{0,128},{1,129},{2,130},{3,131},{4,132},{5,133},{6,134},{7,135}} | collective-permute-start | bytes 393224 | tf_op jit(solution)/shard_map/ppermute | solution.py:317
  130.5 2.4 %collective-permute-start.33 = (f32[256,128]{1,0:T(8,128)S(1)}, f32[256,128]{1,0:T(8,128)S(1)}, u32[]{:S(2)}, u32[]{:S(2)}) collective-permute-start(f32[256,128]{1,0:T(8,128)S(1)} %shard_map.87), channel_id=1, source_target_pairs={{0,64},{1,65},{2,66},{3,67},{4,68},{5,69},{6,70},{7,71}} | collective-permute-start | bytes 393224 | tf_op jit(solution)/shard_map/ppermute | solution.py:317
  132.2 2.9 %collective-permute-start.25 = (f32[2,256,128]{2,1,0:T(8,128)S(1)}, f32[2,256,128]{2,1,0:T(8,128)S(1)}, u32[]{:S(2)}, u32[]{:S(2)}) collective-permute-start(f32[2,256,128]{2,1,0:T(8,128)S(1)} %add_add_fusion.2), channel_id=1, source_target_pairs={{0,16},{64,80},{128,144},{192,208},{1,17},{65,81},{129,145},{193,2... | collective-permute-start | bytes 786440 | tf_op jit(solution)/shard_map/ppermute | solution.py:317
  133.0 3.5 %collective-permute-start.38 = (f32[2,256,128]{2,1,0:T(8,128)S(1)}, f32[2,256,128]{2,1,0:T(8,128)S(1)}, u32[]{:S(2)}, u32[]{:S(2)}) collective-permute-start(f32[2,256,128]{2,1,0:T(8,128)S(1)} %pad_maximum_fusion.2), channel_id=1, source_target_pairs={{0,32},{64,96},{128,160},{192,224},{1,33},{65,97},{129,161},{193,2... | collective-permute-start | bytes 786440 | tf_op jit(solution)/shard_map/ppermute | solution.py:317
  133.7 2.8 %collective-permute-start.37 = (f32[2,256,128]{2,1,0:T(8,128)S(1)}, f32[2,256,128]{2,1,0:T(8,128)S(1)}, u32[]{:S(2)}, u32[]{:S(2)}) collective-permute-start(f32[2,256,128]{2,1,0:T(8,128)S(1)} %pad_maximum_fusion.2), channel_id=1, source_target_pairs={{0,112},{64,48},{128,240},{192,176},{1,113},{65,49},{129,241},{193... | collective-permute-start | bytes 786440 | tf_op jit(solution)/shard_map/ppermute | solution.py:317
  134.4 2.1 %collective-permute-start.36 = (f32[2,256,128]{2,1,0:T(8,128)S(1)}, f32[2,256,128]{2,1,0:T(8,128)S(1)}, u32[]{:S(2)}, u32[]{:S(2)}) collective-permute-start(f32[2,256,128]{2,1,0:T(8,128)S(1)} %pad_maximum_fusion.2), channel_id=1, source_target_pairs={{0,16},{64,80},{128,144},{192,208},{1,17},{65,81},{129,145},{193,2... | collective-permute-start | bytes 786440 | tf_op jit(solution)/shard_map/ppermute | solution.py:317
  135.2 7.5 %collective-permute-start.28 = (f32[2,256,128]{2,1,0:T(8,128)S(1)}, f32[2,256,128]{2,1,0:T(8,128)S(1)}, u32[]{:S(2)}, u32[]{:S(2)}) collective-permute-start(f32[2,256,128]{2,1,0:T(8,128)S(1)} %add_add_fusion.1), channel_id=1, source_target_pairs={{0,8},{16,24},{32,40},{48,56},{64,72},{80,88},{96,104},{112,120},{... | collective-permute-start | bytes 786440 | tf_op jit(solution)/shard_map/ppermute | solution.py:317
  136.6 11.3 %collective-permute-start.39 = (f32[2,256,128]{2,1,0:T(8,128)S(1)}, f32[2,256,128]{2,1,0:T(8,128)S(1)}, u32[]{:S(2)}, u32[]{:S(2)}) collective-permute-start(f32[2,256,128]{2,1,0:T(8,128)S(1)} %add_add_fusion), channel_id=1, source_target_pairs={{0,8},{16,24},{32,40},{48,56},{64,72},{80,88},{96,104},{112,120},{... | collective-permute-start | bytes 786440 | tf_op jit(solution)/shard_map/ppermute | solution.py:317

commit v3 on v2

--- a/solution.py
+++ b/solution.py
@@ -12,6 +12,7 @@
 UNROLL = 8
 CHUNKS = 4
 LIMIT = 24 << 20
+HALO = ((5, 1), (3, 2))
 
 
 def accumulate(acc, kernel_of, picks_of, factor_of, row_of, entries):
@@ -42,9 +43,12 @@
     rest = list(rest[len(halo_shapes) :])
     with_lists = len(steps) == 2
     out_ref = rest.pop(0)
+    pieces = []
     if with_lists:
         lists_ref = rest.pop(0)
-    row_s, col_s, lag_s, mode_ref, acc, blocks_v, state_v, sems, state_sems, table_sems = rest
+    if not halos:
+        pieces = [rest.pop(0) for _ in HALO]
+    row_s, col_s, lag_s, mode_ref, acc, blocks_v, state_v, sems, state_sems, table_sems, *piece_sems = rest
     table_copies = [
         pltpu.make_async_copy(source, target, table_sems.at[k])
         for k, (source, target) in enumerate(((row_h, row_s), (col_h, col_s), (lag_h, lag_s)))
@@ -90,37 +94,43 @@
 
     for copy in table_copies:
         copy.wait()
-    if with_lists:
-        kinds = STEPS - 1
-
-        def place(entry, counts):
-            lag = lag_s[entry]
-            kind = jnp.minimum(lag, kinds)
-            at = counts[kinds]
-            for j in range(kinds):
-                at = jnp.where(lag == j, counts[j], at)
-            lists_ref[kind * entries + at] = entry + row_s[entry] * 1024 + col_s[entry] * 65536
-            return tuple(count + jnp.where(kind == j, 1, 0) for j, count in enumerate(counts))
-
-        counts = lax.fori_loop(0, entries, place, (jnp.int32(0),) * (kinds + 1))
-        for j in range(kinds + 1):
-            lists_ref[(kinds + 1) * entries + j] = counts[j]
+    kinds = STEPS - 1
+
+    def place(entry, counts):
+        lag = lag_s[entry]
+        kind = jnp.minimum(lag, kinds)
+        at = counts[kinds]
+        for j in range(kinds):
+            at = jnp.where(lag == j, counts[j], at)
+        lists_ref[kind * entries + at] = entry + row_s[entry] * 1024 + col_s[entry] * 65536
+        return tuple(count + jnp.where(kind == j, 1, 0) for j, count in enumerate(counts))
+
     for copy in state_copies:
         copy.wait()
 
-    def chunk(c, carry):
+    piece_copies = [
+        pltpu.make_async_copy(
+            state_v.at[pl.ds(start, count)], piece, piece_sems[0].at[k]
+        )
+        for k, (piece, (start, count)) in enumerate(zip(pieces, HALO))
+    ]
+    for copy in piece_copies:
+        copy.start()
+
+    def chunk(c, counts):
         chunk_copy(c).wait()
-        accumulate(
-            acc,
-            lambda e: blocks_v[e],
-            picks_of,
-            factor_of,
-            lambda e: row_s[e],
-            [c * per + u for u in range(per)],
-        )
-        return carry
-
-    lax.fori_loop(0, CHUNKS, chunk, 0)
+        run = [c * per + u for u in range(per)]
+        if with_lists:
+            for entry in run:
+                counts = place(entry, counts)
+        accumulate(acc, lambda e: blocks_v[e], picks_of, factor_of, lambda e: row_s[e], run)
+        return counts
+
+    counts = lax.fori_loop(0, CHUNKS, chunk, (jnp.int32(0),) * (kinds + 1) if with_lists else ())
+    for j, count in enumerate(counts):
+        lists_ref[(kinds + 1) * entries + j] = count
+    for copy in piece_copies:
+        copy.wait()
     if with_lists:
         core = lax.axis_index("lag") % 2
         for k in range(2):
@@ -143,6 +153,13 @@
     if len(steps) == 2:
         out_shape.append(jax.ShapeDtypeStruct((STEPS * entries + STEPS,), jnp.int32))
         out_specs.append(in_smem)
+    more_scratch = []
+    if not halos:
+        out_shape += [
+            jax.ShapeDtypeStruct((count, points, modes), history.dtype) for _, count in HALO
+        ]
+        out_specs += [in_hbm] * len(HALO)
+        more_scratch.append(pltpu.SemaphoreType.DMA((len(HALO),)))
     return pl.pallas_call(
         functools.partial(field_kernel, steps, halo_shapes),
         out_shape=out_shape,
@@ -157,6 +174,7 @@
             pltpu.SemaphoreType.DMA((CHUNKS,)),
             pltpu.SemaphoreType.DMA((1 + len(halos),)),
             pltpu.SemaphoreType.DMA((4,)),
+            *more_scratch,
         ],
         compiler_params=pltpu.CompilerParams(vmem_limit_bytes=LIMIT),
     )(
@@ -206,7 +224,8 @@
     entries, size, _ = blocks_h.shape
     row_blocks = acc.shape[0]
     counts = [lists_s[STEPS * entries + j] for j in range(step)]
-    groups = [(count + UNROLL - 1) // UNROLL for count in counts]
+    root = lax.axis_index("lag") == 0
+    groups = [jnp.where(root, (count + UNROLL - 1) // UNROLL, 0) for count in counts]
     firsts = [sum(groups[:j]) for j in range(step)]
 
     def code_of(j, g, u):
@@ -295,17 +314,27 @@
 
 
 def routes(cores, pairs):
-    return [(lag_of(*a, c), lag_of(*b, c)) for a, b in pairs for c in range(cores)]
+    return [(lag_of(*a, c), lag_of(*b, c)) for a, b in pairs for c in cores]
 
 
 BOTH = (0, 1)
 TO_CORE_0 = [(lag_of(x, z, 1), lag_of(x, z, 0)) for x in BOTH for z in range(8)]
-SWAP = TO_CORE_0 + [(b, a) for a, b in TO_CORE_0]
-FROM_CORE_0 = [(b, a) for a, b in TO_CORE_0]
+TO_CORE_1 = [(b, a) for a, b in TO_CORE_0]
+SWAP = TO_CORE_0 + TO_CORE_1
 HUBS = [[((x, q + k), (x, q)) for x in BOTH for q in (0, 4)] for k in (1, -1, 2)]
 TOPS = [[((0, 4), (0, 0))], [((1, 0), (0, 0))], [((1, 4), (0, 0))]]
-ACROSS = [((1, 0), (0, 0)), ((1, 4), (0, 4))]
-ALONG = [((0, 4), (0, 0))]
+HALVES = [
+    [((x, z + 1), (x, z)) for x in BOTH for z in (0, 2, 4, 6)],
+    [((x, z + 2), (x, z)) for x in BOTH for z in (0, 4)],
+    [((x, 4), (x, 0)) for x in BOTH],
+    [((1, 0), (0, 0))],
+]
+ASIDE = [
+    [((1, z + 1), (1, z)) for z in (0, 2, 4, 6)] + [((0, z), (0, z + 1)) for z in (2, 4, 6)],
+    [((1, z + 2), (1, z)) for z in (0, 4)] + [((0, z + 3), (0, z + 1)) for z in (0, 4)],
+    [((1, 4), (1, 0)), ((0, 5), (0, 1))],
+    [((1, 0), (0, 1))],
+]
 
 
 def turned(pairs):
@@ -333,10 +362,8 @@
     return everyone.reshape(-1, copies.shape[-1])
 
 
-UP_HUBS = [routes(1, pairs) for pairs in HUBS]
-UP_TOPS = [routes(1, pairs) for pairs in TOPS]
-DOWN_HUBS = [routes(1, turned(pairs)) for pairs in HUBS]
-DOWN_TOPS = [routes(1, turned(pairs)) for pairs in TOPS]
+def on_core(core, value, other):
+    return jnp.where(lax.axis_index("lag") % 2 == core, value, other)
 
 
 def per_device(
@@ -347,45 +374,50 @@
     peers = lax.axis_size("pts")
     lags = lax.axis_size("lag")
     first = lax.axis_index("lag") == 0
-    lags_held = history.shape[0]
     next_lag = [(i, i + 1) for i in range(lags - 1)]
     tables = (block_row, block_col, lag_offset, kernel_blocks, mode_kernel)
-    halo_1 = lax.ppermute(history[lags_held - 1 :], "lag", next_lag)
-    (now,) = fields((0,), [], history, tables, row_blocks)
+    now, piece_1, piece_2 = fields((0,), [], history, tables, row_blocks)
     now = plus_arrived(now[0], TO_CORE_0)
-    halo_2 = lax.ppermute(
-        after(history, now)[lags_held - 3 : lags_held - 1], "lag", next_lag
-    )
+    halo_1 = lax.ppermute(piece_1, "lag", next_lag)
+    halo_2 = lax.ppermute(piece_2, "lag", next_lag)
+    now = plus_arrived(now, *[routes((0,), pairs) for pairs in HUBS])
     (second,) = fields((1,), [after(halo_1, now)], history, tables, row_blocks)
-    now = plus_arrived(now, *UP_HUBS)
-    second = plus_arrived(second[0], TO_CORE_0)
-    now = plus_arrived(now, *UP_TOPS)
-    second = plus_arrived(second, *UP_HUBS)
+    now = plus_arrived(now, *[routes((0,), pairs) for pairs in TOPS])
+    second = plus_arrived(second[0], TO_CORE_1)
     args = (self_inverse, mode_kernel, kernel_blocks)
     density_0, copies = densities_of(0, peers, [], incident[0], now, *args, None)
     fresh = [to_everyone(copies)]
-    second = plus_arrived(second, *UP_TOPS)
+    for pairs in HALVES:
+        second = plus_arrived(second, routes((1,), pairs))
+    second = lax.ppermute(second, "lag", [(1, 0)])
     pair, lists = fields((2, 3), [after(halo_2, copies), halo_1], history, tables, row_blocks)
     pair = plus_arrived(pair[0], SWAP, operand=pair[1])
+    for pairs in ASIDE:
+        pair = plus_arrived(pair, routes(BOTH, pairs))
     density_1, copies = densities_of(1, peers, fresh, incident[1], second, *args, lists)
     fresh.append(to_everyone(copies))
-    pair = after(pair, copies)
-    pair = plus_arrived(pair, *[routes(2, pairs) for pairs in HUBS])
-    pair = plus_arrived(pair, routes(2, ACROSS))
-    pair = plus_arrived(pair, routes(2, ALONG))
+    pair = plus_arrived(pair, routes(BOTH, [((0, 1), (0, 0))]), operand=after(pair, copies))
     early = jnp.stack([density_0, density_1])
-    early = plus_arrived(jnp.where(first, early, 0.0), *DOWN_TOPS, operand=early)
+    moving = lax.ppermute(early, "lag", [(0, 1)])
+    for pairs in HALVES[::-1]:
+        moving = plus_arrived(moving, routes((1,), turned(pairs)))
     density_2, copies = densities_of(2, peers, fresh, incident[2], pair, *args, lists)
     fresh.append(to_everyone(copies))
     fourth = lax.ppermute(after(pair, copies), "lag", [(1, 0)])
-    third = plus_arrived(jnp.where(first, density_2, 0.0), *DOWN_TOPS, operand=density_2)
-    early = plus_arrived(after(early, copies), *DOWN_HUBS)
-    early = plus_arrived(early, FROM_CORE_0)
+    third = lax.ppermute(density_2, "lag", [(0, 1)])
+    for pairs in HALVES[:1:-1]:
+        third = plus_arrived(third, routes((1,), turned(pairs)))
+    arrived = lax.ppermute(moving, "lag", TO_CORE_0[1:])
+    early = jnp.where(first, early, on_core(0, arrived, moving))
     (density_3,) = densities_of(3, peers, fresh, incident[3], fourth, *args, lists)
-    final = plus_arrived(jnp.where(first, density_3, 0.0), *DOWN_TOPS, operand=density_3)
-    late = jnp.stack([third, final])
-    late = plus_arrived(late, *DOWN_HUBS)
-    late = plus_arrived(late, FROM_CORE_0)
+    final = plus_arrived(
+        jnp.where(first, density_3, 0.0),
+        *[routes((0,), turned(pairs)) for pairs in TOPS],
+        operand=density_3,
+    )
+    late = plus_arrived(on_core(0, final, third), *[routes(BOTH, turned(pairs)) for pairs in HUBS])
+    other = lax.ppermute(late, "lag", SWAP)
+    late = jnp.stack([on_core(0, other, late), on_core(0, late, other)])
     return jnp.concatenate([early, late])
 
 

time: 151 us -> 146 us (0.967)
  the two profiles are of different devices: /device:TPU:1 before, /device:TPU:97 now
where the time goes in v3:
time: 146 us; the launch traced here: 145 us
  starting transfers between devices  68 us (47%)
  waiting for transfers between devices  50.3 us (34%)
  Pallas kernels  23.8 us (16%)
    ppermute x30, waiting for transfers between devices, plus_arrived(): arrived = [lax.ppermute(operand, 'lag', pairs) for pairs in levels]  41.9 us
    ppermute x30, starting transfers between devices, plus_arrived(): arrived = [lax.ppermute(operand, 'lag', pairs) for pairs in levels]  27.7 us
    pallas_call x3, Pallas kernels, fields(): pl.pallas_call(functools.partial(field_kernel, steps, halo_shapes), out_s...  18 us
    all_to_all x3, starting transfers between devices, to_everyone(): everyone = lax.all_to_all(copies, 'pts', 0, 0, tiled=True)  15.1 us
    ppermute x1, starting transfers between devices, per_device(): other = lax.ppermute(late, 'lag', SWAP)  11.6 us
    all_to_all x3, waiting for transfers between devices, to_everyone(): everyone = lax.all_to_all(copies, 'pts', 0, 0, tiled=True)  7.29 us
    ppermute x1, starting transfers between devices, per_device(): halo_2 = lax.ppermute(piece_2, 'lag', next_lag)  5.04 us
    pallas_call x3, Pallas kernels, densities_of(): pl.pallas_call(functools.partial(chain_kernel, step, last), out_shape=(de...  4.83 us
  transfers between devices with their start and end apart: 41, of which 6 were waited for; matrix products, arithmetic and copies ran while one was open for 0% of the time, Pallas kernels for 12%

profile of v3, /device:TPU:97, one launch (start us, length us, event | category | flops | bytes accessed | tf_op | source)
XLA Modules:
  0.0 144.5 jit_solution(1994525316894507693)
XLA Ops:
  0.0 6.1 %shard_map.82 = (f32[1,2,128,128]{3,2,1,0:T(8,128)S(1)}, bf16[1,2048,128]{2,1,0:T(8,128)(2,1)S(1)}, bf16[2,2048,128]{2,1,0:T(8,128)(2,1)S(1)}) custom-call(s32[192]{0:T(256)} %row_h.5, s32[192]{0:T(256)} %col_h.5, s32[192]{0:T(256)} %lag_h.5, f32[6,128]{1,0:T(8,128)} %rest_3_.1, bf16[192,128,128]{2,1,0:T(8,128)(2,1)} %blocks_h.11, ...), custom_call_target="tpu_custom_call" | custom-call | tf_op jit(solution)/shard_map/pallas_call | solution.py:163
  6.2 2.7 %collective-permute-start = (f32[2,128,128]{2,1,0:T(8,128)S(1)}, f32[2,128,128]{2,1,0:T(8,128)S(1)}, u32[]{:S(2)}, u32[]{:S(2)}) collective-permute-start(f32[2,128,128]{2,1,0:T(8,128)S(1)} %bitcast.36), channel_id=1, source_target_pairs={{8,0},{24,16},{40,32},{56,48},{72,64},{88,80},{104,96},{120,112},{... | collective-permute-start | bytes 393224 | tf_op jit(solution)/shard_map/ppermute | solution.py:346
  8.9 4.0 %collective-permute-start.8 = (bf16[1,2048,128]{2,1,0:T(8,128)(2,1)S(1)}, bf16[1,2048,128]{2,1,0:T(8,128)(2,1)S(1)}, u32[]{:S(2)}, u32[]{:S(2)}) collective-permute-start(bf16[1,2048,128]{2,1,0:T(8,128)(2,1)S(1)} %get-tuple-element.25), channel_id=1, source_target_pairs={{0,8},{8,16},{16,24},{24,32},{32,40},{40,48},{48,56},{56,64},{64,7... | collective-permute-start | bytes 1572872 | tf_op jit(solution)/shard_map/ppermute | solution.py:381
  12.9 0.7 collective-permute-start.3
  13.6 0.7 collective-permute-start.2
  14.3 0.7 collective-permute-start.1
  15.0 5.0 %collective-permute-start.7 = (bf16[2,2048,128]{2,1,0:T(8,128)(2,1)S(1)}, bf16[2,2048,128]{2,1,0:T(8,128)(2,1)S(1)}, u32[]{:S(2)}, u32[]{:S(2)}) collective-permute-start(bf16[2,2048,128]{2,1,0:T(8,128)(2,1)S(1)} %get-tuple-element.22), channel_id=1, source_target_pairs={{0,8},{8,16},{16,24},{24,32},{32,40},{40,48},{48,56},{56,64},{64,7... | collective-permute-start | bytes 3145736 | tf_op jit(solution)/shard_map/ppermute | solution.py:382
  20.1 4.9 %shard_map.84 = f32[1,2,128,128]{3,2,1,0:T(8,128)S(1)} custom-call(s32[192]{0:T(256)} %row_h.5, s32[192]{0:T(256)} %col_h.5, s32[192]{0:T(256)} %lag_h.5, f32[6,128]{1,0:T(8,128)} %rest_3_.1, bf16[192,128,128]{2,1,0:T(8,128)(2,1)} %blocks_h.11, bf16[6,2048,128]{2,1,0:T(8,128)(2,1)} %history_h.5, bf16[1,2048,128]{2,1,0:T(8,128)(2,1)S(1)} %collective-permute-done.8.rest_1_.rest_0_), custom_call_target="tpu_custom_call" | custom-call | tf_op jit(solution)/shard_map/pallas_call | solution.py:163
  25.0 1.3 collective-permute-start.9
  26.3 0.7 collective-permute-start.6
  27.0 0.7 collective-permute-start.5
  27.7 0.7 collective-permute-start.4
  28.4 3.7 %collective-permute-start.10 = (f32[2,128,128]{2,1,0:T(8,128)S(1)}, f32[2,128,128]{2,1,0:T(8,128)S(1)}, u32[]{:S(2)}, u32[]{:S(2)}) collective-permute-start(f32[2,128,128]{2,1,0:T(8,128)S(1)} %bitcast_add_fusion.1), channel_id=1, source_target_pairs={{24,8},{56,40},{88,72},{120,104},{152,136},{184,168},{216,200},{24... | collective-permute-start | bytes 393224 | tf_op jit(solution)/shard_map/ppermute | solution.py:346
  32.1 1.9 %collective-permute-done.10 = f32[2,128,128]{2,1,0:T(8,128)S(1)} collective-permute-done((f32[2,128,128]{2,1,0:T(8,128)S(1)}, f32[2,128,128]{2,1,0:T(8,128)S(1)}, u32[]{:S(2)}, u32[]{:S(2)}) %collective-permute-start.10) | collective-permute-done | bytes 131104 | tf_op jit(solution)/shard_map/ppermute | solution.py:346
  34.0 0.7 collective-permute-start.11
  34.7 1.0 first_density.1
  35.8 0.7 collective-permute-start.12
  36.5 7.0 %shard_map.83 = (f32[2,2,128,128]{3,2,1,0:T(8,128)S(1)}, s32[772]{0:T(1024)S(1)}) custom-call(s32[192]{0:T(256)} %row_h.5, s32[192]{0:T(256)} %col_h.5, s32[192]{0:T(256)} %lag_h.5, f32[6,128]{1,0:T(8,128)} %rest_3_.1, bf16[192,128,128]{2,1,0:T(8,128)(2,1)} %blocks_h.11, bf16[6,2048,128]{2,1,0:T(8,128)(2,1)} %history_h.5, ...), custom_call_target="tpu_custom_call" | custom-call | tf_op jit(solution)/shard_map/pallas_call | solution.py:163
  43.6 5.1 %all-to-all-start = ((bf16[8,256,128]{2,1,0:T(8,128)(2,1)}), bf16[8,256,128]{2,1,0:T(8,128)(2,1)S(1)}, u32[]{:S(2)}, u32[]{:S(2)}) async-start(bf16[8,256,128]{2,1,0:T(8,128)(2,1)} %get-tuple-element.23), calls=%async_computation | async-start | bytes 1048576 | tf_op jit(solution)/shard_map/all_to_all | solution.py:361
  48.7 0.7 collective-permute-start.13
  49.4 1.3 collective-permute-start.22
  51.5 6.0 %collective-permute-done.22 = f32[2,128,128]{2,1,0:T(8,128)S(1)} collective-permute-done((f32[2,128,128]{2,1,0:T(8,128)S(1)}, f32[2,128,128]{2,1,0:T(8,128)S(1)}, u32[]{:S(2)}, u32[]{:S(2)}) %collective-permute-start.22) | collective-permute-done | bytes 131104 | tf_op jit(solution)/shard_map/ppermute | solution.py:346
  57.5 1.3 collective-permute-start.23
  58.8 1.9 %shard_map.85 = (f32[256,128]{1,0:T(8,128)S(1)}, bf16[8,256,128]{2,1,0:T(8,128)(2,1)}) custom-call(s32[772]{0:T(1024)S(1)} %get-tuple-element.26.lists_s, bf16[192,128,128]{2,1,0:T(8,128)(2,1)} %blocks_h.11, bf16[2048,128]{1,0:T(8,128)(2,1)S(1)} %bitcast.25, f32[6,128]{1,0:T(8,128)S(1)} %copy-done.1, bf16[256,128]{1,0:T(8,128)(2,1)S(1)} %get-tuple-element.38.rest_2_, ...), custom_call_target="tpu_custom_call" | custom-call | tf_op jit(solution)/shard_map/pallas_call | solution.py:298
  60.7 4.9 %all-to-all-start.1 = ((bf16[8,256,128]{2,1,0:T(8,128)(2,1)}), bf16[8,256,128]{2,1,0:T(8,128)(2,1)S(1)}, u32[]{:S(2)}, u32[]{:S(2)}) async-start(bf16[8,256,128]{2,1,0:T(8,128)(2,1)} %get-tuple-element.29), calls=%async_computation.1 | async-start | bytes 1048576 | tf_op jit(solution)/shard_map/all_to_all | solution.py:361
  65.6 0.7 collective-permute-start.24
  66.3 0.7 collective-permute-start.25
  67.0 0.7 collective-permute-start.15
  67.7 0.7 collective-permute-start.26
  68.4 4.3 %all-to-all-done.1 = bf16[8,256,128]{2,1,0:T(8,128)(2,1)S(1)} async-done(((bf16[8,256,128]{2,1,0:T(8,128)(2,1)}), bf16[8,256,128]{2,1,0:T(8,128)(2,1)S(1)}, u32[]{:S(2)}, u32[]{:S(2)}) %all-to-all-start.1) | async-done | bytes 524320 | tf_op jit(solution)/shard_map/all_to_all | solution.py:361
  72.7 1.9 %shard_map.86 = (f32[256,128]{1,0:T(8,128)S(1)}, bf16[8,256,128]{2,1,0:T(8,128)(2,1)}) custom-call(s32[772]{0:T(1024)S(1)} %get-tuple-element.26.lists_s, bf16[192,128,128]{2,1,0:T(8,128)(2,1)} %blocks_h.11, bf16[2048,128]{1,0:T(8,128)(2,1)S(1)} %bitcast.26, bf16[2048,128]{1,0:T(8,128)(2,1)S(1)} %bitcast.28, f32[6,128]{1,0:T(8,128)S(1)} %copy-done.1, ...), custom_call_target="tpu_custom_call" | custom-call | tf_op jit(solution)/shard_map/pallas_call | solution.py:298
  74.6 5.1 %all-to-all-start.2 = ((bf16[8,256,128]{2,1,0:T(8,128)(2,1)}), bf16[8,256,128]{2,1,0:T(8,128)(2,1)S(1)}, u32[]{:S(2)}, u32[]{:S(2)}) async-start(bf16[8,256,128]{2,1,0:T(8,128)(2,1)} %get-tuple-element.32), calls=%async_computation.2 | async-start | bytes 1048576 | tf_op jit(solution)/shard_map/all_to_all | solution.py:361
  79.7 0.7 collective-permute-start.16
  81.0 0.7 collective-permute-start.32
  81.7 0.7 collective-permute-start.27
  82.4 0.7 collective-permute-start.17
  83.8 3.0 %all-to-all-done.2 = bf16[8,256,128]{2,1,0:T(8,128)(2,1)S(1)} async-done(((bf16[8,256,128]{2,1,0:T(8,128)(2,1)}), bf16[8,256,128]{2,1,0:T(8,128)(2,1)S(1)}, u32[]{:S(2)}, u32[]{:S(2)}) %all-to-all-start.2) | async-done | bytes 524320 | tf_op jit(solution)/shard_map/all_to_all | solution.py:361
  86.8 1.1 shard_map.87
  89.3 0.7 collective-permute-start.28
  90.0 0.7 collective-permute-start.18
  90.8 0.7 collective-permute-start.36
  91.5 1.3 collective-permute-start.35
  93.5 1.3 collective-permute-start.19
  94.8 34.0 %collective-permute-done.35 = f32[256,128]{1,0:T(8,128)S(1)} collective-permute-done((f32[256,128]{1,0:T(8,128)S(1)}, f32[256,128]{1,0:T(8,128)S(1)}, u32[]{:S(2)}, u32[]{:S(2)}) %collective-permute-start.35) | collective-permute-done | bytes 131104 | tf_op jit(solution)/shard_map/ppermute | solution.py:346
  128.9 11.6 %collective-permute-start.37 = (f32[256,128]{1,0:T(8,128)S(1)}, f32[256,128]{1,0:T(8,128)S(1)}, u32[]{:S(2)}, u32[]{:S(2)}) collective-permute-start(f32[256,128]{1,0:T(8,128)S(1)} %add_add_fusion), channel_id=1, source_target_pairs={{8,0},{24,16},{40,32},{56,48},{72,64},{88,80},{104,96},{120,112},{... | collective-permute-start | bytes 393224 | tf_op jit(solution)/shard_map/ppermute | solution.py:419
  140.5 1.9 %collective-permute-start.20 = (f32[2,256,128]{2,1,0:T(8,128)S(1)}, f32[2,256,128]{2,1,0:T(8,128)S(1)}, u32[]{:S(2)}, u32[]{:S(2)}) collective-permute-start(f32[2,256,128]{2,1,0:T(8,128)S(1)} %add.113), channel_id=1, source_target_pairs={{24,16},{40,32},{56,48},{72,64},{88,80},{104,96},{120,112},{136,12... | collective-permute-start | bytes 786440 | tf_op jit(solution)/shard_map/ppermute | solution.py:410
  142.5 1.1 collective-permute-done.20
  143.7 0.8 pad_maximum_fusion
  (74 shorter events, 4.9 us)
Async XLA Ops:
  6.1 25.9 %copy-start.2 = (bf16[4,256,128]{2,1,0:T(8,128)(2,1)S(1)}, bf16[4,256,128]{2,1,0:T(8,128)(2,1)}, u32[]{:S(2)}) copy-start(bf16[4,256,128]{2,1,0:T(8,128)(2,1)} %param.9) | copy-start | bytes 786436
  6.2 6.8 %collective-permute-start = (f32[2,128,128]{2,1,0:T(8,128)S(1)}, f32[2,128,128]{2,1,0:T(8,128)S(1)}, u32[]{:S(2)}, u32[]{:S(2)}) collective-permute-start(f32[2,128,128]{2,1,0:T(8,128)S(1)} %bitcast.36), channel_id=1, source_target_pairs={{8,0},{24,16},{40,32},{56,48},{72,64},{88,80},{104,96},{120,112},{... | collective-permute-start | bytes 393224 | tf_op jit(solution)/shard_map/ppermute | solution.py:346
  8.9 11.2 %collective-permute-start.8 = (bf16[1,2048,128]{2,1,0:T(8,128)(2,1)S(1)}, bf16[1,2048,128]{2,1,0:T(8,128)(2,1)S(1)}, u32[]{:S(2)}, u32[]{:S(2)}) collective-permute-start(bf16[1,2048,128]{2,1,0:T(8,128)(2,1)S(1)} %get-tuple-element.25), channel_id=1, source_target_pairs={{0,8},{8,16},{16,24},{24,32},{32,40},{40,48},{48,56},{56,64},{64,7... | collective-permute-start | bytes 1572872 | tf_op jit(solution)/shard_map/ppermute | solution.py:381
  12.9 7.1 %collective-permute-start.3 = (f32[2,128,128]{2,1,0:T(8,128)S(1)}, f32[2,128,128]{2,1,0:T(8,128)S(1)}, u32[]{:S(2)}, u32[]{:S(2)}) collective-permute-start(f32[2,128,128]{2,1,0:T(8,128)S(1)} %bitcast_add_fusion.2), channel_id=1, source_target_pairs={{32,0},{96,64},{160,128},{224,192},{33,1},{97,65},{161,129},{225,1... | collective-permute-start | bytes 393224 | tf_op jit(solution)/shard_map/ppermute | solution.py:346
  13.6 6.4 %collective-permute-start.2 = (f32[2,128,128]{2,1,0:T(8,128)S(1)}, f32[2,128,128]{2,1,0:T(8,128)S(1)}, u32[]{:S(2)}, u32[]{:S(2)}) collective-permute-start(f32[2,128,128]{2,1,0:T(8,128)S(1)} %bitcast_add_fusion.2), channel_id=1, source_target_pairs={{112,0},{48,64},{240,128},{176,192},{113,1},{49,65},{241,129},{177... | collective-permute-start | bytes 393224 | tf_op jit(solution)/shard_map/ppermute | solution.py:346
  14.3 5.8 %collective-permute-start.1 = (f32[2,128,128]{2,1,0:T(8,128)S(1)}, f32[2,128,128]{2,1,0:T(8,128)S(1)}, u32[]{:S(2)}, u32[]{:S(2)}) collective-permute-start(f32[2,128,128]{2,1,0:T(8,128)S(1)} %bitcast_add_fusion.2), channel_id=1, source_target_pairs={{16,0},{80,64},{144,128},{208,192},{17,1},{81,65},{145,129},{209,1... | collective-permute-start | bytes 393224 | tf_op jit(solution)/shard_map/ppermute | solution.py:346
  15.0 19.8 %copy-start = (f32[256,128]{1,0:T(8,128)S(1)}, f32[256,128]{1,0:T(8,128)}, u32[]{:S(2)}) copy-start(f32[256,128]{1,0:T(8,128)} %rest_6_.1) | copy-start | bytes 393220
  15.0 21.5 %collective-permute-start.7 = (bf16[2,2048,128]{2,1,0:T(8,128)(2,1)S(1)}, bf16[2,2048,128]{2,1,0:T(8,128)(2,1)S(1)}, u32[]{:S(2)}, u32[]{:S(2)}) collective-permute-start(bf16[2,2048,128]{2,1,0:T(8,128)(2,1)S(1)} %get-tuple-element.22), channel_id=1, source_target_pairs={{0,8},{8,16},{16,24},{24,32},{32,40},{40,48},{48,56},{56,64},{64,7... | collective-permute-start | bytes 3145736 | tf_op jit(solution)/shard_map/ppermute | solution.py:382
  25.0 3.3 %collective-permute-start.9 = (f32[2,128,128]{2,1,0:T(8,128)S(1)}, f32[2,128,128]{2,1,0:T(8,128)S(1)}, u32[]{:S(2)}, u32[]{:S(2)}) collective-permute-start(f32[2,128,128]{2,1,0:T(8,128)S(1)} %bitcast.31), channel_id=1, source_target_pairs={{0,8},{16,24},{32,40},{48,56},{64,72},{80,88},{96,104},{112,120},{... | collective-permute-start | bytes 393224 | tf_op jit(solution)/shard_map/ppermute | solution.py:346
  26.3 8.3 %collective-permute-start.6 = (f32[2,128,128]{2,1,0:T(8,128)S(1)}, f32[2,128,128]{2,1,0:T(8,128)S(1)}, u32[]{:S(2)}, u32[]{:S(2)}) collective-permute-start(f32[2,128,128]{2,1,0:T(8,128)S(1)} %add_add_fusion.2), channel_id=1, source_target_pairs={{192,0},{193,1},{194,2},{195,3},{196,4},{197,5},{198,6},{199,7}} | collective-permute-start | bytes 393224 | tf_op jit(solution)/shard_map/ppermute | solution.py:346
  27.0 7.7 %collective-permute-start.5 = (f32[2,128,128]{2,1,0:T(8,128)S(1)}, f32[2,128,128]{2,1,0:T(8,128)S(1)}, u32[]{:S(2)}, u32[]{:S(2)}) collective-permute-start(f32[2,128,128]{2,1,0:T(8,128)S(1)} %add_add_fusion.2), channel_id=1, source_target_pairs={{128,0},{129,1},{130,2},{131,3},{132,4},{133,5},{134,6},{135,7}} | collective-permute-start | bytes 393224 | tf_op jit(solution)/shard_map/ppermute | solution.py:346
  27.7 7.0 %collective-permute-start.4 = (f32[2,128,128]{2,1,0:T(8,128)S(1)}, f32[2,128,128]{2,1,0:T(8,128)S(1)}, u32[]{:S(2)}, u32[]{:S(2)}) collective-permute-start(f32[2,128,128]{2,1,0:T(8,128)S(1)} %add_add_fusion.2), channel_id=1, source_target_pairs={{64,0},{65,1},{66,2},{67,3},{68,4},{69,5},{70,6},{71,7}} | collective-permute-start | bytes 393224 | tf_op jit(solution)/shard_map/ppermute | solution.py:346
  28.4 5.6 %collective-permute-start.10 = (f32[2,128,128]{2,1,0:T(8,128)S(1)}, f32[2,128,128]{2,1,0:T(8,128)S(1)}, u32[]{:S(2)}, u32[]{:S(2)}) collective-permute-start(f32[2,128,128]{2,1,0:T(8,128)S(1)} %bitcast_add_fusion.1), channel_id=1, source_target_pairs={{24,8},{56,40},{88,72},{120,104},{152,136},{184,168},{216,200},{24... | collective-permute-start | bytes 393224 | tf_op jit(solution)/shard_map/ppermute | solution.py:346
  34.0 1.8 %collective-permute-start.11 = (f32[2,128,128]{2,1,0:T(8,128)S(1)}, f32[2,128,128]{2,1,0:T(8,128)S(1)}, u32[]{:S(2)}, u32[]{:S(2)}) collective-permute-start(f32[2,128,128]{2,1,0:T(8,128)S(1)} %add.105), channel_id=1, source_target_pairs={{40,8},{104,72},{168,136},{232,200},{41,9},{105,73},{169,137},{233... | collective-permute-start | bytes 393224 | tf_op jit(solution)/shard_map/ppermute | solution.py:346
  35.8 12.9 %collective-permute-start.12 = (f32[2,128,128]{2,1,0:T(8,128)S(1)}, f32[2,128,128]{2,1,0:T(8,128)S(1)}, u32[]{:S(2)}, u32[]{:S(2)}) collective-permute-start(f32[2,128,128]{2,1,0:T(8,128)S(1)} %add.106), channel_id=1, source_target_pairs={{72,8},{200,136},{73,9},{201,137},{74,10},{202,138},{75,11},{203,1... | collective-permute-start | bytes 393224 | tf_op jit(solution)/shard_map/ppermute | solution.py:346
  36.5 22.3 %copy-start.1 = (f32[6,128]{1,0:T(8,128)S(1)}, f32[6,128]{1,0:T(8,128)}, u32[]{:S(2)}) copy-start(f32[6,128]{1,0:T(8,128)} %rest_3_.1) | copy-start | bytes 9220
  43.5 5.9 %collective-permute-start.21 = (f32[2,128,128]{2,1,0:T(8,128)S(1)}, f32[2,128,128]{2,1,0:T(8,128)S(1)}, u32[]{:S(2)}, u32[]{:S(2)}) collective-permute-start(f32[2,128,128]{2,1,0:T(8,128)S(1)} %slice_bitcast_fusion), channel_id=1, source_target_pairs={{8,0},{24,16},{40,32},{56,48},{72,64},{88,80},{104,96},{120,112},{... | collective-permute-start | bytes 393224 | tf_op jit(solution)/shard_map/ppermute | solution.py:346
  43.6 15.2 %all-to-all-start = ((bf16[8,256,128]{2,1,0:T(8,128)(2,1)}), bf16[8,256,128]{2,1,0:T(8,128)(2,1)S(1)}, u32[]{:S(2)}, u32[]{:S(2)}) async-start(bf16[8,256,128]{2,1,0:T(8,128)(2,1)} %get-tuple-element.23), calls=%async_computation | async-start | bytes 1048576 | tf_op jit(solution)/shard_map/all_to_all | solution.py:361
  48.7 2.0 %collective-permute-start.13 = (f32[2,128,128]{2,1,0:T(8,128)S(1)}, f32[2,128,128]{2,1,0:T(8,128)S(1)}, u32[]{:S(2)}, u32[]{:S(2)}) collective-permute-start(f32[2,128,128]{2,1,0:T(8,128)S(1)} %add.107), channel_id=1, source_target_pairs={{136,8},{137,9},{138,10},{139,11},{140,12},{141,13},{142,14},{143,... | collective-permute-start | bytes 393224 | tf_op jit(solution)/shard_map/ppermute | solution.py:346
  49.4 8.0 %collective-permute-start.22 = (f32[2,128,128]{2,1,0:T(8,128)S(1)}, f32[2,128,128]{2,1,0:T(8,128)S(1)}, u32[]{:S(2)}, u32[]{:S(2)}) collective-permute-start(f32[2,128,128]{2,1,0:T(8,128)S(1)} %bitcast_add_fusion), channel_id=1, source_target_pairs={{144,128},{152,136},{176,160},{184,168},{208,192},{216,200},{240,2... | collective-permute-start | bytes 393224 | tf_op jit(solution)/shard_map/ppermute | solution.py:346
  50.8 8.0 %collective-permute-start.14 = (f32[2,128,128]{2,1,0:T(8,128)S(1)}, f32[2,128,128]{2,1,0:T(8,128)S(1)}, u32[]{:S(2)}, u32[]{:S(2)}) collective-permute-start(f32[2,128,128]{2,1,0:T(8,128)S(1)} %add.108), channel_id=1, source_target_pairs={{8,0},{9,1},{10,2},{11,3},{12,4},{13,5},{14,6},{15,7}} | collective-permute-start | bytes 393224 | tf_op jit(solution)/shard_map/ppermute | solution.py:392
  57.5 8.1 %collective-permute-start.23 = (f32[2,128,128]{2,1,0:T(8,128)S(1)}, f32[2,128,128]{2,1,0:T(8,128)S(1)}, u32[]{:S(2)}, u32[]{:S(2)}) collective-permute-start(f32[2,128,128]{2,1,0:T(8,128)S(1)} %add.115), channel_id=1, source_target_pairs={{160,128},{168,136},{224,192},{232,200},{48,16},{56,24},{112,80},{... | collective-permute-start | bytes 393224 | tf_op jit(solution)/shard_map/ppermute | solution.py:346
  60.7 12.0 %all-to-all-start.1 = ((bf16[8,256,128]{2,1,0:T(8,128)(2,1)}), bf16[8,256,128]{2,1,0:T(8,128)(2,1)S(1)}, u32[]{:S(2)}, u32[]{:S(2)}) async-start(bf16[8,256,128]{2,1,0:T(8,128)(2,1)} %get-tuple-element.29), calls=%async_computation.1 | async-start | bytes 1048576 | tf_op jit(solution)/shard_map/all_to_all | solution.py:361
  65.6 0.7 collective-permute-start.24
  66.3 1.4 collective-permute-start.25
  67.0 12.7 %collective-permute-start.15 = (f32[2,256,128]{2,1,0:T(8,128)S(1)}, f32[2,256,128]{2,1,0:T(8,128)S(1)}, u32[]{:S(2)}, u32[]{:S(2)}) collective-permute-start(f32[2,256,128]{2,1,0:T(8,128)S(1)} %pad_maximum_fusion.1), channel_id=1, source_target_pairs={{0,8},{1,9},{2,10},{3,11},{4,12},{5,13},{6,14},{7,15}} | collective-permute-start | bytes 786440 | tf_op jit(solution)/shard_map/ppermute | solution.py:401
  67.7 0.7 collective-permute-start.26
  74.6 12.2 %all-to-all-start.2 = ((bf16[8,256,128]{2,1,0:T(8,128)(2,1)}), bf16[8,256,128]{2,1,0:T(8,128)(2,1)S(1)}, u32[]{:S(2)}, u32[]{:S(2)}) async-start(bf16[8,256,128]{2,1,0:T(8,128)(2,1)} %get-tuple-element.32), calls=%async_computation.2 | async-start | bytes 1048576 | tf_op jit(solution)/shard_map/all_to_all | solution.py:361
  79.7 2.7 %collective-permute-start.16 = (f32[2,256,128]{2,1,0:T(8,128)S(1)}, f32[2,256,128]{2,1,0:T(8,128)S(1)}, u32[]{:S(2)}, u32[]{:S(2)}) collective-permute-start(f32[2,256,128]{2,1,0:T(8,128)S(1)} %collective-permute-done.15), channel_id=1, source_target_pairs={{8,136},{9,137},{10,138},{11,139},{12,140},{13,141},{14,142},{15,1... | collective-permute-start | bytes 786440 | tf_op jit(solution)/shard_map/ppermute | solution.py:346
  80.3 0.7 collective-permute-start.31
  81.0 2.1 %collective-permute-start.32 = (f32[256,128]{1,0:T(8,128)S(1)}, f32[256,128]{1,0:T(8,128)S(1)}, u32[]{:S(2)}, u32[]{:S(2)}) collective-permute-start(f32[256,128]{1,0:T(8,128)S(1)} %collective-permute-done.31), channel_id=1, source_target_pairs={{8,136},{9,137},{10,138},{11,139},{12,140},{13,141},{14,142},{15,1... | collective-permute-start | bytes 393224 | tf_op jit(solution)/shard_map/ppermute | solution.py:346
  81.7 2.1 %collective-permute-start.27 = (f32[2,128,128]{2,1,0:T(8,128)S(1)}, f32[2,128,128]{2,1,0:T(8,128)S(1)}, u32[]{:S(2)}, u32[]{:S(2)}) collective-permute-start(f32[2,128,128]{2,1,0:T(8,128)S(1)} %add.119.rest_4_), channel_id=1, source_target_pairs={{8,0},{9,1},{10,2},{11,3},{12,4},{13,5},{14,6},{15,7}} | collective-permute-start | bytes 393224 | tf_op jit(solution)/shard_map/ppermute | solution.py:406
  82.4 7.6 %collective-permute-start.17 = (f32[2,256,128]{2,1,0:T(8,128)S(1)}, f32[2,256,128]{2,1,0:T(8,128)S(1)}, u32[]{:S(2)}, u32[]{:S(2)}) collective-permute-start(f32[2,256,128]{2,1,0:T(8,128)S(1)} %add.110), channel_id=1, source_target_pairs={{8,72},{136,200},{9,73},{137,201},{10,74},{138,202},{11,75},{139,2... | collective-permute-start | bytes 786440 | tf_op jit(solution)/shard_map/ppermute | solution.py:346
  83.2 7.6 %collective-permute-start.33 = (f32[256,128]{1,0:T(8,128)S(1)}, f32[256,128]{1,0:T(8,128)S(1)}, u32[]{:S(2)}, u32[]{:S(2)}) collective-permute-start(f32[256,128]{1,0:T(8,128)S(1)} %add.123), channel_id=1, source_target_pairs={{8,72},{136,200},{9,73},{137,201},{10,74},{138,202},{11,75},{139,2... | collective-permute-start | bytes 393224 | tf_op jit(solution)/shard_map/ppermute | solution.py:346
  87.9 2.8 %collective-permute-start.30 = (f32[256,128]{1,0:T(8,128)S(1)}, f32[256,128]{1,0:T(8,128)S(1)}, u32[]{:S(2)}, u32[]{:S(2)}) collective-permute-start(f32[256,128]{1,0:T(8,128)S(1)} %shard_map.87), channel_id=1, source_target_pairs={{0,192},{1,193},{2,194},{3,195},{4,196},{5,197},{6,198},{7,199}} | collective-permute-start | bytes 393224 | tf_op jit(solution)/shard_map/ppermute | solution.py:346
  88.6 2.1 %collective-permute-start.29 = (f32[256,128]{1,0:T(8,128)S(1)}, f32[256,128]{1,0:T(8,128)S(1)}, u32[]{:S(2)}, u32[]{:S(2)}) collective-permute-start(f32[256,128]{1,0:T(8,128)S(1)} %shard_map.87), channel_id=1, source_target_pairs={{0,128},{1,129},{2,130},{3,131},{4,132},{5,133},{6,134},{7,135}} | collective-permute-start | bytes 393224 | tf_op jit(solution)/shard_map/ppermute | solution.py:346
  89.3 1.5 %collective-permute-start.28 = (f32[256,128]{1,0:T(8,128)S(1)}, f32[256,128]{1,0:T(8,128)S(1)}, u32[]{:S(2)}, u32[]{:S(2)}) collective-permute-start(f32[256,128]{1,0:T(8,128)S(1)} %shard_map.87), channel_id=1, source_target_pairs={{0,64},{1,65},{2,66},{3,67},{4,68},{5,69},{6,70},{7,71}} | collective-permute-start | bytes 393224 | tf_op jit(solution)/shard_map/ppermute | solution.py:346
  90.0 3.4 %collective-permute-start.18 = (f32[2,256,128]{2,1,0:T(8,128)S(1)}, f32[2,256,128]{2,1,0:T(8,128)S(1)}, u32[]{:S(2)}, u32[]{:S(2)}) collective-permute-start(f32[2,256,128]{2,1,0:T(8,128)S(1)} %add.111), channel_id=1, source_target_pairs={{8,40},{72,104},{136,168},{200,232},{9,41},{73,105},{137,169},{201... | collective-permute-start | bytes 786440 | tf_op jit(solution)/shard_map/ppermute | solution.py:346
  90.8 4.0 %collective-permute-start.36 = (f32[256,128]{1,0:T(8,128)S(1)}, f32[256,128]{1,0:T(8,128)S(1)}, u32[]{:S(2)}, u32[]{:S(2)}) collective-permute-start(f32[256,128]{1,0:T(8,128)S(1)} %add_select_fusion), channel_id=1, source_target_pairs={{0,32},{8,40},{64,96},{72,104},{128,160},{136,168},{192,224},{200,... | collective-permute-start | bytes 393224 | tf_op jit(solution)/shard_map/ppermute | solution.py:346
  91.5 37.4 %collective-permute-start.35 = (f32[256,128]{1,0:T(8,128)S(1)}, f32[256,128]{1,0:T(8,128)S(1)}, u32[]{:S(2)}, u32[]{:S(2)}) collective-permute-start(f32[256,128]{1,0:T(8,128)S(1)} %add_select_fusion), channel_id=1, source_target_pairs={{0,112},{8,120},{64,48},{72,56},{128,240},{136,248},{192,176},{200... | collective-permute-start | bytes 393224 | tf_op jit(solution)/shard_map/ppermute | solution.py:346
  92.8 36.1 %collective-permute-start.34 = (f32[256,128]{1,0:T(8,128)S(1)}, f32[256,128]{1,0:T(8,128)S(1)}, u32[]{:S(2)}, u32[]{:S(2)}) collective-permute-start(f32[256,128]{1,0:T(8,128)S(1)} %add_select_fusion), channel_id=1, source_target_pairs={{0,16},{8,24},{64,80},{72,88},{128,144},{136,152},{192,208},{200,2... | collective-permute-start | bytes 393224 | tf_op jit(solution)/shard_map/ppermute | solution.py:346
  93.5 47.0 %collective-permute-start.19 = (f32[2,256,128]{2,1,0:T(8,128)S(1)}, f32[2,256,128]{2,1,0:T(8,128)S(1)}, u32[]{:S(2)}, u32[]{:S(2)}) collective-permute-start(f32[2,256,128]{2,1,0:T(8,128)S(1)} %add.112), channel_id=1, source_target_pairs={{8,24},{40,56},{72,88},{104,120},{136,152},{168,184},{200,216},{23... | collective-permute-start | bytes 786440 | tf_op jit(solution)/shard_map/ppermute | solution.py:346
  128.9 13.6 %collective-permute-start.37 = (f32[256,128]{1,0:T(8,128)S(1)}, f32[256,128]{1,0:T(8,128)S(1)}, u32[]{:S(2)}, u32[]{:S(2)}) collective-permute-start(f32[256,128]{1,0:T(8,128)S(1)} %add_add_fusion), channel_id=1, source_target_pairs={{8,0},{24,16},{40,32},{56,48},{72,64},{88,80},{104,96},{120,112},{... | collective-permute-start | bytes 393224 | tf_op jit(solution)/shard_map/ppermute | solution.py:419
  140.5 3.1 %collective-permute-start.20 = (f32[2,256,128]{2,1,0:T(8,128)S(1)}, f32[2,256,128]{2,1,0:T(8,128)S(1)}, u32[]{:S(2)}, u32[]{:S(2)}) collective-permute-start(f32[2,256,128]{2,1,0:T(8,128)S(1)} %add.113), channel_id=1, source_target_pairs={{24,16},{40,32},{56,48},{72,64},{88,80},{104,96},{120,112},{136,12... | collective-permute-start | bytes 786440 | tf_op jit(solution)/shard_map/ppermute | solution.py:410

commit v4 on v3

--- a/solution.py
+++ b/solution.py
@@ -213,24 +213,27 @@
     solve_into(inverse_ref, net, density_ref, copies_ref)
 
 
-def chain_kernel(step, last, lists_s, blocks_h, *rest):
+def chain_kernel(lags, ahead, last, lists_s, blocks_h, *rest):
+    step = len(lags)
     fresh = rest[:step]
     rest = rest[step:]
-    if last:
+    copies_ref = None
+    if ahead:
+        mode_ref, sum_ref, blocks_v, acc, sems = rest
+    elif last:
         mode_ref, incident_ref, field_ref, inverse_ref, density_ref, blocks_v, acc, sems = rest
-        copies_ref = None
     else:
         mode_ref, incident_ref, field_ref, inverse_ref, density_ref, copies_ref, blocks_v, acc, sems = rest
     entries, size, _ = blocks_h.shape
     row_blocks = acc.shape[0]
-    counts = [lists_s[STEPS * entries + j] for j in range(step)]
+    counts = [lists_s[STEPS * entries + j] for j in lags]
     root = lax.axis_index("lag") == 0
     groups = [jnp.where(root, (count + UNROLL - 1) // UNROLL, 0) for count in counts]
     firsts = [sum(groups[:j]) for j in range(step)]
 
     def code_of(j, g, u):
         at = g * UNROLL + u
-        return at, lists_s[j * entries + jnp.minimum(at, counts[j] - 1)]
+        return at, lists_s[lags[j] * entries + jnp.minimum(at, counts[j] - 1)]
 
     for j in range(step):
 
@@ -246,8 +249,8 @@
         lax.fori_loop(0, groups[j], begin, 0)
     acc[...] = jnp.zeros_like(acc)
     for j in range(step):
-        state = fresh[step - 1 - j]
-        factor = mode_ref[pl.ds(j, 1), :]
+        state = fresh[j]
+        factor = mode_ref[pl.ds(lags[j], 1), :]
 
         def group(g, carry, j=j, state=state, factor=factor):
             slot = firsts[j] + g
@@ -272,6 +275,9 @@
             return carry
 
         lax.fori_loop(0, groups[j], group, 0)
+    if ahead:
+        sum_ref[...] = acc[...]
+        return
     net = incident_ref[...].astype(jnp.float32).reshape(acc.shape) - field_ref[...] - acc[...]
     solve_into(inverse_ref, net, density_ref, copies_ref)
 
@@ -294,19 +300,32 @@
             compiler_params=params,
             name="first_density",
         )(incident, field, inverse)
-    slots = blocks.shape[0] // UNROLL + step
-    return pl.pallas_call(
-        functools.partial(chain_kernel, step, last),
-        out_shape=(density,) if last else (density, copies),
-        in_specs=[in_smem, pl.BlockSpec(memory_space=pltpu.HBM)] + [in_vmem] * (step + 4),
-        out_specs=(in_vmem,) if last else (in_vmem, in_vmem),
-        scratch_shapes=[
-            pltpu.VMEM(((slots * UNROLL), *blocks.shape[1:]), blocks.dtype),
-            pltpu.VMEM(field.shape, jnp.float32),
-            pltpu.SemaphoreType.DMA((slots,)),
-        ],
-        compiler_params=params,
-    )(lists, in_hbm_only(blocks), *fresh, mode_kernel, incident, field, inverse)
+    sum_shape = (rows // size, size, modes)
+
+    def call(lags, ahead, states, more):
+        slots = blocks.shape[0] // UNROLL + len(lags)
+        if ahead:
+            out_shape = (jax.ShapeDtypeStruct(sum_shape, jnp.float32),)
+        else:
+            out_shape = (density,) if last else (density, copies)
+        return pl.pallas_call(
+            functools.partial(chain_kernel, lags, ahead, last),
+            out_shape=out_shape,
+            in_specs=[in_smem, pl.BlockSpec(memory_space=pltpu.HBM)]
+            + [in_vmem] * (len(states) + 1 + len(more)),
+            out_specs=(in_vmem,) * len(out_shape),
+            scratch_shapes=[
+                pltpu.VMEM(((slots * UNROLL), *blocks.shape[1:]), blocks.dtype),
+                pltpu.VMEM(sum_shape, jnp.float32),
+                pltpu.SemaphoreType.DMA((slots,)),
+            ],
+            compiler_params=params,
+        )(lists, in_hbm_only(blocks), *states, mode_kernel, *more)
+
+    if step > 1:
+        (old,) = call(tuple(range(1, step)), True, fresh[step - 2 :: -1], ())
+        field = field + old
+    return call((0,), False, fresh[-1:], (incident, field, inverse))
 
 
 def lag_of(x_hi, z, core):

time: 146 us -> 151 us (1.034)
  the two profiles are of different devices: /device:TPU:97 before, /device:TPU:105 now
where the time goes in v4:
time: 151 us; the launch traced here: 150 us
  starting transfers between devices  65.6 us (43%)
  waiting for transfers between devices  56.8 us (38%)
  Pallas kernels  25.5 us (17%)
    ppermute x30, waiting for transfers between devices, plus_arrived(): arrived = [lax.ppermute(operand, 'lag', pairs) for pairs in levels]  38.3 us
    ppermute x30, starting transfers between devices, plus_arrived(): arrived = [lax.ppermute(operand, 'lag', pairs) for pairs in levels]  25.9 us
    pallas_call x3, Pallas kernels, fields(): pl.pallas_call(functools.partial(field_kernel, steps, halo_shapes), out_s...  18 us
    all_to_all x3, starting transfers between devices, to_everyone(): everyone = lax.all_to_all(copies, 'pts', 0, 0, tiled=True)  15.2 us
    ppermute x1, waiting for transfers between devices, per_device(): halo_1 = lax.ppermute(piece_1, 'lag', next_lag)  13.3 us
    ppermute x1, starting transfers between devices, per_device(): other = lax.ppermute(late, 'lag', SWAP)  11 us
    ppermute x1, starting transfers between devices, per_device(): halo_2 = lax.ppermute(piece_2, 'lag', next_lag)  6.87 us
    pallas_call x5, Pallas kernels, call(): pl.pallas_call(functools.partial(chain_kernel, lags, ahead, last), out_sh...  6.5 us
  transfers between devices with their start and end apart: 41, of which 9 were waited for; matrix products, arithmetic and copies ran while one was open for 0% of the time, Pallas kernels for 13%

profile of v4, /device:TPU:105, one launch (start us, length us, event | category | flops | bytes accessed | tf_op | source)
XLA Modules:
  0.0 150.2 jit_solution(11781268102171657987)
XLA Ops:
  0.0 6.2 %shard_map.82 = (f32[1,2,128,128]{3,2,1,0:T(8,128)S(1)}, bf16[1,2048,128]{2,1,0:T(8,128)(2,1)S(1)}, bf16[2,2048,128]{2,1,0:T(8,128)(2,1)S(1)}) custom-call(s32[192]{0:T(256)} %row_h.5, s32[192]{0:T(256)} %col_h.5, s32[192]{0:T(256)} %lag_h.5, f32[6,128]{1,0:T(8,128)} %rest_1_.7, bf16[192,128,128]{2,1,0:T(8,128)(2,1)} %blocks_h.15, ...), custom_call_target="tpu_custom_call" | custom-call | tf_op jit(solution)/shard_map/pallas_call | solution.py:163
  6.2 2.7 %collective-permute-start = (f32[2,128,128]{2,1,0:T(8,128)S(1)}, f32[2,128,128]{2,1,0:T(8,128)S(1)}, u32[]{:S(2)}, u32[]{:S(2)}) collective-permute-start(f32[2,128,128]{2,1,0:T(8,128)S(1)} %bitcast.36), channel_id=1, source_target_pairs={{8,0},{24,16},{40,32},{56,48},{72,64},{88,80},{104,96},{120,112},{... | collective-permute-start | bytes 393224 | tf_op jit(solution)/shard_map/ppermute | solution.py:365
  8.9 1.0 collective-permute-done
  9.9 0.7 collective-permute-start.3
  10.6 0.7 collective-permute-start.2
  11.2 0.7 collective-permute-start.1
  11.9 6.9 %collective-permute-start.7 = (bf16[2,2048,128]{2,1,0:T(8,128)(2,1)S(1)}, bf16[2,2048,128]{2,1,0:T(8,128)(2,1)S(1)}, u32[]{:S(2)}, u32[]{:S(2)}) collective-permute-start(bf16[2,2048,128]{2,1,0:T(8,128)(2,1)S(1)} %get-tuple-element.22), channel_id=1, source_target_pairs={{0,8},{8,16},{16,24},{24,32},{32,40},{40,48},{48,56},{56,64},{64,7... | collective-permute-start | bytes 3145736 | tf_op jit(solution)/shard_map/ppermute | solution.py:401
  18.8 1.9 %collective-permute-start.8 = (bf16[1,2048,128]{2,1,0:T(8,128)(2,1)S(1)}, bf16[1,2048,128]{2,1,0:T(8,128)(2,1)S(1)}, u32[]{:S(2)}, u32[]{:S(2)}) collective-permute-start(bf16[1,2048,128]{2,1,0:T(8,128)(2,1)S(1)} %get-tuple-element.25), channel_id=1, source_target_pairs={{0,8},{8,16},{16,24},{24,32},{32,40},{40,48},{48,56},{56,64},{64,7... | collective-permute-start | bytes 1572872 | tf_op jit(solution)/shard_map/ppermute | solution.py:400
  20.8 0.7 collective-permute-start.6
  21.5 0.7 collective-permute-start.5
  22.2 0.7 collective-permute-start.4
  22.9 13.3 %collective-permute-done.8.rest_1_.rest_0_ = bf16[1,2048,128]{2,1,0:T(8,128)(2,1)S(1)} collective-permute-done((bf16[1,2048,128]{2,1,0:T(8,128)(2,1)S(1)}, bf16[1,2048,128]{2,1,0:T(8,128)(2,1)S(1)}, u32[]{:S(2)}, u32[]{:S(2)}) %collective-permute-start.8) | collective-permute-done | bytes 524320 | tf_op jit(solution)/shard_map/ppermute | solution.py:400
  36.1 4.9 %shard_map.84 = f32[1,2,128,128]{3,2,1,0:T(8,128)S(1)} custom-call(s32[192]{0:T(256)} %row_h.5, s32[192]{0:T(256)} %col_h.5, s32[192]{0:T(256)} %lag_h.5, f32[6,128]{1,0:T(8,128)} %rest_1_.7, bf16[192,128,128]{2,1,0:T(8,128)(2,1)} %blocks_h.15, bf16[6,2048,128]{2,1,0:T(8,128)(2,1)} %history_h.5, bf16[1,2048,128]{2,1,0:T(8,128)(2,1)S(1)} %collective-permute-done.8.rest_1_.rest_0_), custom_call_target="tpu_custom_call" | custom-call | tf_op jit(solution)/shard_map/pallas_call | solution.py:163
  41.0 1.3 collective-permute-start.9
  42.4 1.0 first_density.1
  43.4 2.6 %collective-permute-done.9 = f32[2,128,128]{2,1,0:T(8,128)S(1)} collective-permute-done((f32[2,128,128]{2,1,0:T(8,128)S(1)}, f32[2,128,128]{2,1,0:T(8,128)S(1)}, u32[]{:S(2)}, u32[]{:S(2)}) %collective-permute-start.9) | collective-permute-done | bytes 131104 | tf_op jit(solution)/shard_map/ppermute | solution.py:365
  46.0 1.9 %collective-permute-start.10 = (f32[2,128,128]{2,1,0:T(8,128)S(1)}, f32[2,128,128]{2,1,0:T(8,128)S(1)}, u32[]{:S(2)}, u32[]{:S(2)}) collective-permute-start(f32[2,128,128]{2,1,0:T(8,128)S(1)} %bitcast_add_fusion.1), channel_id=1, source_target_pairs={{24,8},{56,40},{88,72},{120,104},{152,136},{184,168},{216,200},{24... | collective-permute-start | bytes 393224 | tf_op jit(solution)/shard_map/ppermute | solution.py:365
  48.0 7.0 %shard_map.83 = (f32[2,2,128,128]{3,2,1,0:T(8,128)S(1)}, s32[772]{0:T(1024)S(1)}) custom-call(s32[192]{0:T(256)} %row_h.5, s32[192]{0:T(256)} %col_h.5, s32[192]{0:T(256)} %lag_h.5, f32[6,128]{1,0:T(8,128)} %rest_1_.7, bf16[192,128,128]{2,1,0:T(8,128)(2,1)} %blocks_h.15, bf16[6,2048,128]{2,1,0:T(8,128)(2,1)} %history_h.5, ...), custom_call_target="tpu_custom_call" | custom-call | tf_op jit(solution)/shard_map/pallas_call | solution.py:163
  55.1 5.3 %all-to-all-start = ((bf16[8,256,128]{2,1,0:T(8,128)(2,1)}), bf16[8,256,128]{2,1,0:T(8,128)(2,1)S(1)}, u32[]{:S(2)}, u32[]{:S(2)}) async-start(bf16[8,256,128]{2,1,0:T(8,128)(2,1)} %get-tuple-element.23), calls=%async_computation | async-start | bytes 1048576 | tf_op jit(solution)/shard_map/all_to_all | solution.py:380
  61.1 1.3 collective-permute-start.22
  63.1 4.0 %collective-permute-done.22 = f32[2,128,128]{2,1,0:T(8,128)S(1)} collective-permute-done((f32[2,128,128]{2,1,0:T(8,128)S(1)}, f32[2,128,128]{2,1,0:T(8,128)S(1)}, u32[]{:S(2)}, u32[]{:S(2)}) %collective-permute-start.22) | collective-permute-done | bytes 131104 | tf_op jit(solution)/shard_map/ppermute | solution.py:365
  67.1 1.3 collective-permute-start.23
  68.5 0.7 collective-permute-start.13
  69.2 1.2 collective-permute-done.23
  70.4 0.7 collective-permute-start.24
  72.5 1.9 %shard_map.85 = (f32[256,128]{1,0:T(8,128)S(1)}, bf16[8,256,128]{2,1,0:T(8,128)(2,1)}) custom-call(s32[772]{0:T(1024)S(1)} %get-tuple-element.26.lists_s, bf16[192,128,128]{2,1,0:T(8,128)(2,1)} %blocks_h.15, bf16[2048,128]{1,0:T(8,128)(2,1)S(1)} %bitcast.25, f32[6,128]{1,0:T(8,128)S(1)} %copy-done.1, bf16[256,128]{1,0:T(8,128)(2,1)S(1)} %get-tuple-element.40.rest_2_, ...), custom_call_target="tpu_custom_call" | custom-call | tf_op jit(solution)/shard_map/pallas_call | solution.py:311
  74.4 5.2 %all-to-all-start.1 = ((bf16[8,256,128]{2,1,0:T(8,128)(2,1)}), bf16[8,256,128]{2,1,0:T(8,128)(2,1)S(1)}, u32[]{:S(2)}, u32[]{:S(2)}) async-start(bf16[8,256,128]{2,1,0:T(8,128)(2,1)} %get-tuple-element.29), calls=%async_computation.1 | async-start | bytes 1048576 | tf_op jit(solution)/shard_map/all_to_all | solution.py:380
  79.6 0.7 collective-permute-start.26
  80.2 0.9 shard_map.86
  81.1 0.7 collective-permute-start.15
  81.9 3.4 %all-to-all-done.1 = bf16[8,256,128]{2,1,0:T(8,128)(2,1)S(1)} async-done(((bf16[8,256,128]{2,1,0:T(8,128)(2,1)}), bf16[8,256,128]{2,1,0:T(8,128)(2,1)S(1)}, u32[]{:S(2)}, u32[]{:S(2)}) %all-to-all-start.1) | async-done | bytes 524320 | tf_op jit(solution)/shard_map/all_to_all | solution.py:380
  85.3 1.9 %shard_map.87 = (f32[256,128]{1,0:T(8,128)S(1)}, bf16[8,256,128]{2,1,0:T(8,128)(2,1)}) custom-call(s32[772]{0:T(1024)S(1)} %get-tuple-element.26.lists_s, bf16[192,128,128]{2,1,0:T(8,128)(2,1)} %blocks_h.15, bf16[2048,128]{1,0:T(8,128)(2,1)S(1)} %bitcast.28, f32[6,128]{1,0:T(8,128)S(1)} %copy-done.1, bf16[256,128]{1,0:T(8,128)(2,1)S(1)} %get-tuple-element.42.rest_2_, ...), custom_call_target="tpu_custom_call" | custom-call | tf_op jit(solution)/shard_map/pallas_call | solution.py:311
  87.2 4.8 %all-to-all-start.2 = ((bf16[8,256,128]{2,1,0:T(8,128)(2,1)}), bf16[8,256,128]{2,1,0:T(8,128)(2,1)S(1)}, u32[]{:S(2)}, u32[]{:S(2)}) async-start(bf16[8,256,128]{2,1,0:T(8,128)(2,1)} %get-tuple-element.32), calls=%async_computation.2 | async-start | bytes 1048576 | tf_op jit(solution)/shard_map/all_to_all | solution.py:380
  92.6 0.7 collective-permute-start.31
  93.3 0.7 collective-permute-start.27
  94.7 0.7 collective-permute-start.17
  95.4 0.9 shard_map.88
  96.4 0.7 collective-permute-start.33
  97.0 0.7 all-to-all-done.2
  97.7 1.1 shard_map.89
  100.9 0.7 collective-permute-start.18
  102.3 1.3 collective-permute-start.35
  104.3 1.3 collective-permute-start.19
  105.7 29.4 %collective-permute-done.35 = f32[256,128]{1,0:T(8,128)S(1)} collective-permute-done((f32[256,128]{1,0:T(8,128)S(1)}, f32[256,128]{1,0:T(8,128)S(1)}, u32[]{:S(2)}, u32[]{:S(2)}) %collective-permute-start.35) | collective-permute-done | bytes 131104 | tf_op jit(solution)/shard_map/ppermute | solution.py:365
  135.1 11.0 %collective-permute-start.37 = (f32[256,128]{1,0:T(8,128)S(1)}, f32[256,128]{1,0:T(8,128)S(1)}, u32[]{:S(2)}, u32[]{:S(2)}) collective-permute-start(f32[256,128]{1,0:T(8,128)S(1)} %add_add_fusion), channel_id=1, source_target_pairs={{8,0},{24,16},{40,32},{56,48},{72,64},{88,80},{104,96},{120,112},{... | collective-permute-start | bytes 393224 | tf_op jit(solution)/shard_map/ppermute | solution.py:438
  146.2 1.9 %collective-permute-start.20 = (f32[2,256,128]{2,1,0:T(8,128)S(1)}, f32[2,256,128]{2,1,0:T(8,128)S(1)}, u32[]{:S(2)}, u32[]{:S(2)}) collective-permute-start(f32[2,256,128]{2,1,0:T(8,128)S(1)} %add.119), channel_id=1, source_target_pairs={{24,16},{40,32},{56,48},{72,64},{88,80},{104,96},{120,112},{136,12... | collective-permute-start | bytes 786440 | tf_op jit(solution)/shard_map/ppermute | solution.py:429
  148.2 1.1 collective-permute-done.20
  149.3 0.8 pad_maximum_fusion
  (77 shorter events, 8.2 us)
Async XLA Ops:
  0.0 22.8 %copy-start.2 = (bf16[4,256,128]{2,1,0:T(8,128)(2,1)S(1)}, bf16[4,256,128]{2,1,0:T(8,128)(2,1)}, u32[]{:S(2)}) copy-start(bf16[4,256,128]{2,1,0:T(8,128)(2,1)} %param.9) | copy-start | bytes 786436
  6.2 36.2 %copy-start = (f32[256,128]{1,0:T(8,128)S(1)}, f32[256,128]{1,0:T(8,128)}, u32[]{:S(2)}) copy-start(f32[256,128]{1,0:T(8,128)} %rest_4_.5) | copy-start | bytes 393220
  6.2 3.7 %collective-permute-start = (f32[2,128,128]{2,1,0:T(8,128)S(1)}, f32[2,128,128]{2,1,0:T(8,128)S(1)}, u32[]{:S(2)}, u32[]{:S(2)}) collective-permute-start(f32[2,128,128]{2,1,0:T(8,128)S(1)} %bitcast.36), channel_id=1, source_target_pairs={{8,0},{24,16},{40,32},{56,48},{72,64},{88,80},{104,96},{120,112},{... | collective-permute-start | bytes 393224 | tf_op jit(solution)/shard_map/ppermute | solution.py:365
  9.9 10.8 %collective-permute-start.3 = (f32[2,128,128]{2,1,0:T(8,128)S(1)}, f32[2,128,128]{2,1,0:T(8,128)S(1)}, u32[]{:S(2)}, u32[]{:S(2)}) collective-permute-start(f32[2,128,128]{2,1,0:T(8,128)S(1)} %bitcast_add_fusion.2), channel_id=1, source_target_pairs={{32,0},{96,64},{160,128},{224,192},{33,1},{97,65},{161,129},{225,1... | collective-permute-start | bytes 393224 | tf_op jit(solution)/shard_map/ppermute | solution.py:365
  10.6 10.2 %collective-permute-start.2 = (f32[2,128,128]{2,1,0:T(8,128)S(1)}, f32[2,128,128]{2,1,0:T(8,128)S(1)}, u32[]{:S(2)}, u32[]{:S(2)}) collective-permute-start(f32[2,128,128]{2,1,0:T(8,128)S(1)} %bitcast_add_fusion.2), channel_id=1, source_target_pairs={{112,0},{48,64},{240,128},{176,192},{113,1},{49,65},{241,129},{177... | collective-permute-start | bytes 393224 | tf_op jit(solution)/shard_map/ppermute | solution.py:365
  11.2 9.5 %collective-permute-start.1 = (f32[2,128,128]{2,1,0:T(8,128)S(1)}, f32[2,128,128]{2,1,0:T(8,128)S(1)}, u32[]{:S(2)}, u32[]{:S(2)}) collective-permute-start(f32[2,128,128]{2,1,0:T(8,128)S(1)} %bitcast_add_fusion.2), channel_id=1, source_target_pairs={{16,0},{80,64},{144,128},{208,192},{17,1},{81,65},{145,129},{209,1... | collective-permute-start | bytes 393224 | tf_op jit(solution)/shard_map/ppermute | solution.py:365
  11.9 36.0 %collective-permute-start.7 = (bf16[2,2048,128]{2,1,0:T(8,128)(2,1)S(1)}, bf16[2,2048,128]{2,1,0:T(8,128)(2,1)S(1)}, u32[]{:S(2)}, u32[]{:S(2)}) collective-permute-start(bf16[2,2048,128]{2,1,0:T(8,128)(2,1)S(1)} %get-tuple-element.22), channel_id=1, source_target_pairs={{0,8},{8,16},{16,24},{24,32},{32,40},{40,48},{48,56},{56,64},{64,7... | collective-permute-start | bytes 3145736 | tf_op jit(solution)/shard_map/ppermute | solution.py:401
  18.8 17.3 %collective-permute-start.8 = (bf16[1,2048,128]{2,1,0:T(8,128)(2,1)S(1)}, bf16[1,2048,128]{2,1,0:T(8,128)(2,1)S(1)}, u32[]{:S(2)}, u32[]{:S(2)}) collective-permute-start(bf16[1,2048,128]{2,1,0:T(8,128)(2,1)S(1)} %get-tuple-element.25), channel_id=1, source_target_pairs={{0,8},{8,16},{16,24},{24,32},{32,40},{40,48},{48,56},{56,64},{64,7... | collective-permute-start | bytes 1572872 | tf_op jit(solution)/shard_map/ppermute | solution.py:400
  20.8 21.5 %collective-permute-start.6 = (f32[2,128,128]{2,1,0:T(8,128)S(1)}, f32[2,128,128]{2,1,0:T(8,128)S(1)}, u32[]{:S(2)}, u32[]{:S(2)}) collective-permute-start(f32[2,128,128]{2,1,0:T(8,128)S(1)} %add_add_fusion.2), channel_id=1, source_target_pairs={{192,0},{193,1},{194,2},{195,3},{196,4},{197,5},{198,6},{199,7}} | collective-permute-start | bytes 393224 | tf_op jit(solution)/shard_map/ppermute | solution.py:365
  21.5 20.9 %collective-permute-start.5 = (f32[2,128,128]{2,1,0:T(8,128)S(1)}, f32[2,128,128]{2,1,0:T(8,128)S(1)}, u32[]{:S(2)}, u32[]{:S(2)}) collective-permute-start(f32[2,128,128]{2,1,0:T(8,128)S(1)} %add_add_fusion.2), channel_id=1, source_target_pairs={{128,0},{129,1},{130,2},{131,3},{132,4},{133,5},{134,6},{135,7}} | collective-permute-start | bytes 393224 | tf_op jit(solution)/shard_map/ppermute | solution.py:365
  22.2 20.2 %collective-permute-start.4 = (f32[2,128,128]{2,1,0:T(8,128)S(1)}, f32[2,128,128]{2,1,0:T(8,128)S(1)}, u32[]{:S(2)}, u32[]{:S(2)}) collective-permute-start(f32[2,128,128]{2,1,0:T(8,128)S(1)} %add_add_fusion.2), channel_id=1, source_target_pairs={{64,0},{65,1},{66,2},{67,3},{68,4},{69,5},{70,6},{71,7}} | collective-permute-start | bytes 393224 | tf_op jit(solution)/shard_map/ppermute | solution.py:365
  41.0 5.0 %collective-permute-start.9 = (f32[2,128,128]{2,1,0:T(8,128)S(1)}, f32[2,128,128]{2,1,0:T(8,128)S(1)}, u32[]{:S(2)}, u32[]{:S(2)}) collective-permute-start(f32[2,128,128]{2,1,0:T(8,128)S(1)} %bitcast.31), channel_id=1, source_target_pairs={{0,8},{16,24},{32,40},{48,56},{64,72},{80,88},{96,104},{112,120},{... | collective-permute-start | bytes 393224 | tf_op jit(solution)/shard_map/ppermute | solution.py:365
  46.0 14.3 %collective-permute-start.10 = (f32[2,128,128]{2,1,0:T(8,128)S(1)}, f32[2,128,128]{2,1,0:T(8,128)S(1)}, u32[]{:S(2)}, u32[]{:S(2)}) collective-permute-start(f32[2,128,128]{2,1,0:T(8,128)S(1)} %bitcast_add_fusion.1), channel_id=1, source_target_pairs={{24,8},{56,40},{88,72},{120,104},{152,136},{184,168},{216,200},{24... | collective-permute-start | bytes 393224 | tf_op jit(solution)/shard_map/ppermute | solution.py:365
  48.0 24.5 %copy-start.1 = (f32[6,128]{1,0:T(8,128)S(1)}, f32[6,128]{1,0:T(8,128)}, u32[]{:S(2)}) copy-start(f32[6,128]{1,0:T(8,128)} %rest_1_.7) | copy-start | bytes 9220
  55.0 6.1 %collective-permute-start.21 = (f32[2,128,128]{2,1,0:T(8,128)S(1)}, f32[2,128,128]{2,1,0:T(8,128)S(1)}, u32[]{:S(2)}, u32[]{:S(2)}) collective-permute-start(f32[2,128,128]{2,1,0:T(8,128)S(1)} %slice_bitcast_fusion), channel_id=1, source_target_pairs={{8,0},{24,16},{40,32},{56,48},{72,64},{88,80},{104,96},{120,112},{... | collective-permute-start | bytes 393224 | tf_op jit(solution)/shard_map/ppermute | solution.py:365
  55.1 17.4 %all-to-all-start = ((bf16[8,256,128]{2,1,0:T(8,128)(2,1)}), bf16[8,256,128]{2,1,0:T(8,128)(2,1)S(1)}, u32[]{:S(2)}, u32[]{:S(2)}) async-start(bf16[8,256,128]{2,1,0:T(8,128)(2,1)} %get-tuple-element.23), calls=%async_computation | async-start | bytes 1048576 | tf_op jit(solution)/shard_map/all_to_all | solution.py:380
  60.4 2.0 %collective-permute-start.11 = (f32[2,128,128]{2,1,0:T(8,128)S(1)}, f32[2,128,128]{2,1,0:T(8,128)S(1)}, u32[]{:S(2)}, u32[]{:S(2)}) collective-permute-start(f32[2,128,128]{2,1,0:T(8,128)S(1)} %add.111), channel_id=1, source_target_pairs={{40,8},{104,72},{168,136},{232,200},{41,9},{105,73},{169,137},{233... | collective-permute-start | bytes 393224 | tf_op jit(solution)/shard_map/ppermute | solution.py:365
  61.1 6.0 %collective-permute-start.22 = (f32[2,128,128]{2,1,0:T(8,128)S(1)}, f32[2,128,128]{2,1,0:T(8,128)S(1)}, u32[]{:S(2)}, u32[]{:S(2)}) collective-permute-start(f32[2,128,128]{2,1,0:T(8,128)S(1)} %bitcast_add_fusion), channel_id=1, source_target_pairs={{144,128},{152,136},{176,160},{184,168},{208,192},{216,200},{240,2... | collective-permute-start | bytes 393224 | tf_op jit(solution)/shard_map/ppermute | solution.py:365
  62.5 6.0 %collective-permute-start.12 = (f32[2,128,128]{2,1,0:T(8,128)S(1)}, f32[2,128,128]{2,1,0:T(8,128)S(1)}, u32[]{:S(2)}, u32[]{:S(2)}) collective-permute-start(f32[2,128,128]{2,1,0:T(8,128)S(1)} %add.112), channel_id=1, source_target_pairs={{72,8},{200,136},{73,9},{201,137},{74,10},{202,138},{75,11},{203,1... | collective-permute-start | bytes 393224 | tf_op jit(solution)/shard_map/ppermute | solution.py:365
  67.1 3.2 %collective-permute-start.23 = (f32[2,128,128]{2,1,0:T(8,128)S(1)}, f32[2,128,128]{2,1,0:T(8,128)S(1)}, u32[]{:S(2)}, u32[]{:S(2)}) collective-permute-start(f32[2,128,128]{2,1,0:T(8,128)S(1)} %add.121), channel_id=1, source_target_pairs={{160,128},{168,136},{224,192},{232,200},{48,16},{56,24},{112,80},{... | collective-permute-start | bytes 393224 | tf_op jit(solution)/shard_map/ppermute | solution.py:365
  68.5 2.6 %collective-permute-start.13 = (f32[2,128,128]{2,1,0:T(8,128)S(1)}, f32[2,128,128]{2,1,0:T(8,128)S(1)}, u32[]{:S(2)}, u32[]{:S(2)}) collective-permute-start(f32[2,128,128]{2,1,0:T(8,128)S(1)} %add.113), channel_id=1, source_target_pairs={{136,8},{137,9},{138,10},{139,11},{140,12},{141,13},{142,14},{143,... | collective-permute-start | bytes 393224 | tf_op jit(solution)/shard_map/ppermute | solution.py:365
  70.4 1.4 collective-permute-start.24
  71.1 1.4 collective-permute-start.14
  71.8 7.7 %collective-permute-start.25 = (f32[2,128,128]{2,1,0:T(8,128)S(1)}, f32[2,128,128]{2,1,0:T(8,128)S(1)}, u32[]{:S(2)}, u32[]{:S(2)}) collective-permute-start(f32[2,128,128]{2,1,0:T(8,128)S(1)} %add.123), channel_id=1, source_target_pairs={{128,16},{136,24},{129,17},{137,25},{130,18},{138,26},{131,19},{13... | collective-permute-start | bytes 393224 | tf_op jit(solution)/shard_map/ppermute | solution.py:365
  74.4 10.9 %all-to-all-start.1 = ((bf16[8,256,128]{2,1,0:T(8,128)(2,1)}), bf16[8,256,128]{2,1,0:T(8,128)(2,1)S(1)}, u32[]{:S(2)}, u32[]{:S(2)}) async-start(bf16[8,256,128]{2,1,0:T(8,128)(2,1)} %get-tuple-element.29), calls=%async_computation.1 | async-start | bytes 1048576 | tf_op jit(solution)/shard_map/all_to_all | solution.py:380
  79.6 2.3 %collective-permute-start.26 = (f32[2,128,128]{2,1,0:T(8,128)S(1)}, f32[2,128,128]{2,1,0:T(8,128)S(1)}, u32[]{:S(2)}, u32[]{:S(2)}) collective-permute-start(f32[2,128,128]{2,1,0:T(8,128)S(1)} %add.124), channel_id=1, source_target_pairs={{16,0},{24,8},{17,1},{25,9},{18,2},{26,10},{19,3},{27,11},{20,4},{... | collective-permute-start | bytes 393224 | tf_op jit(solution)/shard_map/ppermute | solution.py:365
  81.1 10.8 %collective-permute-start.15 = (f32[2,256,128]{2,1,0:T(8,128)S(1)}, f32[2,256,128]{2,1,0:T(8,128)S(1)}, u32[]{:S(2)}, u32[]{:S(2)}) collective-permute-start(f32[2,256,128]{2,1,0:T(8,128)S(1)} %pad_maximum_fusion.1), channel_id=1, source_target_pairs={{0,8},{1,9},{2,10},{3,11},{4,12},{5,13},{6,14},{7,15}} | collective-permute-start | bytes 786440 | tf_op jit(solution)/shard_map/ppermute | solution.py:420
  87.2 10.5 %all-to-all-start.2 = ((bf16[8,256,128]{2,1,0:T(8,128)(2,1)}), bf16[8,256,128]{2,1,0:T(8,128)(2,1)S(1)}, u32[]{:S(2)}, u32[]{:S(2)}) async-start(bf16[8,256,128]{2,1,0:T(8,128)(2,1)} %get-tuple-element.32), calls=%async_computation.2 | async-start | bytes 1048576 | tf_op jit(solution)/shard_map/all_to_all | solution.py:380
  92.0 2.7 %collective-permute-start.16 = (f32[2,256,128]{2,1,0:T(8,128)S(1)}, f32[2,256,128]{2,1,0:T(8,128)S(1)}, u32[]{:S(2)}, u32[]{:S(2)}) collective-permute-start(f32[2,256,128]{2,1,0:T(8,128)S(1)} %collective-permute-done.15), channel_id=1, source_target_pairs={{8,136},{9,137},{10,138},{11,139},{12,140},{13,141},{14,142},{15,1... | collective-permute-start | bytes 786440 | tf_op jit(solution)/shard_map/ppermute | solution.py:365
  92.6 1.4 collective-permute-start.31
  93.3 3.0 %collective-permute-start.27 = (f32[2,128,128]{2,1,0:T(8,128)S(1)}, f32[2,128,128]{2,1,0:T(8,128)S(1)}, u32[]{:S(2)}, u32[]{:S(2)}) collective-permute-start(f32[2,128,128]{2,1,0:T(8,128)S(1)} %get-tuple-element.33), channel_id=1, source_target_pairs={{8,0},{9,1},{10,2},{11,3},{12,4},{13,5},{14,6},{15,7}} | collective-permute-start | bytes 393224 | tf_op jit(solution)/shard_map/ppermute | solution.py:425
  94.0 2.3 %collective-permute-start.32 = (f32[256,128]{1,0:T(8,128)S(1)}, f32[256,128]{1,0:T(8,128)S(1)}, u32[]{:S(2)}, u32[]{:S(2)}) collective-permute-start(f32[256,128]{1,0:T(8,128)S(1)} %collective-permute-done.31), channel_id=1, source_target_pairs={{8,136},{9,137},{10,138},{11,139},{12,140},{13,141},{14,142},{15,1... | collective-permute-start | bytes 393224 | tf_op jit(solution)/shard_map/ppermute | solution.py:365
  94.7 6.1 %collective-permute-start.17 = (f32[2,256,128]{2,1,0:T(8,128)S(1)}, f32[2,256,128]{2,1,0:T(8,128)S(1)}, u32[]{:S(2)}, u32[]{:S(2)}) collective-permute-start(f32[2,256,128]{2,1,0:T(8,128)S(1)} %add.116), channel_id=1, source_target_pairs={{8,72},{136,200},{9,73},{137,201},{10,74},{138,202},{11,75},{139,2... | collective-permute-start | bytes 786440 | tf_op jit(solution)/shard_map/ppermute | solution.py:365
  96.4 5.2 %collective-permute-start.33 = (f32[256,128]{1,0:T(8,128)S(1)}, f32[256,128]{1,0:T(8,128)S(1)}, u32[]{:S(2)}, u32[]{:S(2)}) collective-permute-start(f32[256,128]{1,0:T(8,128)S(1)} %add.131), channel_id=1, source_target_pairs={{8,72},{136,200},{9,73},{137,201},{10,74},{138,202},{11,75},{139,2... | collective-permute-start | bytes 393224 | tf_op jit(solution)/shard_map/ppermute | solution.py:365
  98.8 2.8 %collective-permute-start.30 = (f32[256,128]{1,0:T(8,128)S(1)}, f32[256,128]{1,0:T(8,128)S(1)}, u32[]{:S(2)}, u32[]{:S(2)}) collective-permute-start(f32[256,128]{1,0:T(8,128)S(1)} %shard_map.89), channel_id=1, source_target_pairs={{0,192},{1,193},{2,194},{3,195},{4,196},{5,197},{6,198},{7,199}} | collective-permute-start | bytes 393224 | tf_op jit(solution)/shard_map/ppermute | solution.py:365
  99.5 2.1 %collective-permute-start.29 = (f32[256,128]{1,0:T(8,128)S(1)}, f32[256,128]{1,0:T(8,128)S(1)}, u32[]{:S(2)}, u32[]{:S(2)}) collective-permute-start(f32[256,128]{1,0:T(8,128)S(1)} %shard_map.89), channel_id=1, source_target_pairs={{0,128},{1,129},{2,130},{3,131},{4,132},{5,133},{6,134},{7,135}} | collective-permute-start | bytes 393224 | tf_op jit(solution)/shard_map/ppermute | solution.py:365
  100.1 1.5 collective-permute-start.28
  100.9 3.4 %collective-permute-start.18 = (f32[2,256,128]{2,1,0:T(8,128)S(1)}, f32[2,256,128]{2,1,0:T(8,128)S(1)}, u32[]{:S(2)}, u32[]{:S(2)}) collective-permute-start(f32[2,256,128]{2,1,0:T(8,128)S(1)} %add.117), channel_id=1, source_target_pairs={{8,40},{72,104},{136,168},{200,232},{9,41},{73,105},{137,169},{201... | collective-permute-start | bytes 786440 | tf_op jit(solution)/shard_map/ppermute | solution.py:365
  101.6 4.0 %collective-permute-start.36 = (f32[256,128]{1,0:T(8,128)S(1)}, f32[256,128]{1,0:T(8,128)S(1)}, u32[]{:S(2)}, u32[]{:S(2)}) collective-permute-start(f32[256,128]{1,0:T(8,128)S(1)} %add_select_fusion), channel_id=1, source_target_pairs={{0,32},{8,40},{64,96},{72,104},{128,160},{136,168},{192,224},{200,... | collective-permute-start | bytes 393224 | tf_op jit(solution)/shard_map/ppermute | solution.py:365
  102.3 32.8 %collective-permute-start.35 = (f32[256,128]{1,0:T(8,128)S(1)}, f32[256,128]{1,0:T(8,128)S(1)}, u32[]{:S(2)}, u32[]{:S(2)}) collective-permute-start(f32[256,128]{1,0:T(8,128)S(1)} %add_select_fusion), channel_id=1, source_target_pairs={{0,112},{8,120},{64,48},{72,56},{128,240},{136,248},{192,176},{200... | collective-permute-start | bytes 393224 | tf_op jit(solution)/shard_map/ppermute | solution.py:365
  103.6 31.5 %collective-permute-start.34 = (f32[256,128]{1,0:T(8,128)S(1)}, f32[256,128]{1,0:T(8,128)S(1)}, u32[]{:S(2)}, u32[]{:S(2)}) collective-permute-start(f32[256,128]{1,0:T(8,128)S(1)} %add_select_fusion), channel_id=1, source_target_pairs={{0,16},{8,24},{64,80},{72,88},{128,144},{136,152},{192,208},{200,2... | collective-permute-start | bytes 393224 | tf_op jit(solution)/shard_map/ppermute | solution.py:365
  104.3 41.8 %collective-permute-start.19 = (f32[2,256,128]{2,1,0:T(8,128)S(1)}, f32[2,256,128]{2,1,0:T(8,128)S(1)}, u32[]{:S(2)}, u32[]{:S(2)}) collective-permute-start(f32[2,256,128]{2,1,0:T(8,128)S(1)} %add.118), channel_id=1, source_target_pairs={{8,24},{40,56},{72,88},{104,120},{136,152},{168,184},{200,216},{23... | collective-permute-start | bytes 786440 | tf_op jit(solution)/shard_map/ppermute | solution.py:365
  135.1 13.0 %collective-permute-start.37 = (f32[256,128]{1,0:T(8,128)S(1)}, f32[256,128]{1,0:T(8,128)S(1)}, u32[]{:S(2)}, u32[]{:S(2)}) collective-permute-start(f32[256,128]{1,0:T(8,128)S(1)} %add_add_fusion), channel_id=1, source_target_pairs={{8,0},{24,16},{40,32},{56,48},{72,64},{88,80},{104,96},{120,112},{... | collective-permute-start | bytes 393224 | tf_op jit(solution)/shard_map/ppermute | solution.py:438
  146.2 3.1 %collective-permute-start.20 = (f32[2,256,128]{2,1,0:T(8,128)S(1)}, f32[2,256,128]{2,1,0:T(8,128)S(1)}, u32[]{:S(2)}, u32[]{:S(2)}) collective-permute-start(f32[2,256,128]{2,1,0:T(8,128)S(1)} %add.119), channel_id=1, source_target_pairs={{24,16},{40,32},{56,48},{72,64},{88,80},{104,96},{120,112},{136,12... | collective-permute-start | bytes 786440 | tf_op jit(solution)/shard_map/ppermute | solution.py:429
